TPU v7x, 128 devices: a whole 4x4x4 slice. The times are simulated.
128 devices in a mesh: gx: 8 (over z, core), yz: 16 (over y, x).
Axes of the slice: x: 4, y: 4, z: 4, core: 2. Of those that a mesh axis runs over, the one named last changes fastest.
Arguments:
- part_mass: float32 [128, 128, 128], P(('gx', 'yz')), may hold values from 0.2 to 2
- part_vel: float32 [128, 128, 3, 128], P(('gx', 'yz')), may hold values from -6 to 6
- corner_weight: float32 [128, 128, 8, 128], P(('gx', 'yz')), may hold values from 0 to 0.25
- corner_base: int32 [128, 128, 128], P(('gx', 'yz')), may hold values from 0 to 11774, as said below
- slot_counts: int32 [128, 128], P(('gx', 'yz')), may hold values from 1 to 128, as said below
- water_vel: float32 [3, 32, 128, 512], P(None, 'gx', 'yz'), may hold values from -12 to 12
- solid_flag: int32 [32, 128, 512], P('gx', 'yz'), may hold values from 0 to 1
Outputs:
- particle_velocity: float32 [128, 128, 3, 128], P(('gx', 'yz'))
- pressure: float32 [32, 128, 512], P('gx', 'yz')
Inputs may be any that keep to these rules, and one draw needn't show every extreme that they name: corner_base is x * 8 * 512 + y * 512 + z with x < 3, y < 7, z < 511, so the whole tile lies in the block. `slot_counts`: slots below the count are live, the rest padding; in every draw some grid block receives 128 live slots from every source group.
All inputs are finite; a program needn't handle non-finite values.
Results may differ from a plain program's by a relative error of at most 0.0002.
Values sent between devices are 32-bit elements; how exact they have to be, the bound alone decides.
No kernel may reach another device: no remote copies, remote signals or barrier semaphores. Data moves between devices by JAX's collectives and lax.ppermute only.
A program may use at most 64 MiB of HBM per device.

v0:
```python
import math

import jax
import jax.numpy as jnp
from jax import lax
from jax.sharding import Mesh
from jax.sharding import PartitionSpec as P

ITERS = 3
DEGREE = 3
GX_YZ = ("gx_0", "gx_1", "yz_0", "yz_1")
GX = ("gx_0", "gx_1")
YZ = ("yz_0", "yz_1")


damping = 0.05
solid_water = 0.1
flip_ratio = 0.9
lower_bound = 0.1
upper_bound = 2.0


def extended(x, sides, width):
    edges = {}
    for axis, dim in sides:
        peers, length = (lax.axis_size(axis), x.shape[dim])
        up = [(i, (i + 1) % peers) for i in range(peers - 1)]
        last = lax.slice_in_dim(x, length - width, length, axis=dim)
        first = lax.slice_in_dim(x, 0, width, axis=dim)
        edges[dim] = (
            lax.ppermute(last, axis, up),
            lax.ppermute(first, axis, [(b, a) for a, b in up]),
        )
    done = []
    for _, dim in sides:
        low, high = edges[dim]
        around = [(width, width) if d in done else (0, 0) for d in range(x.ndim)]
        x = jnp.concatenate([jnp.pad(low, around), x, jnp.pad(high, around)], axis=dim)
        done.append(dim)
    return x


def one_axis_at_a_time(x, axes):
    for axis in axes:
        x = lax.psum(x, axis)
    return x


def in_one_piece(arrays, axis, split_dim, concat_dim, along):
    columns = [a.reshape(*a.shape[:along], -1) for a in arrays]
    both = jnp.concatenate(columns, axis=along)
    whole, at, done = (
        lax.all_to_all(both, axis, split_axis=split_dim, concat_axis=concat_dim, tiled=True),
        0,
        [],
    )
    for a, column in zip(arrays, columns):
        piece = whole[..., at : at + column.shape[along]]
        done.append(piece.reshape(*piece.shape[:along], *a.shape[along:]))
        at += column.shape[along]
    return tuple(done)


def harmonic(first, second):
    return 2.0 * first * second / (first + second)


def neighbours(padded):
    return [
        padded[2:, 1:-1, 1:-1],
        padded[:-2, 1:-1, 1:-1],
        padded[1:-1, 2:, 1:-1],
        padded[1:-1, :-2, 1:-1],
        padded[1:-1, 1:-1, 2:],
        padded[1:-1, 1:-1, :-2],
    ]


def diagonal_of(betas):
    result = damping
    for weight in betas:
        result = result + weight
    return result


def extend(field):
    padded = extended(field, ((GX, 0), (YZ, 1)), 1)
    return jnp.pad(padded, ((0, 0), (0, 0), (1, 1)))


def operate(field, betas):
    result = damping * field
    for weight, other in zip(betas, neighbours(extend(field))):
        result = result + weight * (field - other)
    return result


def divergence(velocity, padded_all, betas):
    result = jnp.zeros_like(velocity[0])
    for axis_number in range(3):
        component = velocity[axis_number]
        near = neighbours(padded_all[axis_number])
        result = result + betas[2 * axis_number] * (component + near[2 * axis_number]) * 0.5
        result = result - betas[2 * axis_number + 1] * (near[2 * axis_number + 1] + component) * 0.5
    return result


def chebyshev(residual, inverse, betas):
    theta = (upper_bound + lower_bound) / 2.0
    delta = (upper_bound - lower_bound) / 2.0
    sigma = theta / delta
    update = inverse * residual / theta
    result = update
    previous = 1.0 / sigma
    for turn in range(DEGREE - 1):
        misfit = residual - operate(result, betas)
        current = 1.0 / (2.0 * sigma - previous)
        update = current * previous * update + 2.0 * current / delta * inverse * misfit
        result = result + update
        previous = current
    return result


def paired(residual, precond, image):
    return (
        one_axis_at_a_time(jnp.sum(residual * precond), GX_YZ),
        one_axis_at_a_time(jnp.sum(image * precond), GX_YZ),
    )


def plane_masks(plane_cell, plane, width_y):
    plane_iota = jnp.arange(plane, dtype=jnp.int32)[:, None]
    return [
        (plane_iota == (plane_cell + shift_by)[None, :]).astype(jnp.float32)
        for shift_by in (0, 1, width_y, width_y + 1)
    ]


def split_blocks(array, total):
    block_rows = math.gcd(total, 2048)
    count = total // block_rows
    shaped = array.reshape(array.shape[:-1] + (count, block_rows))
    return (jnp.moveaxis(shaped, -2, 0), count, block_rows)


def spread_grid(values, plane_cell, depth_cell, width_x, width_y, depth):
    total = values.shape[-1]
    plane = width_x * width_y
    value_blocks, count, block_rows = split_blocks(values, total)
    plane_blocks = split_blocks(plane_cell, total)[0]
    depth_blocks = split_blocks(depth_cell, total)[0]
    depth_iota = jnp.arange(depth, dtype=jnp.int32)[None, :]

    def step(grid, item):
        block_values, block_plane, block_depth = item
        masks = plane_masks(block_plane, plane, width_y)
        for lift in (0, 1):
            lifted = jnp.zeros((4, plane, block_rows), jnp.float32)
            for corner_pair in range(4):
                lifted = (
                    lifted
                    + block_values[:, 2 * corner_pair + lift][:, None, :] * masks[corner_pair][None]
                )
            onehot = (block_depth[:, None] + lift == depth_iota).astype(jnp.float32)
            grid = grid + jnp.dot(
                lifted.reshape(4 * plane, block_rows),
                onehot,
                precision=lax.Precision.HIGHEST,
                preferred_element_type=jnp.float32,
            )
        return (grid, None)

    start = jnp.zeros((4 * plane, depth), jnp.float32)
    grid, unused = lax.scan(step, start, (value_blocks, plane_blocks, depth_blocks))
    return grid.reshape(4, width_x, width_y, depth)


def gather_corners(carried, plane_cell, depth_cell, width_x, width_y, depth):
    total = plane_cell.shape[0]
    plane = width_x * width_y
    flat_field = carried.reshape(3 * plane, depth)
    plane_blocks, count, block_rows = split_blocks(plane_cell, total)
    depth_blocks = split_blocks(depth_cell, total)[0]
    depth_iota = jnp.arange(depth, dtype=jnp.int32)[:, None]

    def pick(item):
        block_plane, block_depth = item
        masks = plane_masks(block_plane, plane, width_y)
        picked = [None] * 8
        for lift in (0, 1):
            onehot = (depth_iota == block_depth[None, :] + lift).astype(jnp.float32)
            table = jnp.dot(
                flat_field,
                onehot,
                precision=lax.Precision.HIGHEST,
                preferred_element_type=jnp.float32,
            ).reshape(3, plane, block_rows)
            for corner_pair in range(4):
                picked[2 * corner_pair + lift] = jnp.sum(table * masks[corner_pair][None], axis=1)
        return jnp.stack(picked, axis=1)

    gathered = lax.map(pick, (plane_blocks, depth_blocks))
    return jnp.transpose(gathered, (1, 2, 0, 3)).reshape(3, 8, total)


def local(part_mass, part_vel, corner_weight, corner_base, slot_counts, water_vel, solid_flag):
    capacity = part_mass.shape[2]
    width_x, width_y, width_z = solid_flag.shape
    slot_index = jnp.arange(capacity, dtype=jnp.int32)
    mass_in, vel_in, weight_in = in_one_piece((part_mass, part_vel, corner_weight), GX_YZ, 1, 0, 2)
    base_in, count_in = in_one_piece((corner_base, slot_counts), GX_YZ, 1, 0, 2)
    base_in = base_in[:, 0]
    weights_in = weight_in[:, 0]
    live = (slot_index[None, :] < count_in[:, 0][:, None]).astype(jnp.float32)
    masses = mass_in[:, 0] * live
    weighted = weights_in * masses[:, None, :]
    momentum = weighted[:, None] * vel_in[:, 0][:, :, None]
    values = jnp.concatenate([weighted[:, None], momentum], axis=1)
    sources = base_in.shape[0]
    flat_values = jnp.transpose(values, (1, 2, 0, 3)).reshape(4, 8, sources * capacity)
    flat_base = base_in.reshape(-1)
    plane_cell = flat_base // width_z
    depth_cell = flat_base - plane_cell * width_z
    grid = spread_grid(flat_values, plane_cell, depth_cell, width_x, width_y, width_z)
    density = jnp.where(solid_flag == 1, solid_water, 1.0).astype(jnp.float32)
    total = grid[0] + density
    kappa = 1.0 / total
    velocity = (grid[1:] + density[None] * water_vel) / total[None]
    betas = [harmonic(kappa, other) for other in neighbours(extend(kappa))]
    inverse = 1.0 / diagonal_of(betas)
    velocity_padded = extended(velocity, ((GX, 1), (YZ, 2)), 1)
    velocity_padded = jnp.pad(velocity_padded, ((0, 0), (0, 0), (0, 0), (1, 1)))
    source = -divergence(
        velocity, [velocity_padded[axis_number] for axis_number in range(3)], betas
    )
    pressure = jnp.zeros_like(source)
    residual = source
    precond = chebyshev(residual, inverse, betas)
    image = operate(precond, betas)
    agreement, product = paired(residual, precond, image)
    alpha = agreement / product
    search = precond
    along = image
    for turn in range(ITERS):
        pressure = pressure + alpha * search
        residual = residual - alpha * along
        if turn + 1 < ITERS:
            precond = chebyshev(residual, inverse, betas)
            image = operate(precond, betas)
            agreement_next, product = paired(residual, precond, image)
            ratio = agreement_next / agreement
            alpha = agreement_next / (product - ratio * agreement_next / alpha)
            search = precond + ratio * search
            along = image + ratio * along
            agreement = agreement_next
    near = neighbours(extend(pressure))
    slopes = [
        (
            betas[2 * axis_number] * (near[2 * axis_number] - pressure)
            + betas[2 * axis_number + 1] * (pressure - near[2 * axis_number + 1])
        )
        * 0.5
        for axis_number in range(3)
    ]
    corrected = velocity - jnp.stack(slopes)
    carried = corrected - flip_ratio * velocity
    picked = gather_corners(carried, plane_cell, depth_cell, width_x, width_y, width_z)
    flat_weights = jnp.transpose(weights_in, (1, 0, 2)).reshape(8, sources * capacity)
    interpolated = jnp.sum(picked * flat_weights[None], axis=1)
    interpolated = jnp.transpose(interpolated.reshape(3, sources, capacity), (1, 0, 2))[:, None]
    returned = lax.all_to_all(interpolated, GX_YZ, split_axis=0, concat_axis=1, tiled=True)
    return (flip_ratio * part_vel + returned, pressure)


def solution(mesh):
    torus = Mesh(mesh.devices.reshape(4, 2, 4, 4), ("gx_0", "gx_1", "yz_0", "yz_1"))
    in_specs = (
        P(GX_YZ, None, None),
        P(GX_YZ, None, None, None),
        P(GX_YZ, None, None, None),
        P(GX_YZ, None, None),
        P(GX_YZ, None),
        P(None, GX, YZ, None),
        P(GX, YZ, None),
    )
    out_specs = (P(GX_YZ, None, None, None), P(GX, YZ, None))
    return jax.shard_map(local, mesh=torus, in_specs=in_specs, out_specs=out_specs, check_vma=False)
```

profile of v0, /device:TPU:1, one launch (start us, length us, event | category | flops | bytes accessed | tf_op | source)
XLA Modules:
  0.0 445.5 jit_solution(12919971328262584231)
XLA Ops:
  3.1 11.5 %all-to-all-start = ((s32[1,128,129]{2,0,1:T(1,128)}), s32[1,128,129]{2,0,1:T(1,128)S(1)}, u32[]{:S(2)}, u32[]{:S(2)}) async-start(s32[1,128,129]{2,0,1:T(1,128)} %pad_add_fusion), calls=%async_computation | async-start | bytes 262144 | tf_op jit(solution)/shard_map/all_to_all | solution.py:53
  15.8 2.4 pad_maximum_fusion
  18.2 6.4 %all-to-all-done = s32[1,128,129]{2,0,1:T(1,128)S(1)} async-done(((s32[1,128,129]{2,0,1:T(1,128)}), s32[1,128,129]{2,0,1:T(1,128)S(1)}, u32[]{:S(2)}, u32[]{:S(2)}) %all-to-all-start) | async-done | bytes 66080 | tf_op jit(solution)/shard_map/all_to_all | solution.py:53
  24.6 4.2 all-to-all-start.1
  28.9 2.4 slice_reduce_fusion
  31.4 13.9 %all-to-all-done.1 = f32[1,128,1536]{2,0,1:T(1,128)S(1)} async-done(((f32[1,128,1536]{2,0,1:T(1,128)}), f32[1,128,1536]{2,0,1:T(1,128)S(1)}, u32[]{:S(2)}, u32[]{:S(2)}) %all-to-all-start.1) | async-done | bytes 786464 | tf_op jit(solution)/shard_map/all_to_all | solution.py:53
  48.6 49.6 %while.25 = (s32[]{:T(128)}, f32[128,512]{1,0:T(8,128)S(1)}, f32[8,4,8,2048]{3,0,2,1:T(8,128)}, s32[8,2048]{1,0:T(8,128)S(1)}, s32[8,2048]{1,0:T(8,128)S(1)}, /*index=5*/s32[]{:T(128)}, s32[]{:T(128)}) while((s32[]{:T(128)}, f32[128,512]{1,0:T(8,128)S(1)}, f32[8,4,8,2048]{3,0,2,1:T(8,128)}, s32[8,2048]{1,0:T(8,128)S(1)}, ...), condition=%wide.region_1.2_spmd.clone.clone, body=%wide.region_0.1_spmd.clone.clone.sunk | while | flops 3227721728 | bytes 9830495 | solution.py:174
  99.3 2.7 collective-permute-start
  102.0 2.8 collective-permute-start.5
  106.2 4.0 collective-permute-start.7
  110.2 2.5 collective-permute-start.2
  112.7 1.9 collective-permute-start.3
  114.7 2.3 collective-permute-start.1
  118.5 3.6 collective-permute-done.4
  122.7 2.3 collective-permute-start.8
  125.0 4.1 collective-permute-start.9
  130.5 4.6 %collective-permute-start.11 = (f32[4,1,512]{2,1,0:T(1,128)S(1)}, f32[4,1,512]{2,1,0:T(1,128)S(1)}, u32[]{:S(2)}, u32[]{:S(2)}) collective-permute-start(f32[4,1,512]{2,1,0:T(1,128)S(1)} %get-tuple-element.344), channel_id=1, source_target_pairs={{0,1},{1,2},{2,3},{3,4},{4,5},{5,6},{6,7},{7,8},{8,9},{9,10},{10,1... | collective-permute-start | bytes 24584 | tf_op jit(solution)/shard_map/ppermute | solution.py:31
  136.3 1.9 collective-permute-start.12
  138.2 3.6 collective-permute-start.13
  143.2 4.4 collective-permute-start.15
  148.7 1.9 collective-permute-start.16
  150.6 3.6 collective-permute-start.17
  155.6 4.5 collective-permute-start.19
  161.7 6.7 %all-reduce.44 = (f32[]{:T(128)}, f32[]{:T(128)}) all-reduce(f32[]{:T(128)} %get-tuple-element.198, f32[]{:T(128)} %get-tuple-element.197), channel_id=1, replica_groups=mesh['gx_0'=4,'gx_1'=2,'yz_0'=4,'yz_1'=4] {'gx_0'}, use_global_device_ids=true, to_apply=%region_3.4 | all-reduce | flops 2 | bytes 16 | tf_op jit(solution)/shard_map/psum | solution.py:45
  168.4 5.7 %all-reduce.47 = (f32[]{:T(128)}, f32[]{:T(128)}) all-reduce(f32[]{:T(128)} %get-tuple-element.235, f32[]{:T(128)} %get-tuple-element.236), channel_id=1, replica_groups=mesh['gx_0'=4,'gx_1'=2,'yz_0'=4,'yz_1'=4] {'gx_1'}, use_global_device_ids=true, to_apply=%region_4.5 | all-reduce | flops 2 | bytes 16 | tf_op jit(solution)/shard_map/psum | solution.py:45
  174.1 19.5 %all-reduce.41 = (f32[]{:T(128)}, f32[]{:T(128)}) all-reduce(f32[]{:T(128)} %get-tuple-element.241, f32[]{:T(128)} %get-tuple-element.242), channel_id=1, replica_groups=mesh['gx_0'=4,'gx_1'=2,'yz_0'=4,'yz_1'=4] {'yz_0'}, use_global_device_ids=true, to_apply=%region_5.6 | all-reduce | flops 2 | bytes 16 | tf_op jit(solution)/shard_map/psum | solution.py:45
  193.7 6.6 %all-reduce.38 = (f32[]{:T(128)}, f32[]{:T(128)}) all-reduce(f32[]{:T(128)} %get-tuple-element.229, f32[]{:T(128)} %get-tuple-element.230), channel_id=1, replica_groups=mesh['gx_0'=4,'gx_1'=2,'yz_0'=4,'yz_1'=4] {'yz_1'}, use_global_device_ids=true, to_apply=%region_6.7 | all-reduce | flops 2 | bytes 16 | tf_op jit(solution)/shard_map/psum | solution.py:45
  201.6 6.0 %collective-permute-start.20 = (f32[1,8,512]{2,1,0:T(8,128)S(1)}, f32[1,8,512]{2,1,0:T(8,128)S(1)}, u32[]{:S(2)}, u32[]{:S(2)}) collective-permute-start(f32[1,8,512]{2,1,0:T(8,128)S(1)} %get-tuple-element.331), channel_id=1, source_target_pairs={{16,0},{32,16},{48,32},{64,48},{80,64},{96,80},{112,96},{17,1},{33... | collective-permute-start | bytes 49160 | tf_op jit(solution)/shard_map/ppermute | solution.py:32
  210.9 4.3 collective-permute-start.23
  216.3 3.3 collective-permute-start.24
  219.6 2.3 collective-permute-start.25
  223.2 4.2 collective-permute-start.27
  228.6 3.2 collective-permute-start.28
  231.8 2.4 collective-permute-start.29
  235.5 4.2 collective-permute-start.31
  241.5 6.8 %all-reduce.43 = (f32[]{:T(128)}, f32[]{:T(128)}) all-reduce(f32[]{:T(128)} %get-tuple-element.196, f32[]{:T(128)} %get-tuple-element.195), channel_id=1, replica_groups=mesh['gx_0'=4,'gx_1'=2,'yz_0'=4,'yz_1'=4] {'gx_0'}, use_global_device_ids=true, to_apply=%region_13.14 | all-reduce | flops 2 | bytes 16 | tf_op jit(solution)/shard_map/psum | solution.py:45
  248.3 6.0 %all-reduce.46 = (f32[]{:T(128)}, f32[]{:T(128)}) all-reduce(f32[]{:T(128)} %get-tuple-element.233, f32[]{:T(128)} %get-tuple-element.234), channel_id=1, replica_groups=mesh['gx_0'=4,'gx_1'=2,'yz_0'=4,'yz_1'=4] {'gx_1'}, use_global_device_ids=true, to_apply=%region_14.15 | all-reduce | flops 2 | bytes 16 | tf_op jit(solution)/shard_map/psum | solution.py:45
  254.3 16.5 %all-reduce.40 = (f32[]{:T(128)}, f32[]{:T(128)}) all-reduce(f32[]{:T(128)} %get-tuple-element.239, f32[]{:T(128)} %get-tuple-element.240), channel_id=1, replica_groups=mesh['gx_0'=4,'gx_1'=2,'yz_0'=4,'yz_1'=4] {'yz_0'}, use_global_device_ids=true, to_apply=%region_15.16 | all-reduce | flops 2 | bytes 16 | tf_op jit(solution)/shard_map/psum | solution.py:45
  270.8 6.7 %all-reduce.37 = (f32[]{:T(128)}, f32[]{:T(128)}) all-reduce(f32[]{:T(128)} %get-tuple-element.227, f32[]{:T(128)} %get-tuple-element.228), channel_id=1, replica_groups=mesh['gx_0'=4,'gx_1'=2,'yz_0'=4,'yz_1'=4] {'yz_1'}, use_global_device_ids=true, to_apply=%region_16.17 | all-reduce | flops 2 | bytes 16 | tf_op jit(solution)/shard_map/psum | solution.py:45
  282.0 6.0 %collective-permute-start.32 = (f32[1,8,512]{2,1,0:T(8,128)S(1)}, f32[1,8,512]{2,1,0:T(8,128)S(1)}, u32[]{:S(2)}, u32[]{:S(2)}) collective-permute-start(f32[1,8,512]{2,1,0:T(8,128)S(1)} %get-tuple-element.319), channel_id=1, source_target_pairs={{16,0},{32,16},{48,32},{64,48},{80,64},{96,80},{112,96},{17,1},{33... | collective-permute-start | bytes 49160 | tf_op jit(solution)/shard_map/ppermute | solution.py:32
  288.1 3.1 collective-permute-start.33
  292.5 4.3 collective-permute-start.35
  297.9 2.0 collective-permute-start.36
  300.0 3.5 collective-permute-start.37
  304.8 4.3 collective-permute-start.39
  312.8 3.6 collective-permute-start.41
  317.7 4.3 collective-permute-start.43
  323.8 6.6 %all-reduce.42 = (f32[]{:T(128)}, f32[]{:T(128)}) all-reduce(f32[]{:T(128)} %get-tuple-element.249, f32[]{:T(128)} %fusion.51), channel_id=1, replica_groups=mesh['gx_0'=4,'gx_1'=2,'yz_0'=4,'yz_1'=4] {'gx_0'}, use_global_device_ids=true, to_apply=%region_23.24 | all-reduce | flops 2 | bytes 16 | tf_op jit(solution)/shard_map/psum | solution.py:45
  330.4 5.9 %all-reduce.45 = (f32[]{:T(128)}, f32[]{:T(128)}) all-reduce(f32[]{:T(128)} %get-tuple-element.231, f32[]{:T(128)} %get-tuple-element.232), channel_id=1, replica_groups=mesh['gx_0'=4,'gx_1'=2,'yz_0'=4,'yz_1'=4] {'gx_1'}, use_global_device_ids=true, to_apply=%region_24.25 | all-reduce | flops 2 | bytes 16 | tf_op jit(solution)/shard_map/psum | solution.py:45
  336.3 16.4 %all-reduce.39 = (f32[]{:T(128)}, f32[]{:T(128)}) all-reduce(f32[]{:T(128)} %get-tuple-element.237, f32[]{:T(128)} %get-tuple-element.238), channel_id=1, replica_groups=mesh['gx_0'=4,'gx_1'=2,'yz_0'=4,'yz_1'=4] {'yz_0'}, use_global_device_ids=true, to_apply=%region_25.26 | all-reduce | flops 2 | bytes 16 | tf_op jit(solution)/shard_map/psum | solution.py:45
  352.7 6.6 %all-reduce.36 = (f32[]{:T(128)}, f32[]{:T(128)}) all-reduce(f32[]{:T(128)} %get-tuple-element.225, f32[]{:T(128)} %get-tuple-element.226), channel_id=1, replica_groups=mesh['gx_0'=4,'gx_1'=2,'yz_0'=4,'yz_1'=4] {'yz_1'}, use_global_device_ids=true, to_apply=%region_26.27 | all-reduce | flops 2 | bytes 16 | tf_op jit(solution)/shard_map/psum | solution.py:45
  363.3 6.0 %collective-permute-start.44 = (f32[1,8,512]{2,1,0:T(8,128)S(1)}, f32[1,8,512]{2,1,0:T(8,128)S(1)}, u32[]{:S(2)}, u32[]{:S(2)}) collective-permute-start(f32[1,8,512]{2,1,0:T(8,128)S(1)} %get-tuple-element.307), channel_id=1, source_target_pairs={{16,0},{32,16},{48,32},{64,48},{80,64},{96,80},{112,96},{17,1},{33... | collective-permute-start | bytes 49160 | tf_op jit(solution)/shard_map/ppermute | solution.py:32
  369.3 2.0 collective-permute-start.45
  372.7 4.5 %collective-permute-start.47 = (f32[4,1,512]{2,1,0:T(1,128)S(1)}, f32[4,1,512]{2,1,0:T(1,128)S(1)}, u32[]{:S(2)}, u32[]{:S(2)}) collective-permute-start(f32[4,1,512]{2,1,0:T(1,128)S(1)} %get-tuple-element.308), channel_id=1, source_target_pairs={{0,1},{1,2},{2,3},{3,4},{4,5},{5,6},{6,7},{7,8},{8,9},{9,10},{10,1... | collective-permute-start | bytes 24584 | tf_op jit(solution)/shard_map/ppermute | solution.py:31
  378.9 46.0 %while.24 = (s32[]{:T(128)}, f32[8,3,8,2048]{3,2,1,0:T(8,128)S(1)}, s32[8,2048]{1,0:T(8,128)S(1)}, f32[96,512]{1,0:T(8,128)}, s32[8,2048]{1,0:T(8,128)S(1)}, /*index=5*/s32[]{:T(128)}) while((s32[]{:T(128)}, f32[8,3,8,2048]{3,2,1,0:T(8,128)S(1)}, s32[8,2048]{1,0:T(8,128)S(1)}, f32[96,512]{1,0:T(8,128)}, ...), condition=%wide.region_41.42_spmd.clone.clone, body=%wide.region_32.41_spmd.clone.clone.sunk | while | flops 2421645312 | bytes 7921769 | solution.py:202
  378.9 2.6 fusion.300
  384.7 2.6 fusion.300
  390.5 2.6 fusion.300
  396.2 2.6 fusion.300
  402.0 2.6 fusion.300
  407.7 2.6 fusion.300
  413.5 2.6 fusion.300
  419.2 2.6 fusion.300
  425.9 18.6 %all_to_all.36 = f32[128,1,3,128]{3,1,2,0:T(1,128)S(1)} all-to-all(f32[128,1,3,128]{3,1,2,0:T(1,128)S(1)} %copy.109), channel_id=1, replica_groups=mesh['gx_0'=4,'gx_1'=2,'yz_0'=4,'yz_1'=4] {'gx_0','gx_1','yz_0','yz_1'}, dimensions={0} | all-to-all | bytes 393216 | tf_op jit(solution)/shard_map/all_to_all | solution.py:271
  (474 shorter events, 116.7 us)
Async XLA Ops:
  0.6 15.2 %copy-start.2 = (f32[1,128,8,128]{3,2,1,0:T(8,128)S(1)}, f32[1,128,8,128]{3,2,1,0:T(8,128)}, u32[]{:S(2)}) copy-start(f32[1,128,8,128]{3,2,1,0:T(8,128)} %param.13) | copy-start | bytes 1572868
  3.1 21.5 %all-to-all-start = ((s32[1,128,129]{2,0,1:T(1,128)}), s32[1,128,129]{2,0,1:T(1,128)S(1)}, u32[]{:S(2)}, u32[]{:S(2)}) async-start(s32[1,128,129]{2,0,1:T(1,128)} %pad_add_fusion), calls=%async_computation | async-start | bytes 262144 | tf_op jit(solution)/shard_map/all_to_all | solution.py:53
  24.6 20.7 %all-to-all-start.1 = ((f32[1,128,1536]{2,0,1:T(1,128)}), f32[1,128,1536]{2,0,1:T(1,128)S(1)}, u32[]{:S(2)}, u32[]{:S(2)}) async-start(f32[1,128,1536]{2,0,1:T(1,128)} %pad_maximum_fusion), calls=%async_computation.1 | async-start | bytes 1572864 | tf_op jit(solution)/shard_map/all_to_all | solution.py:53
  48.6 49.6 %copy-start.4 = (s32[4,8,512]{2,1,0:T(8,128)S(1)}, s32[4,8,512]{2,1,0:T(8,128)}, u32[]{:S(2)}) copy-start(s32[4,8,512]{2,1,0:T(8,128)} %param.17) | copy-start | bytes 196612
  99.3 17.7 %collective-permute-start = (f32[1,8,512]{2,1,0:T(8,128)S(1)}, f32[1,8,512]{2,1,0:T(8,128)S(1)}, u32[]{:S(2)}, u32[]{:S(2)}) collective-permute-start(f32[1,8,512]{2,1,0:T(8,128)S(1)} %get-tuple-element.349), channel_id=1, source_target_pairs={{16,0},{32,16},{48,32},{64,48},{80,64},{96,80},{112,96},{17,1},{33... | collective-permute-start | bytes 49160 | tf_op jit(solution)/shard_map/ppermute | solution.py:32
  102.0 16.2 %collective-permute-start.5 = (f32[1,8,512]{2,1,0:T(8,128)S(1)}, f32[1,8,512]{2,1,0:T(8,128)S(1)}, u32[]{:S(2)}, u32[]{:S(2)}) collective-permute-start(f32[1,8,512]{2,1,0:T(8,128)S(1)} %get-tuple-element.348), channel_id=1, source_target_pairs={{0,16},{16,32},{32,48},{48,64},{64,80},{80,96},{96,112},{1,17},{17... | collective-permute-start | bytes 49160 | tf_op jit(solution)/shard_map/ppermute | solution.py:31
  104.9 7.8 %collective-permute-start.6 = (f32[4,1,512]{2,1,0:T(1,128)S(1)}, f32[4,1,512]{2,1,0:T(1,128)S(1)}, u32[]{:S(2)}, u32[]{:S(2)}) collective-permute-start(f32[4,1,512]{2,1,0:T(1,128)S(1)} %get-tuple-element.347), channel_id=1, source_target_pairs={{1,0},{2,1},{3,2},{4,3},{5,4},{6,5},{7,6},{8,7},{9,8},{10,9},{11,1... | collective-permute-start | bytes 24584 | tf_op jit(solution)/shard_map/ppermute | solution.py:32
  106.2 8.5 %collective-permute-start.7 = (f32[4,1,512]{2,1,0:T(1,128)S(1)}, f32[4,1,512]{2,1,0:T(1,128)S(1)}, u32[]{:S(2)}, u32[]{:S(2)}) collective-permute-start(f32[4,1,512]{2,1,0:T(1,128)S(1)} %get-tuple-element.346), channel_id=1, source_target_pairs={{0,1},{1,2},{2,3},{3,4},{4,5},{5,6},{6,7},{7,8},{8,9},{9,10},{10,1... | collective-permute-start | bytes 24584 | tf_op jit(solution)/shard_map/ppermute | solution.py:31
  110.2 11.9 %collective-permute-start.2 = (f32[3,1,8,512]{3,2,1,0:T(8,128)S(1)}, f32[3,1,8,512]{3,2,1,0:T(8,128)S(1)}, u32[]{:S(2)}, u32[]{:S(2)}) collective-permute-start(f32[3,1,8,512]{3,2,1,0:T(8,128)S(1)} %get-tuple-element.300), channel_id=1, source_target_pairs={{0,16},{16,32},{32,48},{48,64},{64,80},{80,96},{96,112},{1,17},{17... | collective-permute-start | bytes 147464 | tf_op jit(solution)/shard_map/ppermute | solution.py:31
  112.7 9.4 %collective-permute-start.3 = (f32[3,1,8,512]{3,2,1,0:T(8,128)S(1)}, f32[3,1,8,512]{3,2,1,0:T(8,128)S(1)}, u32[]{:S(2)}, u32[]{:S(2)}) collective-permute-start(f32[3,1,8,512]{3,2,1,0:T(8,128)S(1)} %get-tuple-element.301), channel_id=1, source_target_pairs={{16,0},{32,16},{48,32},{64,48},{80,64},{96,80},{112,96},{17,1},{33... | collective-permute-start | bytes 147464 | tf_op jit(solution)/shard_map/ppermute | solution.py:32
  114.7 3.8 collective-permute-start.1
  117.0 5.1 %collective-permute-start.4 = (f32[3,4,1,512]{3,2,1,0:T(1,128)S(1)}, f32[3,4,1,512]{3,2,1,0:T(1,128)S(1)}, u32[]{:S(2)}, u32[]{:S(2)}) collective-permute-start(f32[3,4,1,512]{3,2,1,0:T(1,128)S(1)} %get-tuple-element.303), channel_id=1, source_target_pairs={{1,0},{2,1},{3,2},{4,3},{5,4},{6,5},{7,6},{8,7},{9,8},{10,9},{11,1... | collective-permute-start | bytes 73736 | tf_op jit(solution)/shard_map/ppermute | solution.py:32
  122.7 13.2 %collective-permute-start.8 = (f32[1,8,512]{2,1,0:T(8,128)S(1)}, f32[1,8,512]{2,1,0:T(8,128)S(1)}, u32[]{:S(2)}, u32[]{:S(2)}) collective-permute-start(f32[1,8,512]{2,1,0:T(8,128)S(1)} %get-tuple-element.343), channel_id=1, source_target_pairs={{16,0},{32,16},{48,32},{64,48},{80,64},{96,80},{112,96},{17,1},{33... | collective-permute-start | bytes 49160 | tf_op jit(solution)/shard_map/ppermute | solution.py:32
  125.0 10.9 %collective-permute-start.9 = (f32[1,8,512]{2,1,0:T(8,128)S(1)}, f32[1,8,512]{2,1,0:T(8,128)S(1)}, u32[]{:S(2)}, u32[]{:S(2)}) collective-permute-start(f32[1,8,512]{2,1,0:T(8,128)S(1)} %get-tuple-element.342), channel_id=1, source_target_pairs={{0,16},{16,32},{32,48},{48,64},{64,80},{80,96},{96,112},{1,17},{17... | collective-permute-start | bytes 49160 | tf_op jit(solution)/shard_map/ppermute | solution.py:31
  129.2 5.9 %collective-permute-start.10 = (f32[4,1,512]{2,1,0:T(1,128)S(1)}, f32[4,1,512]{2,1,0:T(1,128)S(1)}, u32[]{:S(2)}, u32[]{:S(2)}) collective-permute-start(f32[4,1,512]{2,1,0:T(1,128)S(1)} %get-tuple-element.345), channel_id=1, source_target_pairs={{1,0},{2,1},{3,2},{4,3},{5,4},{6,5},{7,6},{8,7},{9,8},{10,9},{11,1... | collective-permute-start | bytes 24584 | tf_op jit(solution)/shard_map/ppermute | solution.py:32
  130.5 5.4 %collective-permute-start.11 = (f32[4,1,512]{2,1,0:T(1,128)S(1)}, f32[4,1,512]{2,1,0:T(1,128)S(1)}, u32[]{:S(2)}, u32[]{:S(2)}) collective-permute-start(f32[4,1,512]{2,1,0:T(1,128)S(1)} %get-tuple-element.344), channel_id=1, source_target_pairs={{0,1},{1,2},{2,3},{3,4},{4,5},{5,6},{6,7},{7,8},{8,9},{9,10},{10,1... | collective-permute-start | bytes 24584 | tf_op jit(solution)/shard_map/ppermute | solution.py:31
  136.3 12.0 %collective-permute-start.12 = (f32[1,8,512]{2,1,0:T(8,128)S(1)}, f32[1,8,512]{2,1,0:T(8,128)S(1)}, u32[]{:S(2)}, u32[]{:S(2)}) collective-permute-start(f32[1,8,512]{2,1,0:T(8,128)S(1)} %get-tuple-element.339), channel_id=1, source_target_pairs={{16,0},{32,16},{48,32},{64,48},{80,64},{96,80},{112,96},{17,1},{33... | collective-permute-start | bytes 49160 | tf_op jit(solution)/shard_map/ppermute | solution.py:32
  138.2 10.0 %collective-permute-start.13 = (f32[1,8,512]{2,1,0:T(8,128)S(1)}, f32[1,8,512]{2,1,0:T(8,128)S(1)}, u32[]{:S(2)}, u32[]{:S(2)}) collective-permute-start(f32[1,8,512]{2,1,0:T(8,128)S(1)} %get-tuple-element.338), channel_id=1, source_target_pairs={{0,16},{16,32},{32,48},{48,64},{64,80},{80,96},{96,112},{1,17},{17... | collective-permute-start | bytes 49160 | tf_op jit(solution)/shard_map/ppermute | solution.py:31
  141.9 5.8 %collective-permute-start.14 = (f32[4,1,512]{2,1,0:T(1,128)S(1)}, f32[4,1,512]{2,1,0:T(1,128)S(1)}, u32[]{:S(2)}, u32[]{:S(2)}) collective-permute-start(f32[4,1,512]{2,1,0:T(1,128)S(1)} %get-tuple-element.341), channel_id=1, source_target_pairs={{1,0},{2,1},{3,2},{4,3},{5,4},{6,5},{7,6},{8,7},{9,8},{10,9},{11,1... | collective-permute-start | bytes 24584 | tf_op jit(solution)/shard_map/ppermute | solution.py:32
  143.2 5.0 %collective-permute-start.15 = (f32[4,1,512]{2,1,0:T(1,128)S(1)}, f32[4,1,512]{2,1,0:T(1,128)S(1)}, u32[]{:S(2)}, u32[]{:S(2)}) collective-permute-start(f32[4,1,512]{2,1,0:T(1,128)S(1)} %get-tuple-element.340), channel_id=1, source_target_pairs={{0,1},{1,2},{2,3},{3,4},{4,5},{5,6},{6,7},{7,8},{8,9},{9,10},{10,1... | collective-permute-start | bytes 24584 | tf_op jit(solution)/shard_map/ppermute | solution.py:31
  148.7 12.2 %collective-permute-start.16 = (f32[1,8,512]{2,1,0:T(8,128)S(1)}, f32[1,8,512]{2,1,0:T(8,128)S(1)}, u32[]{:S(2)}, u32[]{:S(2)}) collective-permute-start(f32[1,8,512]{2,1,0:T(8,128)S(1)} %get-tuple-element.335), channel_id=1, source_target_pairs={{16,0},{32,16},{48,32},{64,48},{80,64},{96,80},{112,96},{17,1},{33... | collective-permute-start | bytes 49160 | tf_op jit(solution)/shard_map/ppermute | solution.py:32
  150.6 10.2 %collective-permute-start.17 = (f32[1,8,512]{2,1,0:T(8,128)S(1)}, f32[1,8,512]{2,1,0:T(8,128)S(1)}, u32[]{:S(2)}, u32[]{:S(2)}) collective-permute-start(f32[1,8,512]{2,1,0:T(8,128)S(1)} %get-tuple-element.334), channel_id=1, source_target_pairs={{0,16},{16,32},{32,48},{48,64},{64,80},{80,96},{96,112},{1,17},{17... | collective-permute-start | bytes 49160 | tf_op jit(solution)/shard_map/ppermute | solution.py:31
  154.3 5.8 %collective-permute-start.18 = (f32[4,1,512]{2,1,0:T(1,128)S(1)}, f32[4,1,512]{2,1,0:T(1,128)S(1)}, u32[]{:S(2)}, u32[]{:S(2)}) collective-permute-start(f32[4,1,512]{2,1,0:T(1,128)S(1)} %get-tuple-element.337), channel_id=1, source_target_pairs={{1,0},{2,1},{3,2},{4,3},{5,4},{6,5},{7,6},{8,7},{9,8},{10,9},{11,1... | collective-permute-start | bytes 24584 | tf_op jit(solution)/shard_map/ppermute | solution.py:32
  155.6 5.2 %collective-permute-start.19 = (f32[4,1,512]{2,1,0:T(1,128)S(1)}, f32[4,1,512]{2,1,0:T(1,128)S(1)}, u32[]{:S(2)}, u32[]{:S(2)}) collective-permute-start(f32[4,1,512]{2,1,0:T(1,128)S(1)} %get-tuple-element.336), channel_id=1, source_target_pairs={{0,1},{1,2},{2,3},{3,4},{4,5},{5,6},{6,7},{7,8},{8,9},{9,10},{10,1... | collective-permute-start | bytes 24584 | tf_op jit(solution)/shard_map/ppermute | solution.py:31
  201.6 14.3 %collective-permute-start.20 = (f32[1,8,512]{2,1,0:T(8,128)S(1)}, f32[1,8,512]{2,1,0:T(8,128)S(1)}, u32[]{:S(2)}, u32[]{:S(2)}) collective-permute-start(f32[1,8,512]{2,1,0:T(8,128)S(1)} %get-tuple-element.331), channel_id=1, source_target_pairs={{16,0},{32,16},{48,32},{64,48},{80,64},{96,80},{112,96},{17,1},{33... | collective-permute-start | bytes 49160 | tf_op jit(solution)/shard_map/ppermute | solution.py:32
  207.7 8.3 %collective-permute-start.21 = (f32[1,8,512]{2,1,0:T(8,128)S(1)}, f32[1,8,512]{2,1,0:T(8,128)S(1)}, u32[]{:S(2)}, u32[]{:S(2)}) collective-permute-start(f32[1,8,512]{2,1,0:T(8,128)S(1)} %get-tuple-element.330), channel_id=1, source_target_pairs={{0,16},{16,32},{32,48},{48,64},{64,80},{80,96},{96,112},{1,17},{17... | collective-permute-start | bytes 49160 | tf_op jit(solution)/shard_map/ppermute | solution.py:31
  209.6 5.6 %collective-permute-start.22 = (f32[4,1,512]{2,1,0:T(1,128)S(1)}, f32[4,1,512]{2,1,0:T(1,128)S(1)}, u32[]{:S(2)}, u32[]{:S(2)}) collective-permute-start(f32[4,1,512]{2,1,0:T(1,128)S(1)} %get-tuple-element.333), channel_id=1, source_target_pairs={{1,0},{2,1},{3,2},{4,3},{5,4},{6,5},{7,6},{8,7},{9,8},{10,9},{11,1... | collective-permute-start | bytes 24584 | tf_op jit(solution)/shard_map/ppermute | solution.py:32
  210.9 5.0 %collective-permute-start.23 = (f32[4,1,512]{2,1,0:T(1,128)S(1)}, f32[4,1,512]{2,1,0:T(1,128)S(1)}, u32[]{:S(2)}, u32[]{:S(2)}) collective-permute-start(f32[4,1,512]{2,1,0:T(1,128)S(1)} %get-tuple-element.332), channel_id=1, source_target_pairs={{0,1},{1,2},{2,3},{3,4},{4,5},{5,6},{6,7},{7,8},{8,9},{9,10},{10,1... | collective-permute-start | bytes 24584 | tf_op jit(solution)/shard_map/ppermute | solution.py:31
  216.3 11.9 %collective-permute-start.24 = (f32[1,8,512]{2,1,0:T(8,128)S(1)}, f32[1,8,512]{2,1,0:T(8,128)S(1)}, u32[]{:S(2)}, u32[]{:S(2)}) collective-permute-start(f32[1,8,512]{2,1,0:T(8,128)S(1)} %get-tuple-element.327), channel_id=1, source_target_pairs={{16,0},{32,16},{48,32},{64,48},{80,64},{96,80},{112,96},{17,1},{33... | collective-permute-start | bytes 49160 | tf_op jit(solution)/shard_map/ppermute | solution.py:32
  219.6 8.7 %collective-permute-start.25 = (f32[1,8,512]{2,1,0:T(8,128)S(1)}, f32[1,8,512]{2,1,0:T(8,128)S(1)}, u32[]{:S(2)}, u32[]{:S(2)}) collective-permute-start(f32[1,8,512]{2,1,0:T(8,128)S(1)} %get-tuple-element.326), channel_id=1, source_target_pairs={{0,16},{16,32},{32,48},{48,64},{64,80},{80,96},{96,112},{1,17},{17... | collective-permute-start | bytes 49160 | tf_op jit(solution)/shard_map/ppermute | solution.py:31
  221.9 5.6 %collective-permute-start.26 = (f32[4,1,512]{2,1,0:T(1,128)S(1)}, f32[4,1,512]{2,1,0:T(1,128)S(1)}, u32[]{:S(2)}, u32[]{:S(2)}) collective-permute-start(f32[4,1,512]{2,1,0:T(1,128)S(1)} %get-tuple-element.329), channel_id=1, source_target_pairs={{1,0},{2,1},{3,2},{4,3},{5,4},{6,5},{7,6},{8,7},{9,8},{10,9},{11,1... | collective-permute-start | bytes 24584 | tf_op jit(solution)/shard_map/ppermute | solution.py:32
  223.2 5.0 %collective-permute-start.27 = (f32[4,1,512]{2,1,0:T(1,128)S(1)}, f32[4,1,512]{2,1,0:T(1,128)S(1)}, u32[]{:S(2)}, u32[]{:S(2)}) collective-permute-start(f32[4,1,512]{2,1,0:T(1,128)S(1)} %get-tuple-element.328), channel_id=1, source_target_pairs={{0,1},{1,2},{2,3},{3,4},{4,5},{5,6},{6,7},{7,8},{8,9},{9,10},{10,1... | collective-permute-start | bytes 24584 | tf_op jit(solution)/shard_map/ppermute | solution.py:31
  228.6 11.9 %collective-permute-start.28 = (f32[1,8,512]{2,1,0:T(8,128)S(1)}, f32[1,8,512]{2,1,0:T(8,128)S(1)}, u32[]{:S(2)}, u32[]{:S(2)}) collective-permute-start(f32[1,8,512]{2,1,0:T(8,128)S(1)} %get-tuple-element.323), channel_id=1, source_target_pairs={{16,0},{32,16},{48,32},{64,48},{80,64},{96,80},{112,96},{17,1},{33... | collective-permute-start | bytes 49160 | tf_op jit(solution)/shard_map/ppermute | solution.py:32
  231.8 8.8 %collective-permute-start.29 = (f32[1,8,512]{2,1,0:T(8,128)S(1)}, f32[1,8,512]{2,1,0:T(8,128)S(1)}, u32[]{:S(2)}, u32[]{:S(2)}) collective-permute-start(f32[1,8,512]{2,1,0:T(8,128)S(1)} %get-tuple-element.322), channel_id=1, source_target_pairs={{0,16},{16,32},{32,48},{48,64},{64,80},{80,96},{96,112},{1,17},{17... | collective-permute-start | bytes 49160 | tf_op jit(solution)/shard_map/ppermute | solution.py:31
  234.2 5.6 %collective-permute-start.30 = (f32[4,1,512]{2,1,0:T(1,128)S(1)}, f32[4,1,512]{2,1,0:T(1,128)S(1)}, u32[]{:S(2)}, u32[]{:S(2)}) collective-permute-start(f32[4,1,512]{2,1,0:T(1,128)S(1)} %get-tuple-element.325), channel_id=1, source_target_pairs={{1,0},{2,1},{3,2},{4,3},{5,4},{6,5},{7,6},{8,7},{9,8},{10,9},{11,1... | collective-permute-start | bytes 24584 | tf_op jit(solution)/shard_map/ppermute | solution.py:32
  235.5 5.0 %collective-permute-start.31 = (f32[4,1,512]{2,1,0:T(1,128)S(1)}, f32[4,1,512]{2,1,0:T(1,128)S(1)}, u32[]{:S(2)}, u32[]{:S(2)}) collective-permute-start(f32[4,1,512]{2,1,0:T(1,128)S(1)} %get-tuple-element.324), channel_id=1, source_target_pairs={{0,1},{1,2},{2,3},{3,4},{4,5},{5,6},{6,7},{7,8},{8,9},{9,10},{10,1... | collective-permute-start | bytes 24584 | tf_op jit(solution)/shard_map/ppermute | solution.py:31
  282.0 15.6 %collective-permute-start.32 = (f32[1,8,512]{2,1,0:T(8,128)S(1)}, f32[1,8,512]{2,1,0:T(8,128)S(1)}, u32[]{:S(2)}, u32[]{:S(2)}) collective-permute-start(f32[1,8,512]{2,1,0:T(8,128)S(1)} %get-tuple-element.319), channel_id=1, source_target_pairs={{16,0},{32,16},{48,32},{64,48},{80,64},{96,80},{112,96},{17,1},{33... | collective-permute-start | bytes 49160 | tf_op jit(solution)/shard_map/ppermute | solution.py:32
  288.1 9.5 %collective-permute-start.33 = (f32[1,8,512]{2,1,0:T(8,128)S(1)}, f32[1,8,512]{2,1,0:T(8,128)S(1)}, u32[]{:S(2)}, u32[]{:S(2)}) collective-permute-start(f32[1,8,512]{2,1,0:T(8,128)S(1)} %get-tuple-element.318), channel_id=1, source_target_pairs={{0,16},{16,32},{32,48},{48,64},{64,80},{80,96},{96,112},{1,17},{17... | collective-permute-start | bytes 49160 | tf_op jit(solution)/shard_map/ppermute | solution.py:31
  291.2 5.6 %collective-permute-start.34 = (f32[4,1,512]{2,1,0:T(1,128)S(1)}, f32[4,1,512]{2,1,0:T(1,128)S(1)}, u32[]{:S(2)}, u32[]{:S(2)}) collective-permute-start(f32[4,1,512]{2,1,0:T(1,128)S(1)} %get-tuple-element.321), channel_id=1, source_target_pairs={{1,0},{2,1},{3,2},{4,3},{5,4},{6,5},{7,6},{8,7},{9,8},{10,9},{11,1... | collective-permute-start | bytes 24584 | tf_op jit(solution)/shard_map/ppermute | solution.py:32
  292.5 5.0 %collective-permute-start.35 = (f32[4,1,512]{2,1,0:T(1,128)S(1)}, f32[4,1,512]{2,1,0:T(1,128)S(1)}, u32[]{:S(2)}, u32[]{:S(2)}) collective-permute-start(f32[4,1,512]{2,1,0:T(1,128)S(1)} %get-tuple-element.320), channel_id=1, source_target_pairs={{0,1},{1,2},{2,3},{3,4},{4,5},{5,6},{6,7},{7,8},{8,9},{9,10},{10,1... | collective-permute-start | bytes 24584 | tf_op jit(solution)/shard_map/ppermute | solution.py:31
  297.9 12.0 %collective-permute-start.36 = (f32[1,8,512]{2,1,0:T(8,128)S(1)}, f32[1,8,512]{2,1,0:T(8,128)S(1)}, u32[]{:S(2)}, u32[]{:S(2)}) collective-permute-start(f32[1,8,512]{2,1,0:T(8,128)S(1)} %get-tuple-element.315), channel_id=1, source_target_pairs={{16,0},{32,16},{48,32},{64,48},{80,64},{96,80},{112,96},{17,1},{33... | collective-permute-start | bytes 49160 | tf_op jit(solution)/shard_map/ppermute | solution.py:32
  300.0 9.9 %collective-permute-start.37 = (f32[1,8,512]{2,1,0:T(8,128)S(1)}, f32[1,8,512]{2,1,0:T(8,128)S(1)}, u32[]{:S(2)}, u32[]{:S(2)}) collective-permute-start(f32[1,8,512]{2,1,0:T(8,128)S(1)} %get-tuple-element.314), channel_id=1, source_target_pairs={{0,16},{16,32},{32,48},{48,64},{64,80},{80,96},{96,112},{1,17},{17... | collective-permute-start | bytes 49160 | tf_op jit(solution)/shard_map/ppermute | solution.py:31
  303.5 5.6 %collective-permute-start.38 = (f32[4,1,512]{2,1,0:T(1,128)S(1)}, f32[4,1,512]{2,1,0:T(1,128)S(1)}, u32[]{:S(2)}, u32[]{:S(2)}) collective-permute-start(f32[4,1,512]{2,1,0:T(1,128)S(1)} %get-tuple-element.317), channel_id=1, source_target_pairs={{1,0},{2,1},{3,2},{4,3},{5,4},{6,5},{7,6},{8,7},{9,8},{10,9},{11,1... | collective-permute-start | bytes 24584 | tf_op jit(solution)/shard_map/ppermute | solution.py:32
  304.8 5.1 %collective-permute-start.39 = (f32[4,1,512]{2,1,0:T(1,128)S(1)}, f32[4,1,512]{2,1,0:T(1,128)S(1)}, u32[]{:S(2)}, u32[]{:S(2)}) collective-permute-start(f32[4,1,512]{2,1,0:T(1,128)S(1)} %get-tuple-element.316), channel_id=1, source_target_pairs={{0,1},{1,2},{2,3},{3,4},{4,5},{5,6},{6,7},{7,8},{8,9},{9,10},{10,1... | collective-permute-start | bytes 24584 | tf_op jit(solution)/shard_map/ppermute | solution.py:31
  310.8 12.0 %collective-permute-start.40 = (f32[1,8,512]{2,1,0:T(8,128)S(1)}, f32[1,8,512]{2,1,0:T(8,128)S(1)}, u32[]{:S(2)}, u32[]{:S(2)}) collective-permute-start(f32[1,8,512]{2,1,0:T(8,128)S(1)} %get-tuple-element.311), channel_id=1, source_target_pairs={{16,0},{32,16},{48,32},{64,48},{80,64},{96,80},{112,96},{17,1},{33... | collective-permute-start | bytes 49160 | tf_op jit(solution)/shard_map/ppermute | solution.py:32
  312.8 10.1 %collective-permute-start.41 = (f32[1,8,512]{2,1,0:T(8,128)S(1)}, f32[1,8,512]{2,1,0:T(8,128)S(1)}, u32[]{:S(2)}, u32[]{:S(2)}) collective-permute-start(f32[1,8,512]{2,1,0:T(8,128)S(1)} %get-tuple-element.310), channel_id=1, source_target_pairs={{0,16},{16,32},{32,48},{48,64},{64,80},{80,96},{96,112},{1,17},{17... | collective-permute-start | bytes 49160 | tf_op jit(solution)/shard_map/ppermute | solution.py:31
  316.4 5.6 %collective-permute-start.42 = (f32[4,1,512]{2,1,0:T(1,128)S(1)}, f32[4,1,512]{2,1,0:T(1,128)S(1)}, u32[]{:S(2)}, u32[]{:S(2)}) collective-permute-start(f32[4,1,512]{2,1,0:T(1,128)S(1)} %get-tuple-element.313), channel_id=1, source_target_pairs={{1,0},{2,1},{3,2},{4,3},{5,4},{6,5},{7,6},{8,7},{9,8},{10,9},{11,1... | collective-permute-start | bytes 24584 | tf_op jit(solution)/shard_map/ppermute | solution.py:32
  317.7 5.1 %collective-permute-start.43 = (f32[4,1,512]{2,1,0:T(1,128)S(1)}, f32[4,1,512]{2,1,0:T(1,128)S(1)}, u32[]{:S(2)}, u32[]{:S(2)}) collective-permute-start(f32[4,1,512]{2,1,0:T(1,128)S(1)} %get-tuple-element.312), channel_id=1, source_target_pairs={{0,1},{1,2},{2,3},{3,4},{4,5},{5,6},{6,7},{7,8},{8,9},{9,10},{10,1... | collective-permute-start | bytes 24584 | tf_op jit(solution)/shard_map/ppermute | solution.py:31
  363.3 14.8 %copy-start = (f32[4,8,512]{2,1,0:T(8,128)}, f32[4,8,512]{2,1,0:T(8,128)S(1)}, u32[]{:S(2)}) copy-start(f32[4,8,512]{2,1,0:T(8,128)S(1)} %multiply_add_fusion.2) | copy-start | bytes 196612
  363.3 14.5 %collective-permute-start.44 = (f32[1,8,512]{2,1,0:T(8,128)S(1)}, f32[1,8,512]{2,1,0:T(8,128)S(1)}, u32[]{:S(2)}, u32[]{:S(2)}) collective-permute-start(f32[1,8,512]{2,1,0:T(8,128)S(1)} %get-tuple-element.307), channel_id=1, source_target_pairs={{16,0},{32,16},{48,32},{64,48},{80,64},{96,80},{112,96},{17,1},{33... | collective-permute-start | bytes 49160 | tf_op jit(solution)/shard_map/ppermute | solution.py:32
  369.3 8.5 %collective-permute-start.45 = (f32[1,8,512]{2,1,0:T(8,128)S(1)}, f32[1,8,512]{2,1,0:T(8,128)S(1)}, u32[]{:S(2)}, u32[]{:S(2)}) collective-permute-start(f32[1,8,512]{2,1,0:T(8,128)S(1)} %get-tuple-element.306), channel_id=1, source_target_pairs={{0,16},{16,32},{32,48},{48,64},{64,80},{80,96},{96,112},{1,17},{17... | collective-permute-start | bytes 49160 | tf_op jit(solution)/shard_map/ppermute | solution.py:31
  371.4 6.4 %collective-permute-start.46 = (f32[4,1,512]{2,1,0:T(1,128)S(1)}, f32[4,1,512]{2,1,0:T(1,128)S(1)}, u32[]{:S(2)}, u32[]{:S(2)}) collective-permute-start(f32[4,1,512]{2,1,0:T(1,128)S(1)} %get-tuple-element.309), channel_id=1, source_target_pairs={{1,0},{2,1},{3,2},{4,3},{5,4},{6,5},{7,6},{8,7},{9,8},{10,9},{11,1... | collective-permute-start | bytes 24584 | tf_op jit(solution)/shard_map/ppermute | solution.py:32
  372.7 5.1 %collective-permute-start.47 = (f32[4,1,512]{2,1,0:T(1,128)S(1)}, f32[4,1,512]{2,1,0:T(1,128)S(1)}, u32[]{:S(2)}, u32[]{:S(2)}) collective-permute-start(f32[4,1,512]{2,1,0:T(1,128)S(1)} %get-tuple-element.308), channel_id=1, source_target_pairs={{0,1},{1,2},{2,3},{3,4},{4,5},{5,6},{6,7},{7,8},{8,9},{9,10},{10,1... | collective-permute-start | bytes 24584 | tf_op jit(solution)/shard_map/ppermute | solution.py:31
  378.9 2.6 copy-start.3
  384.7 2.6 copy-start.3
  390.4 2.6 copy-start.3
  396.2 2.6 copy-start.3
  401.9 2.6 copy-start.3
  407.7 2.6 copy-start.3
  413.4 2.6 copy-start.3
  419.2 2.6 copy-start.3
  424.9 19.6 %copy-start.1 = (f32[1,128,3,128]{3,1,2,0:T(8,128)S(1)}, f32[1,128,3,128]{3,1,2,0:T(8,128)}, u32[]{:S(2)}) copy-start(f32[1,128,3,128]{3,1,2,0:T(8,128)} %param.12) | copy-start | bytes 589828
where the time goes:
time: 448 us; the launch traced here: 446 us
  starting transfers between devices  156 us (35%)
  blocking collectives  129 us (29%)
  matrix products  59.7 us (13%)
  local copies, waits for them, and re-layouts  30.9 us (7%)
  waiting for transfers between devices  30.5 us (7%)
  other arithmetic  25.7 us (6%)
  between operations  11.8 us (3%)
    psum x12, blocking collectives, one_axis_at_a_time(): x = lax.psum(x, axis)  110 us
    ppermute x24, starting transfers between devices, extended(): lax.ppermute(last, axis, up)  85.5 us
    ppermute x24, starting transfers between devices, extended(): lax.ppermute(first, axis, [(b, a) for a, b in up])  54.7 us
    dot_general x16, matrix products, pick(): jnp.dot(flat_field, onehot, precision=lax.Precision.HIGHEST, preferred_el...  33.6 us
    dot_general x16, matrix products, step(): jnp.dot(lifted.reshape(4 * plane, block_rows), onehot, precision=lax.Prec...  26.1 us
    all_to_all x2, waiting for transfers between devices, in_one_piece(): lax.all_to_all(both, axis, split_axis=split_dim, concat_axis=concat_dim,...  20.3 us
    all_to_all x1, blocking collectives, local(): lax.all_to_all(interpolated, GX_YZ, split_axis=0, concat_axis=1, tiled=True)  18.6 us
    all_to_all x2, starting transfers between devices, in_one_piece(): lax.all_to_all(both, axis, split_axis=split_dim, concat_axis=concat_dim,...  15.6 us
  transfers between devices with their start and end apart: 50, of which 12 were waited for; matrix products, arithmetic and copies ran while one was open for 2% of the time, Pallas kernels for 0%

commit v1 on v0

v1 whole, which is shorter than its diff:
```python
import jax
import jax.numpy as jnp
from jax import lax
from jax.experimental import pallas as pl
from jax.experimental.pallas import tpu as pltpu
from jax.sharding import PartitionSpec as P

ALL = ("gx", "yz")
DAMPING = 0.05
SOLID_WATER = 0.1
FLIP = 0.9
LOWER = 0.1
UPPER = 2.0
DEGREE = 3
GROUPS = 128
CAP = 128
FIELDS = 13
ROW_W = 3
ROW_M = 11
ROW_B = 12
CELLS = 32
DEPTH = 512
CHUNK = 8
HALO = 4
YE = 8 + 2 * HALO
XE = 16
PARAMS = pltpu.CompilerParams(vmem_limit_bytes=60 * 1024 * 1024)
VM = pl.BlockSpec(memory_space=pltpu.VMEM)
SM = pl.BlockSpec(memory_space=pltpu.SMEM)
F32 = jnp.float32
BF16 = jnp.bfloat16


def shape(*dims):
    return jax.ShapeDtypeStruct(dims, F32)


def split(value):
    high = value.astype(BF16)
    return high, (value - high.astype(F32)).astype(BF16)


def cells_of(msg, plane_s, depth_s):
    base = msg[pl.ds(ROW_B, GROUPS, stride=FIELDS), :].astype(jnp.int32)
    plane = base >> 9
    plane_s[...] = (plane & 7) * 4 + (plane >> 3)
    depth_s[...] = base & 511


def tile_weights(msg, source, plane_row):
    away = lax.broadcasted_iota(jnp.int32, (CELLS, CAP), 0) - plane_row
    here, next_y, next_x, next_xy = away == 0, away == 4, away == 1, away == 5
    zero = jnp.zeros((CELLS, CAP), F32)

    def weight(corner):
        row = msg[pl.ds(FIELDS * source + ROW_W + corner, 1), :]
        return jnp.broadcast_to(row, (CELLS, CAP))

    lifts = []
    for lift in (0, 1):
        value = jnp.where(next_xy, weight(6 + lift), zero)
        value = jnp.where(next_x, weight(4 + lift), value)
        value = jnp.where(next_y, weight(2 + lift), value)
        lifts.append(jnp.where(here, weight(lift), value))
    return jnp.concatenate(lifts, axis=0)


def depth_hot(depth_row):
    level = lax.broadcasted_iota(jnp.int32, (DEPTH, CAP), 0)
    return jnp.where(level == depth_row, 1.0, 0.0).astype(BF16)


def spread_kernel(msg, density, water, out, plane_s, depth_s, value_s, left_a, hot_a, left_b, hot_b, acc):
    cells_of(msg, plane_s, depth_s)
    mass = msg[pl.ds(ROW_M, GROUPS, stride=FIELDS), :]
    value_s[0] = mass
    for axis in range(3):
        value_s[1 + axis] = mass * msg[pl.ds(axis, GROUPS, stride=FIELDS), :]
    acc[...] = jnp.zeros_like(acc)

    def build(chunk, left, hot):
        for j in range(CHUNK):
            source = chunk * CHUNK + j
            columns = slice(j * CAP, (j + 1) * CAP)
            weights = tile_weights(msg, source, plane_s[pl.ds(source, 1), :])
            for f in range(4):
                high, low = split(weights * value_s[f, pl.ds(source, 1), :])
                left[f * 64 : (f + 1) * 64, columns] = high
                left[256 + f * 64 : 256 + (f + 1) * 64, columns] = low
            hot[:, columns] = depth_hot(depth_s[pl.ds(source, 1), :])

    def multiply(left, hot):
        acc[...] += lax.dot_general(
            left[...], hot[...], (((1,), (1,)), ((), ())), preferred_element_type=F32
        )

    turns = GROUPS // CHUNK // 2
    build(0, left_a, hot_a)

    def body(turn, carry):
        build(2 * turn + 1, left_b, hot_b)
        multiply(left_a, hot_a)

        @pl.when(turn < turns - 1)
        def _():
            build(2 * turn + 2, left_a, hot_a)

        multiply(left_b, hot_b)
        return carry

    lax.fori_loop(0, turns, body, 0)
    grid = []
    for f in range(4):
        both = acc[f * 64 : (f + 1) * 64, :] + acc[256 + f * 64 : 256 + (f + 1) * 64, :]
        grid.append(both[:CELLS] + pltpu.roll(both[CELLS:], 1, 1))
    total = grid[0] + density[...]
    out[0] = total
    for axis in range(3):
        out[1 + axis] = (grid[1 + axis] + density[...] * water[axis]) / total


def spread(msg, density, water):
    operand = pltpu.VMEM((512, CHUNK * CAP), BF16)
    index = pltpu.VMEM((GROUPS, CAP), jnp.int32)
    return pl.pallas_call(
        spread_kernel,
        out_shape=shape(4, CELLS, DEPTH),
        in_specs=[VM] * 3,
        out_specs=VM,
        scratch_shapes=[index, index, pltpu.VMEM((4, GROUPS, CAP), F32)]
        + [operand] * 4
        + [pltpu.VMEM((512, DEPTH), F32)],
        compiler_params=PARAMS,
        name="spread",
    )(msg, density, water)


def next_x(row):
    return pltpu.roll(row, XE - 1, 0)


def prev_x(row):
    return pltpu.roll(row, 1, 0)


def next_z(row):
    return pltpu.roll(row, DEPTH - 1, 1)


def prev_z(row):
    return pltpu.roll(row, 1, 1)


def each_row(first, last, body):
    def step(y, carry):
        body(y)
        return carry

    lax.fori_loop(first, last, step, 0)


def operate_row(field, y, offset, beta_x, beta_y, beta_z):
    here = field[y - offset]
    flux_x = beta_x[y] * (here - next_x(here))
    flux_z = beta_z[y] * (here - next_z(here))
    flux_y = beta_y[y] * (here - field[y - offset + 1])
    from_y = beta_y[y - 1] * (field[y - offset - 1] - here)
    return (
        DAMPING * here
        + (flux_x - prev_x(flux_x))
        + (flux_y - from_y)
        + (flux_z - prev_z(flux_z))
    )


def place(ext, own, low_x, high_x, low_y, high_y, fix):
    for block, source in enumerate((low_x, own, high_x)):
        columns = slice(4 * block, 4 * block + 4)
        for y in range(8):
            ext[HALO + y, columns, :] = fix(source(slice(4 * y, 4 * y + 4)), block, 1)
        for y in range(HALO):
            rows = slice(4 * y, 4 * y + 4)
            ext[y, columns, :] = fix(low_y(block, rows), block, 0)
            ext[HALO + 8 + y, columns, :] = fix(high_y(block, rows), block, 2)


def precondition(residual, inverse, beta_x, beta_y, beta_z, update, first, second, finish):
    theta = (UPPER + LOWER) / 2.0
    delta = (UPPER - LOWER) / 2.0
    sigma = theta / delta

    def start(y):
        value = inverse[y] * residual[y] * (1.0 / theta)
        update[y] = value
        first[y] = value

    each_row(1, YE - 1, start)
    previous = 1.0 / sigma
    current = 1.0 / (2.0 * sigma - previous)

    def middle(y):
        misfit = residual[y] - operate_row(first, y, 0, beta_x, beta_y, beta_z)
        value = current * previous * update[y] + (2.0 * current / delta) * inverse[y] * misfit
        update[y] = value
        second[y] = first[y] + value

    each_row(2, YE - 2, middle)
    latest = 1.0 / (2.0 * sigma - current)

    def last(y):
        misfit = residual[y] - operate_row(second, y, 0, beta_x, beta_y, beta_z)
        value = latest * current * update[y] + (2.0 * latest / delta) * inverse[y] * misfit
        finish(y, second[y] + value)

    each_row(3, YE - 3, last)


def each_pair(body):
    def step(pair, carry):
        y = HALO + 2 * pair
        rows = pl.ds(pl.multiple_of(8 * pair, 8), 8)
        lower_half = lax.broadcasted_iota(jnp.int32, (8, DEPTH), 0) < 4
        for ref, first, second in zip(*body(y)):
            ref[rows, :] = jnp.where(lower_half, pltpu.roll(first[:8], 4, 0), second[:8])
        return carry

    lax.fori_loop(0, 4, step, 0)


def start_kernel(
    edge, own, low_x, high_x, low_y, high_y,
    beta_x, beta_y, beta_z, inverse, basis, basis_own, image, source_own,
    ext, residual, update, first, second,
):
    infinite = jnp.full((4, DEPTH), jnp.inf, F32)
    for f in range(4):
        ext[f, :, 12:16, :] = jnp.full((YE, 4, DEPTH), jnp.inf if f == 0 else 0.0, F32)

        def fix(value, block, row, f=f):
            if f or (block == 1 and row == 1):
                return value
            outside = 0
            if block != 1:
                outside = outside + edge[0 if block == 0 else 1]
            if row != 1:
                outside = outside + edge[2 if row == 0 else 3]
            return jnp.where(outside > 0, infinite, value)

        place(
            ext.at[f],
            lambda rows, f=f: own[f, rows, :],
            lambda rows, f=f: low_x[f, rows, :],
            lambda rows, f=f: high_x[f, rows, :],
            lambda block, rows, f=f: low_y[block, f, rows, :],
            lambda block, rows, f=f: high_y[block, f, rows, :],
            fix,
        )
    end = lax.broadcasted_iota(jnp.int32, (XE, DEPTH), 1) == DEPTH - 1

    def faces(y):
        total = ext[0, y]
        beta_x[y] = 2.0 / (total + next_x(total))
        beta_y[y] = 2.0 / (total + ext[0, y + 1])
        beta_z[y] = jnp.where(end, 0.0, 2.0 / (total + next_z(total)))

    each_row(0, YE - 1, faces)

    def source(y):
        across, along = beta_x[y], beta_z[y]
        diagonal = (
            DAMPING + across + prev_x(across) + beta_y[y] + beta_y[y - 1] + along + prev_z(along)
        )
        inverse[y] = 1.0 / diagonal
        vx, vy, vz = ext[1, y], ext[2, y], ext[3, y]
        flow_x = across * (vx + next_x(vx))
        flow_z = along * (vz + next_z(vz))
        flow_y = beta_y[y] * (vy + ext[2, y + 1]) - beta_y[y - 1] * (ext[2, y - 1] + vy)
        residual[y] = -0.5 * (
            (flow_x - prev_x(flow_x)) + flow_y + (flow_z - prev_z(flow_z))
        )

    each_row(1, YE - 1, source)

    def finish(y, value):
        basis[y - 3] = value

    precondition(residual, inverse, beta_x, beta_y, beta_z, update, first, second, finish)

    def apply(y):
        return operate_row(basis, y, 3, beta_x, beta_y, beta_z), basis[y - 3], residual[y]

    each_pair(lambda y: ((image, basis_own, source_own), apply(y), apply(y + 1)))


EXT = (YE, XE, DEPTH)
BASIS = (10, XE, DEPTH)
BLOCK = (CELLS, DEPTH)


def start_solve(edge, own, low_x, high_x, low_y, high_y):
    return pl.pallas_call(
        start_kernel,
        out_shape=[shape(*EXT)] * 4 + [shape(*BASIS)] + [shape(*BLOCK)] * 3,
        in_specs=[SM] + [VM] * 5,
        out_specs=[VM] * 8,
        scratch_shapes=[pltpu.VMEM((4,) + EXT, F32)] + [pltpu.VMEM(EXT, F32)] * 4,
        compiler_params=PARAMS,
        name="start_solve",
    )(edge, own, low_x, high_x, low_y, high_y)


def next_basis(own, low_x, high_x, low_y, high_y, betas, inverse, before, basis, basis_own, image, scratch):
    ext, update, first, second = scratch
    ext[:, 12:16, :] = jnp.zeros((YE, 4, DEPTH), F32)
    place(
        ext,
        lambda rows: own[rows, :],
        lambda rows: low_x[rows, :],
        lambda rows: high_x[rows, :],
        lambda block, rows: low_y[block, rows, :],
        lambda block, rows: high_y[block, rows, :],
        lambda value, block, row: value,
    )

    def finish(y, value):
        basis[y - 3] = before[y - 3] - value

    precondition(ext, inverse, *betas, update, first, second, finish)

    def apply(y):
        return operate_row(basis, y, 3, *betas), basis[y - 3]

    each_pair(lambda y: ((image, basis_own), apply(y), apply(y + 1)))


def middle_kernel(
    own, low_x, high_x, low_y, high_y, beta_x, beta_y, beta_z, inverse, before,
    basis, basis_own, image, *scratch,
):
    next_basis(
        own, low_x, high_x, low_y, high_y, (beta_x, beta_y, beta_z), inverse, before,
        basis, basis_own, image, scratch,
    )


def last_kernel(
    own, low_x, high_x, low_y, high_y, beta_x, beta_y, beta_z, inverse, before,
    own_0, own_1, image_0, source_own, basis, sums, own_2, image_2, *scratch,
):
    next_basis(
        own, low_x, high_x, low_y, high_y, (beta_x, beta_y, beta_z), inverse, before,
        basis, own_2, image_2, scratch,
    )
    vectors = (own_0[...], own_1[...], own_2[...])
    images = (image_0[...], own[...], image_2[...])
    source = source_own[...]
    pairs = [(vectors[i], images[j]) for i in range(3) for j in range(i, 3)]
    pairs += [(vector, source) for vector in vectors]
    lane = lax.broadcasted_iota(jnp.int32, (1, CAP), 1)
    row = jnp.zeros((1, CAP), F32)
    for place_in, (a, b) in enumerate(pairs):
        folded = jnp.sum((a * b).reshape(4, 8, DEPTH), axis=0)
        folded = (folded[:, :128] + folded[:, 128:256]) + (folded[:, 256:384] + folded[:, 384:])
        row = jnp.where(lane == place_in, jnp.sum(folded, keepdims=True), row)
    sums[...] = jnp.broadcast_to(row, (GROUPS, CAP))


def middle_solve(own, low_x, high_x, low_y, high_y, betas, inverse, before):
    return pl.pallas_call(
        middle_kernel,
        out_shape=[shape(*BASIS), shape(*BLOCK), shape(*BLOCK)],
        in_specs=[VM] * 10,
        out_specs=[VM] * 3,
        scratch_shapes=[pltpu.VMEM(EXT, F32)] * 4,
        compiler_params=PARAMS,
        name="middle_solve",
    )(own, low_x, high_x, low_y, high_y, *betas, inverse, before)


def last_solve(own, low_x, high_x, low_y, high_y, betas, inverse, before, *inner):
    return pl.pallas_call(
        last_kernel,
        out_shape=[shape(*BASIS), shape(GROUPS, CAP)],
        in_specs=[VM] * 14,
        out_specs=[VM] * 2,
        scratch_shapes=[pltpu.VMEM(BLOCK, F32)] * 2 + [pltpu.VMEM(EXT, F32)] * 4,
        compiler_params=PARAMS,
        name="last_solve",
    )(own, low_x, high_x, low_y, high_y, *betas, inverse, before, *inner)


def coefficients(sums):
    total = jnp.sum(sums[...], axis=0, keepdims=True)
    g00, g01, g02, g11, g12, g22, b0, b1, b2 = [total[:, k : k + 1] for k in range(9)]
    l1 = g01 / g00
    l2 = g02 / g00
    d1 = g11 - l1 * g01
    keep_1 = d1 > 1e-7 * g11
    d1 = jnp.where(keep_1, d1, 1.0)
    m = jnp.where(keep_1, (g12 - l2 * g01) / d1, 0.0)
    d2 = g22 - l2 * g02 - m * m * d1
    keep_2 = d2 > 1e-7 * g22
    d2 = jnp.where(keep_2, d2, 1.0)
    y1 = b1 - l1 * b0
    y2 = b2 - l2 * b0 - m * y1
    c2 = jnp.where(keep_2, y2 / d2, 0.0)
    c1 = jnp.where(keep_1, y1 / d1, 0.0) - m * c2
    c0 = b0 / g00 - l1 * c1 - l2 * c2
    return c0, c1, c2


def gather_kernel(
    sums, basis_0, basis_1, basis_2, beta_x, beta_y, beta_z, own, msg,
    out, pressure_out, plane_s, depth_s, pressure, carried, high_s, low_s,
):
    c0, c1, c2 = [jnp.broadcast_to(c, (XE, DEPTH)) for c in coefficients(sums)]

    def combine(y):
        pressure[y] = c0 * basis_0[y] + c1 * basis_1[y] + c2 * basis_2[y]

    each_row(0, 10, combine)

    def slopes(y):
        here = pressure[y - 3]
        flux_x = beta_x[y] * (here - next_x(here))
        flux_z = beta_z[y] * (here - next_z(here))
        flux_y = beta_y[y] * (here - pressure[y - 2])
        from_y = beta_y[y - 1] * (pressure[y - 4] - here)
        return (
            (flux_x + prev_x(flux_x)) * 0.5,
            (flux_y + from_y) * 0.5,
            (flux_z + prev_z(flux_z)) * 0.5,
            here,
        )

    targets = (carried.at[0], carried.at[1], carried.at[2], pressure_out)
    each_pair(lambda y: (targets, slopes(y), slopes(y + 1)))
    for axis in range(3):
        velocity = own[1 + axis]
        value = (velocity + carried[axis]) - FLIP * velocity
        for lift, level in ((0, value), (1, next_z(value))):
            high, low = split(level)
            rows = slice(axis * 64 + lift * CELLS, axis * 64 + (lift + 1) * CELLS)
            high_s[rows, :] = high
            low_s[rows, :] = low
    cells_of(msg, plane_s, depth_s)

    def body(chunk, carry):
        hots = [depth_hot(depth_s[pl.ds(chunk * CHUNK + j, 1), :]) for j in range(CHUNK)]
        hot = jnp.concatenate(hots, axis=1)
        table = jnp.dot(high_s[...], hot, preferred_element_type=F32)
        table = table + jnp.dot(low_s[...], hot, preferred_element_type=F32)
        for j in range(CHUNK):
            source = chunk * CHUNK + j
            weights = tile_weights(msg, source, plane_s[pl.ds(source, 1), :])
            for axis in range(3):
                picked = table[axis * 64 : (axis + 1) * 64, j * CAP : (j + 1) * CAP] * weights
                out[pl.ds(3 * source + axis, 1), :] = jnp.sum(picked, axis=0, keepdims=True)
        return carry

    lax.fori_loop(0, GROUPS // CHUNK, body, 0)


def gather(sums, bases, betas, own, msg):
    index = pltpu.VMEM((GROUPS, CAP), jnp.int32)
    operand = pltpu.VMEM((192, DEPTH), BF16)
    return pl.pallas_call(
        gather_kernel,
        out_shape=[shape(3 * GROUPS, CAP), shape(*BLOCK)],
        in_specs=[VM] * 9,
        out_specs=[VM] * 2,
        scratch_shapes=[index, index, pltpu.VMEM(BASIS, F32), pltpu.VMEM((3,) + BLOCK, F32), operand, operand],
        compiler_params=PARAMS,
        name="gather",
    )(sums, *bases, *betas, own, msg)


def exchange(block, n_x, n_y):
    up_x = [(i, (i + 1) % n_x) for i in range(n_x)]
    up_y = [(i, (i + 1) % n_y) for i in range(n_y)]
    low_x = lax.ppermute(block, "gx", up_x)
    high_x = lax.ppermute(block, "gx", [(b, a) for a, b in up_x])
    half = CELLS // 2
    upper = jnp.stack([b[..., half:, :] for b in (low_x, block, high_x)])
    lower = jnp.stack([b[..., :half, :] for b in (low_x, block, high_x)])
    low_y = lax.ppermute(upper, "yz", up_y)
    high_y = lax.ppermute(lower, "yz", [(b, a) for a, b in up_y])
    return low_x, high_x, low_y, high_y


def by_block(field):
    turned = jnp.swapaxes(field, -3, -2)
    return turned.reshape(turned.shape[:-3] + (CELLS, DEPTH))


def local(part_mass, part_vel, corner_weight, corner_base, slot_counts, water_vel, solid_flag):
    n_x, n_y = lax.axis_size("gx"), lax.axis_size("yz")
    at_x, at_y = lax.axis_index("gx"), lax.axis_index("yz")
    edge = jnp.stack([at_x == 0, at_x == n_x - 1, at_y == 0, at_y == n_y - 1]).astype(jnp.int32)
    slot = jnp.arange(CAP, dtype=jnp.int32)
    live = (slot[None, :] < slot_counts[0][:, None]).astype(F32)
    masses = part_mass[0] * live
    message = jnp.concatenate(
        [part_vel[0], corner_weight[0], masses[:, None], corner_base[0].astype(F32)[:, None]], axis=1
    )
    msg = lax.all_to_all(message.reshape(GROUPS, FIELDS * CAP), ALL, 0, 0, tiled=True)
    msg = msg.reshape(GROUPS * FIELDS, CAP)
    density = by_block(jnp.where(solid_flag == 1, SOLID_WATER, 1.0).astype(F32))
    own = spread(msg, density, by_block(water_vel))
    *rest, basis_0, own_0, image_0, source = start_solve(edge, own, *exchange(own, n_x, n_y))
    betas, inverse = rest[:3], rest[3]
    basis_1, own_1, image_1 = middle_solve(image_0, *exchange(image_0, n_x, n_y), betas, inverse, basis_0)
    basis_2, sums = last_solve(
        image_1, *exchange(image_1, n_x, n_y), betas, inverse, basis_1, own_0, own_1, image_0, source
    )
    sums = lax.all_to_all(sums, ALL, 0, 0, tiled=True)
    sampled, pressure = gather(sums, (basis_0, basis_1, basis_2), betas, own, msg)
    returned = lax.all_to_all(sampled.reshape(GROUPS, 3 * CAP), ALL, 0, 0, tiled=True)
    returned = returned.reshape(1, GROUPS, 3, CAP)
    pressure = jnp.swapaxes(pressure.reshape(8, 4, DEPTH), 0, 1)
    return FLIP * part_vel + returned, pressure


def solution(mesh):
    parts = P(ALL, None, None)
    in_specs = (parts, P(ALL, None, None, None), P(ALL, None, None, None), parts, P(ALL, None), P(None, "gx", "yz", None), P("gx", "yz", None))
    out_specs = (P(ALL, None, None, None), P("gx", "yz", None))
    return jax.shard_map(local, mesh=mesh, in_specs=in_specs, out_specs=out_specs, check_vma=False)
```

time: 448 us -> 189 us (0.42)
  starting transfers between devices: 156 us -> 39.5 us
  blocking collectives: 129 us -> 20.9 us
  Pallas kernels: 0 us -> 65.8 us
  matrix products: 59.7 us -> 0 us
  other arithmetic: 25.7 us -> 0.84 us
  local copies, waits for them, and re-layouts: 30.9 us -> 18.6 us
  waiting for transfers between devices: 30.5 us -> 42.1 us
  between operations: 11.8 us -> 0.91 us
    ppermute x48 -> x12, starting transfers between devices: 140 us -> 23.6 us  [the longest x3 14.5 us: exchange(): high_y = lax.ppermute(lower, 'yz', [(b, a) for a, b in up_y])]
    psum x12 -> x0, blocking collectives: 110 us -> none  [one_axis_at_a_time(): x = lax.psum(x, axis)]
    pallas_call x0 -> x5, Pallas kernels: none -> 65.8 us  [the longest x1 25.8 us: spread(): pl.pallas_call(spread_kernel, out_shape=shape(4, CELLS, DEPTH), in_specs=...]
    dot_general x32 -> x0, matrix products: 59.7 us -> none  [the longest x16 33.6 us: pick(): jnp.dot(flat_field, onehot, precision=lax.Precision.HIGHEST, preferred_el...]
    dynamic_slice x16 -> x0, local copies, waits for them, and re-layouts: 15.1 us -> none  [spread_grid(): lax.scan(step, start, (value_blocks, plane_blocks, depth_blocks))]
    reduce_sum x13 -> x0, other arithmetic: 9.88 us -> none  [the longest x8 6.4 us: pick(): jnp.sum(table * masks[corner_pair][None], axis=1)]
    unnamed x10 -> x47, local copies, waits for them, and re-layouts: 1.77 us -> 11.5 us
    ppermute x48 -> x12, waiting for transfers between devices: 10.2 us -> 16.7 us  [the longest x3 11.1 us: exchange(): low_y = lax.ppermute(upper, 'yz', up_y)]
  transfers between devices with their start and end apart: 50 -> 14, of which waited for: 12 -> 9; matrix products, arithmetic and copies ran while one was open for 2% -> 3% of each run, Pallas kernels for 0% -> 0%
where the time goes in v1:
time: 189 us
  Pallas kernels  65.8 us (35%)
  waiting for transfers between devices  42.1 us (22%)
  starting transfers between devices  39.5 us (21%)
  blocking collectives  20.9 us (11%)
  local copies, waits for them, and re-layouts  18.6 us (10%)
    pallas_call x1, Pallas kernels, spread(): pl.pallas_call(spread_kernel, out_shape=shape(4, CELLS, DEPTH), in_specs=...  25.8 us
    all_to_all x1, blocking collectives, local(): sums = lax.all_to_all(sums, ALL, 0, 0, tiled=True)  20.9 us
    pallas_call x1, Pallas kernels, gather(): pl.pallas_call(gather_kernel, out_shape=[shape(3 * GROUPS, CAP), shape(*B...  15.7 us
    all_to_all x1, waiting for transfers between devices, local(): lax.all_to_all(message.reshape(GROUPS, FIELDS * CAP), ALL, 0, 0, tiled=True)  15.4 us
    ppermute x3, starting transfers between devices, exchange(): high_y = lax.ppermute(lower, 'yz', [(b, a) for a, b in up_y])  14.5 us
    unnamed x47, local copies, waits for them, and re-layouts  11.5 us
    all_to_all x1, starting transfers between devices, local(): lax.all_to_all(message.reshape(GROUPS, FIELDS * CAP), ALL, 0, 0, tiled=True)  11.5 us
    ppermute x3, waiting for transfers between devices, exchange(): low_y = lax.ppermute(upper, 'yz', up_y)  11.1 us
  transfers between devices with their start and end apart: 14, of which 9 were waited for; matrix products, arithmetic and copies ran while one was open for 3% of the time, Pallas kernels for 0%

profile of v1, /device:TPU:1, one launch (start us, length us, event | category | flops | bytes accessed | tf_op | source)
XLA Modules:
  0.0 188.7 jit_solution(998711569425543239)
XLA Ops:
  0.6 1.0 copy.28
  1.7 0.9 copy.29
  2.6 0.1 copy.25
  2.8 0.2 copy.27
  3.0 0.0 copy-start.20
  3.0 0.7 copy-done.20
  3.7 0.1 pad_maximum_fusion
  3.7 2.0 %copy.30 = f32[128,1,1664]{2,1,0:T(1,128)} copy(f32[128,1,1664]{0,2,1:T(8,128)S(1)} %bitcast.63) | data formatting | bytes 1703936 | tf_op jit(solution)/shard_map/all_to_all | solution.py:506
  5.8 11.5 %all-to-all-start = ((f32[128,1,1664]{2,1,0:T(1,128)}), f32[128,1,1664]{2,1,0:T(1,128)S(1)}, u32[]{:S(2)}, u32[]{:S(2)}) async-start(f32[128,1,1664]{2,1,0:T(1,128)} %copy.30), calls=%async_computation | async-start | bytes 1703936 | tf_op jit(solution)/shard_map/all_to_all | solution.py:506
  17.3 0.0 copy-start.13
  17.3 0.7 reshape.91.density
  18.0 0.2 copy-done.13
  18.2 0.1 copy.32
  18.3 0.7 reshape.92.water
  19.1 15.4 %all-to-all-done = f32[128,1,1664]{2,1,0:T(1,128)S(1)} async-done(((f32[128,1,1664]{2,1,0:T(1,128)}), f32[128,1,1664]{2,1,0:T(1,128)S(1)}, u32[]{:S(2)}, u32[]{:S(2)}) %all-to-all-start) | async-done | bytes 852000 | tf_op jit(solution)/shard_map/all_to_all | solution.py:506
  34.5 0.9 copy-done
  35.4 25.8 %spread.1.own = f32[4,32,512]{2,1,0:T(8,128)} custom-call(f32[1664,128]{1,0:T(8,128)} %bitcast.61, f32[32,512]{1,0:T(8,128)} %reshape.91.density, f32[3,32,512]{2,1,0:T(8,128)} %reshape.92.water), custom_call_target="tpu_custom_call" | custom-call | tf_op jit(solution)/shard_map/spread/pallas_call | solution.py:125
  61.2 0.8 collective-permute-start.1
  62.0 0.9 collective-permute-start
  62.9 1.0 slice_bitcast_fusion.1
  63.9 3.6 %collective-permute-done.1.high_x = f32[4,32,512]{2,1,0:T(8,128)S(1)} collective-permute-done((f32[4,32,512]{2,1,0:T(8,128)}, f32[4,32,512]{2,1,0:T(8,128)S(1)}, u32[]{:S(2)}, u32[]{:S(2)}) %collective-permute-start.1) | collective-permute-done | bytes 262176 | tf_op jit(solution)/shard_map/ppermute | solution.py:482
  67.5 0.7 copy-done.1
  68.2 0.7 copy-done.2
  68.9 0.4 collective-permute-start.2
  69.4 4.5 %collective-permute-start.3 = (f32[3,4,16,512]{3,2,1,0:T(8,128)S(1)}, f32[3,4,16,512]{3,2,1,0:T(8,128)S(1)}, u32[]{:S(2)}, u32[]{:S(2)}) collective-permute-start(f32[3,4,16,512]{3,2,1,0:T(8,128)S(1)} %pad_maximum_fusion.2), channel_id=1, source_target_pairs={{1,0},{2,1},{3,2},{4,3},{5,4},{6,5},{7,6},{8,7},{9,8},{10,9},{11,1... | collective-permute-start | bytes 1179656 | tf_op jit(solution)/shard_map/ppermute | solution.py:487
  73.9 0.6 add_convert_fusion.edge
  74.5 7.3 %collective-permute-done.2.low_y = f32[3,4,16,512]{3,2,1,0:T(8,128)S(1)} collective-permute-done((f32[3,4,16,512]{3,2,1,0:T(8,128)S(1)}, f32[3,4,16,512]{3,2,1,0:T(8,128)S(1)}, u32[]{:S(2)}, u32[]{:S(2)}) %collective-permute-start.2) | collective-permute-done | bytes 393248 | tf_op jit(solution)/shard_map/ppermute | solution.py:486
  81.8 0.0 collective-permute-done.3.high_y
  81.8 0.8 copy-done.5
  82.6 0.7 copy-done.6
  83.3 10.7 %start_solve.1 = (f32[16,16,512]{2,1,0:T(8,128)}, f32[16,16,512]{2,1,0:T(8,128)}, f32[16,16,512]{2,1,0:T(8,128)}, f32[16,16,512]{2,1,0:T(8,128)}, f32[10,16,512]...) custom-call(s32[4]{0:T(128)} %add_convert_fusion.edge, f32[4,32,512]{2,1,0:T(8,128)} %spread.1.own, ...), custom_call_target="tpu_custom_call" | custom-call | tf_op jit(solution)/shard_map/start_solve/pallas_call | solution.py:301
  94.0 2.1 %collective-permute-start.5 = (f32[32,512]{1,0:T(8,128)}, f32[32,512]{1,0:T(8,128)S(1)}, u32[]{:S(2)}, u32[]{:S(2)}) collective-permute-start(f32[32,512]{1,0:T(8,128)} %get-tuple-element.17.own.image_0), channel_id=1, source_target_pairs={{16,0},{32,16},{48,32},{64,48},{80,64},{96,80},{112,96},{0,112},{1... | collective-permute-start | bytes 196616 | tf_op jit(solution)/shard_map/ppermute | solution.py:482
  96.1 0.8 slice_bitcast_fusion.16
  96.9 0.5 collective-permute-start.4
  97.4 1.3 collective-permute-done.5.high_x
  98.7 0.6 copy-done.10
  99.3 0.0 collective-permute-done.4.low_x
  99.3 0.6 copy-done.11
  100.0 0.1 collective-permute-start.6
  100.1 4.8 %collective-permute-start.7 = (f32[3,16,512]{2,1,0:T(8,128)S(1)}, f32[3,16,512]{2,1,0:T(8,128)S(1)}, u32[]{:S(2)}, u32[]{:S(2)}) collective-permute-start(f32[3,16,512]{2,1,0:T(8,128)S(1)} %pad_maximum_fusion.4), channel_id=1, source_target_pairs={{1,0},{2,1},{3,2},{4,3},{5,4},{6,5},{7,6},{8,7},{9,8},{10,9},{11,1... | collective-permute-start | bytes 294920 | tf_op jit(solution)/shard_map/ppermute | solution.py:487
  104.9 1.9 %collective-permute-done.6.low_y = f32[3,16,512]{2,1,0:T(8,128)S(1)} collective-permute-done((f32[3,16,512]{2,1,0:T(8,128)S(1)}, f32[3,16,512]{2,1,0:T(8,128)S(1)}, u32[]{:S(2)}, u32[]{:S(2)}) %collective-permute-start.6) | collective-permute-done | bytes 98336 | tf_op jit(solution)/shard_map/ppermute | solution.py:486
  106.8 0.6 copy-done.15
  107.5 0.0 copy-done.17
  107.5 6.7 %middle_solve.1 = (f32[10,16,512]{2,1,0:T(8,128)}, f32[32,512]{1,0:T(8,128)}, f32[32,512]{1,0:T(8,128)}) custom-call(f32[32,512]{1,0:T(8,128)} %get-tuple-element.17.own.image_0, f32[32,512]{1,0:T(8,128)} %copy-done.11, f32[32,512]{1,0:T(8,128)} %copy-done.10, f32[3,16,512]{2,1,0:T(8,128)} %copy-done.15, f32[3,16,512]{2,1,0:T(8,128)} %copy-done.17, ...), custom_call_target="tpu_custom_call" | custom-call | tf_op jit(solution)/shard_map/middle_solve/pallas_call | solution.py:369
  114.2 4.2 %collective-permute-start.9 = (f32[32,512]{1,0:T(8,128)}, f32[32,512]{1,0:T(8,128)S(1)}, u32[]{:S(2)}, u32[]{:S(2)}) collective-permute-start(f32[32,512]{1,0:T(8,128)} %get-tuple-element.23.own), channel_id=1, source_target_pairs={{16,0},{32,16},{48,32},{64,48},{80,64},{96,80},{112,96},{0,112},{1... | collective-permute-start | bytes 196616 | tf_op jit(solution)/shard_map/ppermute | solution.py:482
  118.4 0.8 slice_bitcast_fusion.14
  119.2 0.0 collective-permute-start.8
  119.2 0.3 collective-permute-done.9.high_x
  119.5 0.6 copy-done.8
  120.1 0.4 collective-permute-done.8.low_x
  120.5 0.6 copy-done.9
  121.2 0.1 collective-permute-start.10
  121.3 5.2 %collective-permute-start.11 = (f32[3,16,512]{2,1,0:T(8,128)S(1)}, f32[3,16,512]{2,1,0:T(8,128)S(1)}, u32[]{:S(2)}, u32[]{:S(2)}) collective-permute-start(f32[3,16,512]{2,1,0:T(8,128)S(1)} %pad_maximum_fusion.6), channel_id=1, source_target_pairs={{1,0},{2,1},{3,2},{4,3},{5,4},{6,5},{7,6},{8,7},{9,8},{10,9},{11,1... | collective-permute-start | bytes 294920 | tf_op jit(solution)/shard_map/ppermute | solution.py:487
  126.4 1.9 %collective-permute-done.10.low_y = f32[3,16,512]{2,1,0:T(8,128)S(1)} collective-permute-done((f32[3,16,512]{2,1,0:T(8,128)S(1)}, f32[3,16,512]{2,1,0:T(8,128)S(1)}, u32[]{:S(2)}, u32[]{:S(2)}) %collective-permute-start.10) | collective-permute-done | bytes 98336 | tf_op jit(solution)/shard_map/ppermute | solution.py:486
  128.3 0.6 copy-done.14
  129.0 0.0 copy-done.16
  129.0 6.9 %last_solve.1 = (f32[10,16,512]{2,1,0:T(8,128)}, f32[128,128]{1,0:T(8,128)}) custom-call(f32[32,512]{1,0:T(8,128)} %get-tuple-element.23.own, f32[32,512]{1,0:T(8,128)} %copy-done.9, f32[32,512]{1,0:T(8,128)} %copy-done.8, f32[3,16,512]{2,1,0:T(8,128)} %copy-done.14, f32[3,16,512]{2,1,0:T(8,128)} %copy-done.16, f32[16,16,512]{2,1,0:T(8,128)} %get-tuple-element.18.beta_x, ...), custom_call_target="tpu_custom_call" | custom-call | tf_op jit(solution)/shard_map/last_solve/pallas_call | solution.py:381
  135.9 20.9 %all_to_all.29 = f32[128,1,128]{2,1,0:T(1,128)} all-to-all(f32[128,1,128]{2,1,0:T(1,128)} %bitcast.71), channel_id=1, replica_groups=mesh['gx'=8,'yz'=16] {'gx','yz'}, dimensions={0} | all-to-all | bytes 131072 | tf_op jit(solution)/shard_map/all_to_all | solution.py:516
  156.8 15.7 %gather.1 = (f32[384,128]{1,0:T(8,128)}, f32[32,512]{1,0:T(8,128)}) custom-call(f32[128,128]{1,0:T(8,128)} %bitcast.67, f32[10,16,512]{2,1,0:T(8,128)} %get-tuple-element.22.before.basis_0, f32[10,16,512]{2,1,0:T(8,128)} %get-tuple-element.24.before.basis_1, f32[10,16,512]{2,1,0:T(8,128)} %get-tuple-element.29.basis_2, ...), custom_call_target="tpu_custom_call" | custom-call | tf_op jit(solution)/shard_map/gather/pallas_call | solution.py:467
  172.6 4.4 %all-to-all-start.2 = ((f32[128,1,384]{2,1,0:T(1,128)}), f32[128,1,384]{2,1,0:T(1,128)S(1)}, u32[]{:S(2)}, u32[]{:S(2)}) async-start(f32[128,1,384]{2,1,0:T(1,128)} %bitcast.69), calls=%async_computation.2 | async-start | bytes 393216 | tf_op jit(solution)/shard_map/all_to_all | solution.py:518
  177.0 0.7 copy.39
  177.6 10.0 %all-to-all-done.2 = f32[128,1,384]{2,1,0:T(1,128)S(1)} async-done(((f32[128,1,384]{2,1,0:T(1,128)}), f32[128,1,384]{2,1,0:T(1,128)S(1)}, u32[]{:S(2)}, u32[]{:S(2)}) %all-to-all-start.2) | async-done | bytes 196640 | tf_op jit(solution)/shard_map/all_to_all | solution.py:518
  187.7 0.2 copy.35
  187.8 0.8 copy.37
  (46 shorter events, 0.3 us)
Async XLA Ops:
  0.6 2.0 %copy-start.12 = (f32[1,128,3,128]{3,1,2,0:T(8,128)S(1)}, f32[1,128,3,128]{3,1,2,0:T(8,128)}, u32[]{:S(2)}) copy-start(f32[1,128,3,128]{3,1,2,0:T(8,128)} %param.8) | copy-start | bytes 589828
  0.6 2.1 %copy-start.4 = (f32[1,128,8,128]{3,2,1,0:T(8,128)S(1)}, f32[1,128,8,128]{3,2,1,0:T(8,128)}, u32[]{:S(2)}) copy-start(f32[1,128,8,128]{3,2,1,0:T(8,128)} %param.9) | copy-start | bytes 1572868
  3.0 0.7 copy-start.20
  5.8 11.5 %copy-start.18 = (s32[4,8,512]{2,1,0:T(8,128)S(1)}, s32[4,8,512]{2,1,0:T(8,128)}, u32[]{:S(2)}) copy-start(s32[4,8,512]{2,1,0:T(8,128)} %param.13) | copy-start | bytes 196612
  5.8 28.7 %all-to-all-start = ((f32[128,1,1664]{2,1,0:T(1,128)}), f32[128,1,1664]{2,1,0:T(1,128)S(1)}, u32[]{:S(2)}, u32[]{:S(2)}) async-start(f32[128,1,1664]{2,1,0:T(1,128)} %copy.30), calls=%async_computation | async-start | bytes 1703936 | tf_op jit(solution)/shard_map/all_to_all | solution.py:506
  17.3 0.9 copy-start.13
  34.5 0.9 copy-start
  61.2 6.3 %collective-permute-start.1 = (f32[4,32,512]{2,1,0:T(8,128)}, f32[4,32,512]{2,1,0:T(8,128)S(1)}, u32[]{:S(2)}, u32[]{:S(2)}) collective-permute-start(f32[4,32,512]{2,1,0:T(8,128)} %spread.1.own), channel_id=1, source_target_pairs={{16,0},{32,16},{48,32},{64,48},{80,64},{96,80},{112,96},{0,112},{1... | collective-permute-start | bytes 786440 | tf_op jit(solution)/shard_map/ppermute | solution.py:482
  62.0 6.2 %collective-permute-start = (f32[4,32,512]{2,1,0:T(8,128)}, f32[4,32,512]{2,1,0:T(8,128)S(1)}, u32[]{:S(2)}, u32[]{:S(2)}) collective-permute-start(f32[4,32,512]{2,1,0:T(8,128)} %spread.1.own), channel_id=1, source_target_pairs={{0,16},{16,32},{32,48},{48,64},{64,80},{80,96},{96,112},{112,0},{1... | collective-permute-start | bytes 786440 | tf_op jit(solution)/shard_map/ppermute | solution.py:481
  67.5 0.7 copy-start.1
  68.2 0.7 copy-start.2
  68.9 12.9 %collective-permute-start.2 = (f32[3,4,16,512]{3,2,1,0:T(8,128)S(1)}, f32[3,4,16,512]{3,2,1,0:T(8,128)S(1)}, u32[]{:S(2)}, u32[]{:S(2)}) collective-permute-start(f32[3,4,16,512]{3,2,1,0:T(8,128)S(1)} %pad_maximum_fusion.1), channel_id=1, source_target_pairs={{0,1},{1,2},{2,3},{3,4},{4,5},{5,6},{6,7},{7,8},{8,9},{9,10},{10,1... | collective-permute-start | bytes 1179656 | tf_op jit(solution)/shard_map/ppermute | solution.py:486
  69.4 12.4 %collective-permute-start.3 = (f32[3,4,16,512]{3,2,1,0:T(8,128)S(1)}, f32[3,4,16,512]{3,2,1,0:T(8,128)S(1)}, u32[]{:S(2)}, u32[]{:S(2)}) collective-permute-start(f32[3,4,16,512]{3,2,1,0:T(8,128)S(1)} %pad_maximum_fusion.2), channel_id=1, source_target_pairs={{1,0},{2,1},{3,2},{4,3},{5,4},{6,5},{7,6},{8,7},{9,8},{10,9},{11,1... | collective-permute-start | bytes 1179656 | tf_op jit(solution)/shard_map/ppermute | solution.py:487
  81.8 0.8 copy-start.5
  82.6 0.7 copy-start.6
  94.0 2.9 %copy-start.3 = (f32[32,512]{1,0:T(8,128)S(1)}, f32[32,512]{1,0:T(8,128)}, u32[]{:S(2)}) copy-start(f32[32,512]{1,0:T(8,128)} %get-tuple-element.17.own.image_0) | copy-start | bytes 196612
  94.0 4.7 %collective-permute-start.5 = (f32[32,512]{1,0:T(8,128)}, f32[32,512]{1,0:T(8,128)S(1)}, u32[]{:S(2)}, u32[]{:S(2)}) collective-permute-start(f32[32,512]{1,0:T(8,128)} %get-tuple-element.17.own.image_0), channel_id=1, source_target_pairs={{16,0},{32,16},{48,32},{64,48},{80,64},{96,80},{112,96},{0,112},{1... | collective-permute-start | bytes 196616 | tf_op jit(solution)/shard_map/ppermute | solution.py:482
  96.9 2.5 %collective-permute-start.4 = (f32[32,512]{1,0:T(8,128)S(1)}, f32[32,512]{1,0:T(8,128)S(1)}, u32[]{:S(2)}, u32[]{:S(2)}) collective-permute-start(f32[32,512]{1,0:T(8,128)S(1)} %copy-done.3), channel_id=1, source_target_pairs={{0,16},{16,32},{32,48},{48,64},{64,80},{80,96},{96,112},{112,0},{1... | collective-permute-start | bytes 196616 | tf_op jit(solution)/shard_map/ppermute | solution.py:481
  98.7 0.6 copy-start.10
  99.3 0.6 copy-start.11
  100.0 6.9 %collective-permute-start.6 = (f32[3,16,512]{2,1,0:T(8,128)S(1)}, f32[3,16,512]{2,1,0:T(8,128)S(1)}, u32[]{:S(2)}, u32[]{:S(2)}) collective-permute-start(f32[3,16,512]{2,1,0:T(8,128)S(1)} %pad_maximum_fusion.3), channel_id=1, source_target_pairs={{0,1},{1,2},{2,3},{3,4},{4,5},{5,6},{6,7},{7,8},{8,9},{9,10},{10,1... | collective-permute-start | bytes 294920 | tf_op jit(solution)/shard_map/ppermute | solution.py:486
  100.1 6.8 %collective-permute-start.7 = (f32[3,16,512]{2,1,0:T(8,128)S(1)}, f32[3,16,512]{2,1,0:T(8,128)S(1)}, u32[]{:S(2)}, u32[]{:S(2)}) collective-permute-start(f32[3,16,512]{2,1,0:T(8,128)S(1)} %pad_maximum_fusion.4), channel_id=1, source_target_pairs={{1,0},{2,1},{3,2},{4,3},{5,4},{6,5},{7,6},{8,7},{9,8},{10,9},{11,1... | collective-permute-start | bytes 294920 | tf_op jit(solution)/shard_map/ppermute | solution.py:487
  106.8 0.6 copy-start.15
  106.8 0.7 copy-start.17
  114.2 5.0 %copy-start.7 = (f32[32,512]{1,0:T(8,128)S(1)}, f32[32,512]{1,0:T(8,128)}, u32[]{:S(2)}) copy-start(f32[32,512]{1,0:T(8,128)} %get-tuple-element.23.own) | copy-start | bytes 196612
  114.2 5.3 %collective-permute-start.9 = (f32[32,512]{1,0:T(8,128)}, f32[32,512]{1,0:T(8,128)S(1)}, u32[]{:S(2)}, u32[]{:S(2)}) collective-permute-start(f32[32,512]{1,0:T(8,128)} %get-tuple-element.23.own), channel_id=1, source_target_pairs={{16,0},{32,16},{48,32},{64,48},{80,64},{96,80},{112,96},{0,112},{1... | collective-permute-start | bytes 196616 | tf_op jit(solution)/shard_map/ppermute | solution.py:482
  119.2 1.3 collective-permute-start.8
  119.5 0.6 copy-start.8
  120.5 0.6 copy-start.9
  121.2 7.2 %collective-permute-start.10 = (f32[3,16,512]{2,1,0:T(8,128)S(1)}, f32[3,16,512]{2,1,0:T(8,128)S(1)}, u32[]{:S(2)}, u32[]{:S(2)}) collective-permute-start(f32[3,16,512]{2,1,0:T(8,128)S(1)} %pad_maximum_fusion.5), channel_id=1, source_target_pairs={{0,1},{1,2},{2,3},{3,4},{4,5},{5,6},{6,7},{7,8},{8,9},{9,10},{10,1... | collective-permute-start | bytes 294920 | tf_op jit(solution)/shard_map/ppermute | solution.py:486
  121.3 7.1 %collective-permute-start.11 = (f32[3,16,512]{2,1,0:T(8,128)S(1)}, f32[3,16,512]{2,1,0:T(8,128)S(1)}, u32[]{:S(2)}, u32[]{:S(2)}) collective-permute-start(f32[3,16,512]{2,1,0:T(8,128)S(1)} %pad_maximum_fusion.6), channel_id=1, source_target_pairs={{1,0},{2,1},{3,2},{4,3},{5,4},{6,5},{7,6},{8,7},{9,8},{10,9},{11,1... | collective-permute-start | bytes 294920 | tf_op jit(solution)/shard_map/ppermute | solution.py:487
  128.3 0.6 copy-start.14
  128.3 0.7 copy-start.16
  172.6 4.4 %copy-start.19 = (f32[32,512]{1,0:T(8,128)S(1)}, f32[32,512]{1,0:T(8,128)}, u32[]{:S(2)}) copy-start(f32[32,512]{1,0:T(8,128)} %get-tuple-element.31) | copy-start | bytes 196612
  172.6 15.1 %all-to-all-start.2 = ((f32[128,1,384]{2,1,0:T(1,128)}), f32[128,1,384]{2,1,0:T(1,128)S(1)}, u32[]{:S(2)}, u32[]{:S(2)}) async-start(f32[128,1,384]{2,1,0:T(1,128)} %bitcast.69), calls=%async_computation.2 | async-start | bytes 393216 | tf_op jit(solution)/shard_map/all_to_all | solution.py:518

commit v2 on v1

--- a/solution.py
+++ b/solution.py
@@ -24,7 +24,7 @@
 HALO = 4
 YE = 8 + 2 * HALO
 XE = 16
-PARAMS = pltpu.CompilerParams(vmem_limit_bytes=60 * 1024 * 1024)
+PARAMS = pltpu.CompilerParams(vmem_limit_bytes=20 * 1024 * 1024)
 VM = pl.BlockSpec(memory_space=pltpu.VMEM)
 SM = pl.BlockSpec(memory_space=pltpu.SMEM)
 F32 = jnp.float32
@@ -35,9 +35,14 @@
     return jax.ShapeDtypeStruct(dims, F32)
 
 
-def split(value):
-    high = value.astype(BF16)
-    return high, (value - high.astype(F32)).astype(BF16)
+def remainder(value):
+    return value - value.astype(BF16).astype(F32)
+
+
+def one_pass(left, right):
+    return lax.dot_general(
+        left, right, (((1,), (0,)), ((), ())), precision=lax.Precision.DEFAULT, preferred_element_type=F32
+    )
 
 
 def cells_of(msg, plane_s, depth_s):
@@ -65,50 +70,42 @@
     return jnp.concatenate(lifts, axis=0)
 
 
-def depth_hot(depth_row):
-    level = lax.broadcasted_iota(jnp.int32, (DEPTH, CAP), 0)
-    return jnp.where(level == depth_row, 1.0, 0.0).astype(BF16)
-
-
 def spread_kernel(msg, density, water, out, plane_s, depth_s, value_s, left_a, hot_a, left_b, hot_b, acc):
     cells_of(msg, plane_s, depth_s)
+    depth_s[...] = depth_s[...].astype(F32).T.astype(jnp.int32)
     mass = msg[pl.ds(ROW_M, GROUPS, stride=FIELDS), :]
     value_s[0] = mass
     for axis in range(3):
         value_s[1 + axis] = mass * msg[pl.ds(axis, GROUPS, stride=FIELDS), :]
     acc[...] = jnp.zeros_like(acc)
+    level = lax.broadcasted_iota(jnp.int32, (CAP, DEPTH), 1)
 
     def build(chunk, left, hot):
+        depths = pltpu.roll(depth_s[...], (GROUPS - chunk * CHUNK) % GROUPS, 1)
         for j in range(CHUNK):
             source = chunk * CHUNK + j
             columns = slice(j * CAP, (j + 1) * CAP)
             weights = tile_weights(msg, source, plane_s[pl.ds(source, 1), :])
             for f in range(4):
-                high, low = split(weights * value_s[f, pl.ds(source, 1), :])
-                left[f * 64 : (f + 1) * 64, columns] = high
-                left[256 + f * 64 : 256 + (f + 1) * 64, columns] = low
-            hot[:, columns] = depth_hot(depth_s[pl.ds(source, 1), :])
+                value = weights * value_s[f, pl.ds(source, 1), :]
+                left[f * 64 : (f + 1) * 64, columns] = value
+                left[256 + f * 64 : 256 + (f + 1) * 64, columns] = remainder(value)
+            hot[columns, :] = jnp.where(level == depths[:, j : j + 1], 1.0, 0.0)
 
     def multiply(left, hot):
-        acc[...] += lax.dot_general(
-            left[...], hot[...], (((1,), (1,)), ((), ())), preferred_element_type=F32
-        )
-
-    turns = GROUPS // CHUNK // 2
+        acc[...] += one_pass(left[...], hot[...])
+
+    turns = GROUPS // CHUNK
     build(0, left_a, hot_a)
 
     def body(turn, carry):
         build(2 * turn + 1, left_b, hot_b)
         multiply(left_a, hot_a)
-
-        @pl.when(turn < turns - 1)
-        def _():
-            build(2 * turn + 2, left_a, hot_a)
-
+        build((2 * turn + 2) & (turns - 1), left_a, hot_a)
         multiply(left_b, hot_b)
         return carry
 
-    lax.fori_loop(0, turns, body, 0)
+    lax.fori_loop(0, turns // 2, body, 0)
     grid = []
     for f in range(4):
         both = acc[f * 64 : (f + 1) * 64, :] + acc[256 + f * 64 : 256 + (f + 1) * 64, :]
@@ -120,7 +117,8 @@
 
 
 def spread(msg, density, water):
-    operand = pltpu.VMEM((512, CHUNK * CAP), BF16)
+    left = pltpu.VMEM((512, CHUNK * CAP), F32)
+    hot = pltpu.VMEM((CHUNK * CAP, DEPTH), F32)
     index = pltpu.VMEM((GROUPS, CAP), jnp.int32)
     return pl.pallas_call(
         spread_kernel,
@@ -128,7 +126,7 @@
         in_specs=[VM] * 3,
         out_specs=VM,
         scratch_shapes=[index, index, pltpu.VMEM((4, GROUPS, CAP), F32)]
-        + [operand] * 4
+        + [left, hot, left, hot]
         + [pltpu.VMEM((512, DEPTH), F32)],
         compiler_params=PARAMS,
         name="spread",
@@ -411,7 +409,7 @@
 
 def gather_kernel(
     sums, basis_0, basis_1, basis_2, beta_x, beta_y, beta_z, own, msg,
-    out, pressure_out, plane_s, depth_s, pressure, carried, high_s, low_s,
+    out, pressure_out, plane_s, depth_s, pressure, carried, table_s, hot_a, hot_b,
 ):
     c0, c1, c2 = [jnp.broadcast_to(c, (XE, DEPTH)) for c in coefficients(sums)]
 
@@ -439,37 +437,49 @@
         velocity = own[1 + axis]
         value = (velocity + carried[axis]) - FLIP * velocity
         for lift, level in ((0, value), (1, next_z(value))):
-            high, low = split(level)
-            rows = slice(axis * 64 + lift * CELLS, axis * 64 + (lift + 1) * CELLS)
-            high_s[rows, :] = high
-            low_s[rows, :] = low
+            first = axis * 64 + lift * CELLS
+            table_s[first : first + CELLS, :] = level
+            table_s[192 + first : 192 + first + CELLS, :] = remainder(level)
     cells_of(msg, plane_s, depth_s)
-
-    def body(chunk, carry):
-        hots = [depth_hot(depth_s[pl.ds(chunk * CHUNK + j, 1), :]) for j in range(CHUNK)]
-        hot = jnp.concatenate(hots, axis=1)
-        table = jnp.dot(high_s[...], hot, preferred_element_type=F32)
-        table = table + jnp.dot(low_s[...], hot, preferred_element_type=F32)
+    level = lax.broadcasted_iota(jnp.int32, (DEPTH, CAP), 0)
+
+    def build(chunk, hot):
+        for j in range(CHUNK):
+            depth_row = depth_s[pl.ds(chunk * CHUNK + j, 1), :]
+            hot[:, j * CAP : (j + 1) * CAP] = jnp.where(level == depth_row, 1.0, 0.0)
+
+    def pick(chunk, hot):
+        both = one_pass(table_s[...], hot[...])
+        table = both[:192] + both[192:]
         for j in range(CHUNK):
             source = chunk * CHUNK + j
             weights = tile_weights(msg, source, plane_s[pl.ds(source, 1), :])
             for axis in range(3):
                 picked = table[axis * 64 : (axis + 1) * 64, j * CAP : (j + 1) * CAP] * weights
                 out[pl.ds(3 * source + axis, 1), :] = jnp.sum(picked, axis=0, keepdims=True)
+
+    turns = GROUPS // CHUNK
+    build(0, hot_a)
+
+    def body(turn, carry):
+        build(2 * turn + 1, hot_b)
+        pick(2 * turn, hot_a)
+        build((2 * turn + 2) & (turns - 1), hot_a)
+        pick(2 * turn + 1, hot_b)
         return carry
 
-    lax.fori_loop(0, GROUPS // CHUNK, body, 0)
+    lax.fori_loop(0, turns // 2, body, 0)
 
 
 def gather(sums, bases, betas, own, msg):
     index = pltpu.VMEM((GROUPS, CAP), jnp.int32)
-    operand = pltpu.VMEM((192, DEPTH), BF16)
+    hot = pltpu.VMEM((DEPTH, CHUNK * CAP), F32)
     return pl.pallas_call(
         gather_kernel,
         out_shape=[shape(3 * GROUPS, CAP), shape(*BLOCK)],
         in_specs=[VM] * 9,
         out_specs=[VM] * 2,
-        scratch_shapes=[index, index, pltpu.VMEM(BASIS, F32), pltpu.VMEM((3,) + BLOCK, F32), operand, operand],
+        scratch_shapes=[index, index, pltpu.VMEM(BASIS, F32), pltpu.VMEM((3,) + BLOCK, F32), pltpu.VMEM((384, DEPTH), F32), hot, hot],
         compiler_params=PARAMS,
         name="gather",
     )(sums, *bases, *betas, own, msg)

time: 189 us -> 156 us (0.83)
  Pallas kernels: 65.8 us -> 40.7 us
  local copies, waits for them, and re-layouts: 18.6 us -> 7.81 us
  waiting for transfers between devices: 42.1 us -> 44.5 us
    pallas_call x1, Pallas kernels: 25.8 us -> 11.9 us  [spread(): pl.pallas_call(spread_kernel, out_shape=shape(4, CELLS, DEPTH), in_specs=...]
    unnamed x47 -> x15, local copies, waits for them, and re-layouts: 11.5 us -> 4.58 us
    pallas_call x1, Pallas kernels: 15.7 us -> 11.4 us  [gather(): pl.pallas_call(gather_kernel, out_shape=[shape(3 * GROUPS, CAP), shape(*B...]
    another operation x9, local copies, waits for them, and re-layouts: 2.61 us -> 0.09 us  [exchange(): lower = jnp.stack([b[..., :half, :] for b in (low_x, block, high_x)])]
    pallas_call x1, Pallas kernels: 6.91 us -> 4.5 us  [last_solve(): pl.pallas_call(last_kernel, out_shape=[shape(*BASIS), shape(GROUPS, CAP)]...]
    pallas_call x1, Pallas kernels: 6.7 us -> 4.33 us  [middle_solve(): pl.pallas_call(middle_kernel, out_shape=[shape(*BASIS), shape(*BLOCK), sh...]
    pallas_call x1, Pallas kernels: 10.7 us -> 8.57 us  [start_solve(): pl.pallas_call(start_kernel, out_shape=[shape(*EXT)] * 4 + [shape(*BASIS)...]
    ppermute x3, waiting for transfers between devices: 5.2 us -> 7.12 us  [exchange(): high_x = lax.ppermute(block, 'gx', [(b, a) for a, b in up_x])]
  transfers between devices with their start and end apart: 14 -> 14, of which waited for: 9 -> 9; matrix products, arithmetic and copies ran while one was open for 3% -> 1% of each run, Pallas kernels for 0% -> 0%
where the time goes in v2:
time: 156 us
  waiting for transfers between devices  44.5 us (29%)
  starting transfers between devices  41.2 us (26%)
  Pallas kernels  40.7 us (26%)
  blocking collectives  20.2 us (13%)
  local copies, waits for them, and re-layouts  7.81 us (5%)
    all_to_all x1, blocking collectives, local(): sums = lax.all_to_all(sums, ALL, 0, 0, tiled=True)  20.2 us
    all_to_all x1, waiting for transfers between devices, local(): lax.all_to_all(message.reshape(GROUPS, FIELDS * CAP), ALL, 0, 0, tiled=True)  16.1 us
    ppermute x3, starting transfers between devices, exchange(): high_y = lax.ppermute(lower, 'yz', [(b, a) for a, b in up_y])  14.6 us
    pallas_call x1, Pallas kernels, spread(): pl.pallas_call(spread_kernel, out_shape=shape(4, CELLS, DEPTH), in_specs=...  11.9 us
    all_to_all x1, starting transfers between devices, local(): lax.all_to_all(message.reshape(GROUPS, FIELDS * CAP), ALL, 0, 0, tiled=True)  11.5 us
    pallas_call x1, Pallas kernels, gather(): pl.pallas_call(gather_kernel, out_shape=[shape(3 * GROUPS, CAP), shape(*B...  11.4 us
    ppermute x3, waiting for transfers between devices, exchange(): low_y = lax.ppermute(upper, 'yz', up_y)  10.9 us
    all_to_all x1, waiting for transfers between devices, local(): lax.all_to_all(sampled.reshape(GROUPS, 3 * CAP), ALL, 0, 0, tiled=True)  9.93 us
  transfers between devices with their start and end apart: 14, of which 9 were waited for; matrix products, arithmetic and copies ran while one was open for 1% of the time, Pallas kernels for 0%

profile of v2, /device:TPU:1, one launch (start us, length us, event | category | flops | bytes accessed | tf_op | source)
XLA Modules:
  0.0 155.6 jit_solution(14252682146752670563)
XLA Ops:
  0.6 0.0 copy-start.1
  0.6 0.0 copy-start
  0.6 1.0 copy.28
  1.7 0.9 copy.29
  2.6 0.0 copy-done.1
  2.6 0.1 copy.25
  2.7 0.0 copy-done
  2.8 0.2 copy.27
  3.0 0.0 copy-start.4
  3.0 0.7 copy-done.4
  3.7 0.1 pad_maximum_fusion
  3.7 2.0 %copy.30 = f32[128,1,1664]{2,1,0:T(1,128)} copy(f32[128,1,1664]{0,2,1:T(8,128)S(1)} %bitcast.65) | data formatting | bytes 1703936 | tf_op jit(solution)/shard_map/all_to_all | solution.py:516
  5.8 0.0 copy-start.3
  5.8 11.5 %all-to-all-start = ((f32[128,1,1664]{2,1,0:T(1,128)}), f32[128,1,1664]{2,1,0:T(1,128)S(1)}, u32[]{:S(2)}, u32[]{:S(2)}) async-start(f32[128,1,1664]{2,1,0:T(1,128)} %copy.30), calls=%async_computation | async-start | bytes 1703936 | tf_op jit(solution)/shard_map/all_to_all | solution.py:516
  17.3 0.0 copy-done.3
  17.3 0.0 copy-start.2
  17.4 0.8 copy-done.2
  18.2 0.1 copy.32
  18.3 0.1 reshape.92.water
  18.4 16.1 %all-to-all-done = f32[128,1,1664]{2,1,0:T(1,128)S(1)} async-done(((f32[128,1,1664]{2,1,0:T(1,128)}), f32[128,1,1664]{2,1,0:T(1,128)S(1)}, u32[]{:S(2)}, u32[]{:S(2)}) %all-to-all-start) | async-done | bytes 852000 | tf_op jit(solution)/shard_map/all_to_all | solution.py:516
  34.5 11.9 %spread.1.own = f32[4,32,512]{2,1,0:T(8,128)S(1)} custom-call(f32[1664,128]{1,0:T(8,128)S(1)} %bitcast.61, f32[32,512]{1,0:T(8,128)S(1)} %reshape.91.density, f32[3,32,512]{2,1,0:T(8,128)S(1)} %reshape.92.water), custom_call_target="tpu_custom_call" | custom-call | tf_op jit(solution)/shard_map/spread/pallas_call | solution.py:123
  46.4 0.8 collective-permute-start.1
  47.3 0.9 collective-permute-start
  48.2 4.3 %collective-permute-done.1.high_x = f32[4,32,512]{2,1,0:T(8,128)S(1)} collective-permute-done((f32[4,32,512]{2,1,0:T(8,128)S(1)}, f32[4,32,512]{2,1,0:T(8,128)S(1)}, u32[]{:S(2)}, u32[]{:S(2)}) %collective-permute-start.1) | collective-permute-done | bytes 262176 | tf_op jit(solution)/shard_map/ppermute | solution.py:492
  52.6 0.0 collective-permute-done.low_x
  52.6 0.4 collective-permute-start.2
  53.1 4.5 %collective-permute-start.3 = (f32[3,4,16,512]{3,2,1,0:T(8,128)S(1)}, f32[3,4,16,512]{3,2,1,0:T(8,128)S(1)}, u32[]{:S(2)}, u32[]{:S(2)}) collective-permute-start(f32[3,4,16,512]{3,2,1,0:T(8,128)S(1)} %pad_maximum_fusion.2), channel_id=1, source_target_pairs={{1,0},{2,1},{3,2},{4,3},{5,4},{6,5},{7,6},{8,7},{9,8},{10,9},{11,1... | collective-permute-start | bytes 1179656 | tf_op jit(solution)/shard_map/ppermute | solution.py:497
  57.6 0.1 add_convert_fusion.edge
  57.7 7.1 %collective-permute-done.2.low_y = f32[3,4,16,512]{3,2,1,0:T(8,128)S(1)} collective-permute-done((f32[3,4,16,512]{3,2,1,0:T(8,128)S(1)}, f32[3,4,16,512]{3,2,1,0:T(8,128)S(1)}, u32[]{:S(2)}, u32[]{:S(2)}) %collective-permute-start.2) | collective-permute-done | bytes 393248 | tf_op jit(solution)/shard_map/ppermute | solution.py:496
  64.8 0.0 collective-permute-done.3.high_y
  64.8 8.6 %start_solve.1 = (f32[16,16,512]{2,1,0:T(8,128)S(1)}, f32[16,16,512]{2,1,0:T(8,128)S(1)}, f32[16,16,512]{2,1,0:T(8,128)S(1)}, f32[16,16,512]{2,1,0:T(8,128)S(1)}...) custom-call(s32[4]{0:T(128)S(1)} %add_convert_fusion.edge, ...), custom_call_target="tpu_custom_call" | custom-call | tf_op jit(solution)/shard_map/start_solve/pallas_call | solution.py:299
  73.4 2.8 %collective-permute-start.5 = (f32[32,512]{1,0:T(8,128)S(1)}, f32[32,512]{1,0:T(8,128)S(1)}, u32[]{:S(2)}, u32[]{:S(2)}) collective-permute-start(f32[32,512]{1,0:T(8,128)S(1)} %get-tuple-element.17.own.image_0), channel_id=1, source_target_pairs={{16,0},{32,16},{48,32},{64,48},{80,64},{96,80},{112,96},{0,112},{1... | collective-permute-start | bytes 196616 | tf_op jit(solution)/shard_map/ppermute | solution.py:492
  76.2 0.5 collective-permute-start.4
  76.6 1.9 %collective-permute-done.5.high_x = f32[32,512]{1,0:T(8,128)S(1)} collective-permute-done((f32[32,512]{1,0:T(8,128)S(1)}, f32[32,512]{1,0:T(8,128)S(1)}, u32[]{:S(2)}, u32[]{:S(2)}) %collective-permute-start.5) | collective-permute-done | bytes 65568 | tf_op jit(solution)/shard_map/ppermute | solution.py:492
  78.5 0.0 collective-permute-done.4.low_x
  78.6 0.1 collective-permute-start.6
  78.7 5.0 %collective-permute-start.7 = (f32[3,16,512]{2,1,0:T(8,128)S(1)}, f32[3,16,512]{2,1,0:T(8,128)S(1)}, u32[]{:S(2)}, u32[]{:S(2)}) collective-permute-start(f32[3,16,512]{2,1,0:T(8,128)S(1)} %pad_maximum_fusion.4), channel_id=1, source_target_pairs={{1,0},{2,1},{3,2},{4,3},{5,4},{6,5},{7,6},{8,7},{9,8},{10,9},{11,1... | collective-permute-start | bytes 294920 | tf_op jit(solution)/shard_map/ppermute | solution.py:497
  83.6 1.9 %collective-permute-done.6.low_y = f32[3,16,512]{2,1,0:T(8,128)S(1)} collective-permute-done((f32[3,16,512]{2,1,0:T(8,128)S(1)}, f32[3,16,512]{2,1,0:T(8,128)S(1)}, u32[]{:S(2)}, u32[]{:S(2)}) %collective-permute-start.6) | collective-permute-done | bytes 98336 | tf_op jit(solution)/shard_map/ppermute | solution.py:496
  85.5 0.0 collective-permute-done.7.high_y
  85.5 4.3 %middle_solve.1 = (f32[10,16,512]{2,1,0:T(8,128)S(1)}, f32[32,512]{1,0:T(8,128)S(1)}, f32[32,512]{1,0:T(8,128)S(1)}) custom-call(f32[32,512]{1,0:T(8,128)S(1)} %get-tuple-element.17.own.image_0, f32[32,512]{1,0:T(8,128)S(1)} %collective-permute-done.4.low_x, f32[32,512]{1,0:T(8,128)S(1)} %collective-permute-done.5.high_x, ...), custom_call_target="tpu_custom_call" | custom-call | tf_op jit(solution)/shard_map/middle_solve/pallas_call | solution.py:367
  89.9 5.0 %collective-permute-start.9 = (f32[32,512]{1,0:T(8,128)S(1)}, f32[32,512]{1,0:T(8,128)S(1)}, u32[]{:S(2)}, u32[]{:S(2)}) collective-permute-start(f32[32,512]{1,0:T(8,128)S(1)} %get-tuple-element.23.own), channel_id=1, source_target_pairs={{16,0},{32,16},{48,32},{64,48},{80,64},{96,80},{112,96},{0,112},{1... | collective-permute-start | bytes 196616 | tf_op jit(solution)/shard_map/ppermute | solution.py:492
  94.9 0.0 collective-permute-start.8
  94.9 0.9 collective-permute-done.9.high_x
  95.8 0.4 collective-permute-done.8.low_x
  96.2 0.1 collective-permute-start.10
  96.3 5.2 %collective-permute-start.11 = (f32[3,16,512]{2,1,0:T(8,128)S(1)}, f32[3,16,512]{2,1,0:T(8,128)S(1)}, u32[]{:S(2)}, u32[]{:S(2)}) collective-permute-start(f32[3,16,512]{2,1,0:T(8,128)S(1)} %pad_maximum_fusion.6), channel_id=1, source_target_pairs={{1,0},{2,1},{3,2},{4,3},{5,4},{6,5},{7,6},{8,7},{9,8},{10,9},{11,1... | collective-permute-start | bytes 294920 | tf_op jit(solution)/shard_map/ppermute | solution.py:497
  101.5 1.9 %collective-permute-done.10.low_y = f32[3,16,512]{2,1,0:T(8,128)S(1)} collective-permute-done((f32[3,16,512]{2,1,0:T(8,128)S(1)}, f32[3,16,512]{2,1,0:T(8,128)S(1)}, u32[]{:S(2)}, u32[]{:S(2)}) %collective-permute-start.10) | collective-permute-done | bytes 98336 | tf_op jit(solution)/shard_map/ppermute | solution.py:496
  103.5 0.0 collective-permute-done.11.high_y
  103.5 4.5 %last_solve.1 = (f32[10,16,512]{2,1,0:T(8,128)S(1)}, f32[128,128]{1,0:T(8,128)S(1)}) custom-call(f32[32,512]{1,0:T(8,128)S(1)} %get-tuple-element.23.own, f32[32,512]{1,0:T(8,128)S(1)} %collective-permute-done.8.low_x, f32[32,512]{1,0:T(8,128)S(1)} %collective-permute-done.9.high_x, f32[3,16,512]{2,1,0:T(8,128)S(1)} %collective-permute-done.10.low_y, ...), custom_call_target="tpu_custom_call" | custom-call | tf_op jit(solution)/shard_map/last_solve/pallas_call | solution.py:379
  108.0 20.2 %all_to_all.29 = f32[128,1,128]{2,1,0:T(1,128)S(1)} all-to-all(f32[128,1,128]{2,1,0:T(1,128)S(1)} %bitcast.64), channel_id=1, replica_groups=mesh['gx'=8,'yz'=16] {'gx','yz'}, dimensions={0} | all-to-all | bytes 131072 | tf_op jit(solution)/shard_map/all_to_all | solution.py:526
  128.2 11.4 %gather.1 = (f32[384,128]{1,0:T(8,128)}, f32[32,512]{1,0:T(8,128)S(1)}) custom-call(f32[128,128]{1,0:T(8,128)S(1)} %bitcast.63, f32[10,16,512]{2,1,0:T(8,128)S(1)} %get-tuple-element.22.before.basis_0, f32[10,16,512]{2,1,0:T(8,128)S(1)} %get-tuple-element.24.before.basis_1, f32[10,16,512]{2,1,0:T(8,128)S(1)} %get-tuple-element.29.basis_2, ...), custom_call_target="tpu_custom_call" | custom-call | tf_op jit(solution)/shard_map/gather/pallas_call | solution.py:477
  139.5 4.5 %all-to-all-start.2 = ((f32[128,1,384]{2,1,0:T(1,128)}), f32[128,1,384]{2,1,0:T(1,128)S(1)}, u32[]{:S(2)}, u32[]{:S(2)}) async-start(f32[128,1,384]{2,1,0:T(1,128)} %bitcast.34), calls=%async_computation.2 | async-start | bytes 393216 | tf_op jit(solution)/shard_map/all_to_all | solution.py:528
  144.1 0.7 copy.39
  144.7 9.9 %all-to-all-done.2 = f32[128,1,384]{2,1,0:T(1,128)S(1)} async-done(((f32[128,1,384]{2,1,0:T(1,128)}), f32[128,1,384]{2,1,0:T(1,128)S(1)}, u32[]{:S(2)}, u32[]{:S(2)}) %all-to-all-start.2) | async-done | bytes 196640 | tf_op jit(solution)/shard_map/all_to_all | solution.py:528
  154.6 0.2 copy.35
  154.8 0.8 copy.37
  (22 shorter events, 0.3 us)
Async XLA Ops:
  0.6 2.0 %copy-start.1 = (f32[1,128,3,128]{3,1,2,0:T(8,128)S(1)}, f32[1,128,3,128]{3,1,2,0:T(8,128)}, u32[]{:S(2)}) copy-start(f32[1,128,3,128]{3,1,2,0:T(8,128)} %param.8) | copy-start | bytes 589828
  0.6 2.1 %copy-start = (f32[1,128,8,128]{3,2,1,0:T(8,128)S(1)}, f32[1,128,8,128]{3,2,1,0:T(8,128)}, u32[]{:S(2)}) copy-start(f32[1,128,8,128]{3,2,1,0:T(8,128)} %param.9) | copy-start | bytes 1572868
  3.0 0.7 copy-start.4
  5.8 11.5 %copy-start.3 = (s32[4,8,512]{2,1,0:T(8,128)S(1)}, s32[4,8,512]{2,1,0:T(8,128)}, u32[]{:S(2)}) copy-start(s32[4,8,512]{2,1,0:T(8,128)} %param.13) | copy-start | bytes 196612
  5.8 28.7 %all-to-all-start = ((f32[128,1,1664]{2,1,0:T(1,128)}), f32[128,1,1664]{2,1,0:T(1,128)S(1)}, u32[]{:S(2)}, u32[]{:S(2)}) async-start(f32[128,1,1664]{2,1,0:T(1,128)} %copy.30), calls=%async_computation | async-start | bytes 1703936 | tf_op jit(solution)/shard_map/all_to_all | solution.py:516
  17.3 0.9 copy-start.2
  46.4 6.1 %collective-permute-start.1 = (f32[4,32,512]{2,1,0:T(8,128)S(1)}, f32[4,32,512]{2,1,0:T(8,128)S(1)}, u32[]{:S(2)}, u32[]{:S(2)}) collective-permute-start(f32[4,32,512]{2,1,0:T(8,128)S(1)} %spread.1.own), channel_id=1, source_target_pairs={{16,0},{32,16},{48,32},{64,48},{80,64},{96,80},{112,96},{0,112},{1... | collective-permute-start | bytes 786440 | tf_op jit(solution)/shard_map/ppermute | solution.py:492
  47.3 5.3 %collective-permute-start = (f32[4,32,512]{2,1,0:T(8,128)S(1)}, f32[4,32,512]{2,1,0:T(8,128)S(1)}, u32[]{:S(2)}, u32[]{:S(2)}) collective-permute-start(f32[4,32,512]{2,1,0:T(8,128)S(1)} %spread.1.own), channel_id=1, source_target_pairs={{0,16},{16,32},{32,48},{48,64},{64,80},{80,96},{96,112},{112,0},{1... | collective-permute-start | bytes 786440 | tf_op jit(solution)/shard_map/ppermute | solution.py:491
  52.6 12.2 %collective-permute-start.2 = (f32[3,4,16,512]{3,2,1,0:T(8,128)S(1)}, f32[3,4,16,512]{3,2,1,0:T(8,128)S(1)}, u32[]{:S(2)}, u32[]{:S(2)}) collective-permute-start(f32[3,4,16,512]{3,2,1,0:T(8,128)S(1)} %pad_maximum_fusion.1), channel_id=1, source_target_pairs={{0,1},{1,2},{2,3},{3,4},{4,5},{5,6},{6,7},{7,8},{8,9},{9,10},{10,1... | collective-permute-start | bytes 1179656 | tf_op jit(solution)/shard_map/ppermute | solution.py:496
  53.1 11.7 %collective-permute-start.3 = (f32[3,4,16,512]{3,2,1,0:T(8,128)S(1)}, f32[3,4,16,512]{3,2,1,0:T(8,128)S(1)}, u32[]{:S(2)}, u32[]{:S(2)}) collective-permute-start(f32[3,4,16,512]{3,2,1,0:T(8,128)S(1)} %pad_maximum_fusion.2), channel_id=1, source_target_pairs={{1,0},{2,1},{3,2},{4,3},{5,4},{6,5},{7,6},{8,7},{9,8},{10,9},{11,1... | collective-permute-start | bytes 1179656 | tf_op jit(solution)/shard_map/ppermute | solution.py:497
  73.4 5.2 %collective-permute-start.5 = (f32[32,512]{1,0:T(8,128)S(1)}, f32[32,512]{1,0:T(8,128)S(1)}, u32[]{:S(2)}, u32[]{:S(2)}) collective-permute-start(f32[32,512]{1,0:T(8,128)S(1)} %get-tuple-element.17.own.image_0), channel_id=1, source_target_pairs={{16,0},{32,16},{48,32},{64,48},{80,64},{96,80},{112,96},{0,112},{1... | collective-permute-start | bytes 196616 | tf_op jit(solution)/shard_map/ppermute | solution.py:492
  76.2 2.4 %collective-permute-start.4 = (f32[32,512]{1,0:T(8,128)S(1)}, f32[32,512]{1,0:T(8,128)S(1)}, u32[]{:S(2)}, u32[]{:S(2)}) collective-permute-start(f32[32,512]{1,0:T(8,128)S(1)} %get-tuple-element.17.own.image_0), channel_id=1, source_target_pairs={{0,16},{16,32},{32,48},{48,64},{64,80},{80,96},{96,112},{112,0},{1... | collective-permute-start | bytes 196616 | tf_op jit(solution)/shard_map/ppermute | solution.py:491
  78.6 7.0 %collective-permute-start.6 = (f32[3,16,512]{2,1,0:T(8,128)S(1)}, f32[3,16,512]{2,1,0:T(8,128)S(1)}, u32[]{:S(2)}, u32[]{:S(2)}) collective-permute-start(f32[3,16,512]{2,1,0:T(8,128)S(1)} %pad_maximum_fusion.3), channel_id=1, source_target_pairs={{0,1},{1,2},{2,3},{3,4},{4,5},{5,6},{6,7},{7,8},{8,9},{9,10},{10,1... | collective-permute-start | bytes 294920 | tf_op jit(solution)/shard_map/ppermute | solution.py:496
  78.7 6.9 %collective-permute-start.7 = (f32[3,16,512]{2,1,0:T(8,128)S(1)}, f32[3,16,512]{2,1,0:T(8,128)S(1)}, u32[]{:S(2)}, u32[]{:S(2)}) collective-permute-start(f32[3,16,512]{2,1,0:T(8,128)S(1)} %pad_maximum_fusion.4), channel_id=1, source_target_pairs={{1,0},{2,1},{3,2},{4,3},{5,4},{6,5},{7,6},{8,7},{9,8},{10,9},{11,1... | collective-permute-start | bytes 294920 | tf_op jit(solution)/shard_map/ppermute | solution.py:497
  89.9 5.9 %collective-permute-start.9 = (f32[32,512]{1,0:T(8,128)S(1)}, f32[32,512]{1,0:T(8,128)S(1)}, u32[]{:S(2)}, u32[]{:S(2)}) collective-permute-start(f32[32,512]{1,0:T(8,128)S(1)} %get-tuple-element.23.own), channel_id=1, source_target_pairs={{16,0},{32,16},{48,32},{64,48},{80,64},{96,80},{112,96},{0,112},{1... | collective-permute-start | bytes 196616 | tf_op jit(solution)/shard_map/ppermute | solution.py:492
  94.9 1.3 collective-permute-start.8
  96.2 7.2 %collective-permute-start.10 = (f32[3,16,512]{2,1,0:T(8,128)S(1)}, f32[3,16,512]{2,1,0:T(8,128)S(1)}, u32[]{:S(2)}, u32[]{:S(2)}) collective-permute-start(f32[3,16,512]{2,1,0:T(8,128)S(1)} %pad_maximum_fusion.5), channel_id=1, source_target_pairs={{0,1},{1,2},{2,3},{3,4},{4,5},{5,6},{6,7},{7,8},{8,9},{9,10},{10,1... | collective-permute-start | bytes 294920 | tf_op jit(solution)/shard_map/ppermute | solution.py:496
  96.3 7.1 %collective-permute-start.11 = (f32[3,16,512]{2,1,0:T(8,128)S(1)}, f32[3,16,512]{2,1,0:T(8,128)S(1)}, u32[]{:S(2)}, u32[]{:S(2)}) collective-permute-start(f32[3,16,512]{2,1,0:T(8,128)S(1)} %pad_maximum_fusion.6), channel_id=1, source_target_pairs={{1,0},{2,1},{3,2},{4,3},{5,4},{6,5},{7,6},{8,7},{9,8},{10,9},{11,1... | collective-permute-start | bytes 294920 | tf_op jit(solution)/shard_map/ppermute | solution.py:497
  139.5 15.1 %all-to-all-start.2 = ((f32[128,1,384]{2,1,0:T(1,128)}), f32[128,1,384]{2,1,0:T(1,128)S(1)}, u32[]{:S(2)}, u32[]{:S(2)}) async-start(f32[128,1,384]{2,1,0:T(1,128)} %bitcast.34), calls=%async_computation.2 | async-start | bytes 393216 | tf_op jit(solution)/shard_map/all_to_all | solution.py:528

commit v3 on v2

--- a/solution.py
+++ b/solution.py
@@ -22,9 +22,11 @@
 DEPTH = 512
 CHUNK = 8
 HALO = 4
+CORNER = 3
 YE = 8 + 2 * HALO
 XE = 16
 PARAMS = pltpu.CompilerParams(vmem_limit_bytes=20 * 1024 * 1024)
+SMALL = pltpu.CompilerParams(vmem_limit_bytes=8 * 1024 * 1024)
 VM = pl.BlockSpec(memory_space=pltpu.VMEM)
 SM = pl.BlockSpec(memory_space=pltpu.SMEM)
 F32 = jnp.float32
@@ -68,6 +70,55 @@
         value = jnp.where(next_y, weight(2 + lift), value)
         lifts.append(jnp.where(here, weight(lift), value))
     return jnp.concatenate(lifts, axis=0)
+
+
+def pack_kernel(mass_h, velocity_h, weight_h, base_h, count_h, out, mass, velocity, weight, base, count, sems):
+    pairs = ((count_h, count), (mass_h, mass), (base_h, base), (velocity_h, velocity), (weight_h, weight))
+    copies = [pltpu.make_async_copy(a, b, sems.at[k]) for k, (a, b) in enumerate(pairs)]
+    for copy in copies:
+        copy.start()
+    copies[0].wait()
+    limit = jnp.broadcast_to(count[...], (GROUPS, CAP)).astype(F32).T
+    slot = lax.broadcasted_iota(jnp.int32, (GROUPS, CAP), 1).astype(F32)
+    live = jnp.where(slot < limit, 1.0, 0.0)
+    copies[1].wait()
+    out[pl.ds(ROW_M, GROUPS, stride=FIELDS), :] = mass[...] * live
+    copies[2].wait()
+    out[pl.ds(ROW_B, GROUPS, stride=FIELDS), :] = base[...].astype(F32)
+    copies[3].wait()
+    for axis in range(3):
+        out[pl.ds(axis, GROUPS, stride=FIELDS), :] = velocity[axis]
+    copies[4].wait()
+    for corner in range(8):
+        out[pl.ds(ROW_W + corner, GROUPS, stride=FIELDS), :] = weight[pl.ds(corner, GROUPS, stride=8), :]
+
+
+def pack(*operands):
+    return pl.pallas_call(
+        pack_kernel,
+        out_shape=shape(GROUPS * FIELDS, CAP),
+        in_specs=[pl.BlockSpec(memory_space=pl.ANY)] * 5,
+        out_specs=VM,
+        scratch_shapes=[pltpu.VMEM(a.shape, a.dtype) for a in operands] + [pltpu.SemaphoreType.DMA((5,))],
+        compiler_params=pltpu.CompilerParams(vmem_limit_bytes=67_000_000),
+        name="pack",
+    )(*operands)
+
+
+def unpack_kernel(velocity, returned, out):
+    for axis in range(3):
+        out[axis] = FLIP * velocity[axis] + returned[pl.ds(axis, GROUPS, stride=3), :]
+
+
+def unpack(velocity, returned):
+    return pl.pallas_call(
+        unpack_kernel,
+        out_shape=shape(3, GROUPS, CAP),
+        in_specs=[VM] * 2,
+        out_specs=VM,
+        compiler_params=SMALL,
+        name="unpack",
+    )(velocity, returned)
 
 
 def spread_kernel(msg, density, water, out, plane_s, depth_s, value_s, left_a, hot_a, left_b, hot_b, acc):
@@ -150,11 +201,14 @@
 
 
 def each_row(first, last, body):
-    def step(y, carry):
-        body(y)
+    def step(pair, carry):
+        body(first + 2 * pair)
+        body(first + 2 * pair + 1)
         return carry
 
-    lax.fori_loop(first, last, step, 0)
+    lax.fori_loop(0, (last - first) // 2, step, 0)
+    if (last - first) % 2:
+        body(last - 1)
 
 
 def operate_row(field, y, offset, beta_x, beta_y, beta_z):
@@ -171,15 +225,21 @@
     )
 
 
-def place(ext, own, low_x, high_x, low_y, high_y, fix):
-    for block, source in enumerate((low_x, own, high_x)):
-        columns = slice(4 * block, 4 * block + 4)
+def place(ext, corner, own, low_y, high_y, low_x, high_x, fix):
+    for y in range(8):
+        ext[HALO + y, 4:8, :] = own(slice(4 * y, 4 * y + 4))
+    for y in range(HALO):
+        rows = slice(4 * y, 4 * y + 4)
+        ext[y, 4:8, :] = fix(low_y(rows), 1, 0)
+        ext[HALO + 8 + y, 4:8, :] = fix(high_y(rows), 1, 2)
+    for side, columns, source in ((0, slice(0, 4), low_x), (2, slice(8, 12), high_x)):
         for y in range(8):
-            ext[HALO + y, columns, :] = fix(source(slice(4 * y, 4 * y + 4)), block, 1)
-        for y in range(HALO):
-            rows = slice(4 * y, 4 * y + 4)
-            ext[y, columns, :] = fix(low_y(block, rows), block, 0)
-            ext[HALO + 8 + y, columns, :] = fix(high_y(block, rows), block, 2)
+            ext[HALO + y, columns, :] = fix(source(slice(4 * y, 4 * y + 4)), side, 1)
+        for y in range(corner):
+            first = CELLS + 4 * y
+            ext[HALO - corner + y, columns, :] = fix(source(slice(first, first + 4)), side, 0)
+            first = first + 4 * corner
+            ext[HALO + 8 + y, columns, :] = fix(source(slice(first, first + 4)), side, 2)
 
 
 def precondition(residual, inverse, beta_x, beta_y, beta_z, update, first, second, finish):
@@ -226,31 +286,32 @@
 
 
 def start_kernel(
-    edge, own, low_x, high_x, low_y, high_y,
+    edge, own, low_y, high_y, low_x, high_x,
     beta_x, beta_y, beta_z, inverse, basis, basis_own, image, source_own,
     ext, residual, update, first, second,
 ):
     infinite = jnp.full((4, DEPTH), jnp.inf, F32)
     for f in range(4):
-        ext[f, :, 12:16, :] = jnp.full((YE, 4, DEPTH), jnp.inf if f == 0 else 0.0, F32)
-
-        def fix(value, block, row, f=f):
-            if f or (block == 1 and row == 1):
+        empty = jnp.inf if f == 0 else 0.0
+        ext[f, :, 12:16, :] = jnp.full((YE, 4, DEPTH), empty, F32)
+        for y in range(HALO - CORNER):
+            for row in (y, YE - 1 - y):
+                ext[f, row] = jnp.full((XE, DEPTH), empty, F32)
+
+        def fix(value, column, row, f=f):
+            if f:
                 return value
             outside = 0
-            if block != 1:
-                outside = outside + edge[0 if block == 0 else 1]
+            if column != 1:
+                outside = outside + edge[0 if column == 0 else 1]
             if row != 1:
                 outside = outside + edge[2 if row == 0 else 3]
             return jnp.where(outside > 0, infinite, value)
 
         place(
             ext.at[f],
-            lambda rows, f=f: own[f, rows, :],
-            lambda rows, f=f: low_x[f, rows, :],
-            lambda rows, f=f: high_x[f, rows, :],
-            lambda block, rows, f=f: low_y[block, f, rows, :],
-            lambda block, rows, f=f: high_y[block, f, rows, :],
+            CORNER,
+            *[(lambda rows, ref=ref, f=f: ref[f, rows, :]) for ref in (own, low_y, high_y, low_x, high_x)],
             fix,
         )
     end = lax.broadcasted_iota(jnp.int32, (XE, DEPTH), 1) == DEPTH - 1
@@ -295,7 +356,7 @@
 BLOCK = (CELLS, DEPTH)
 
 
-def start_solve(edge, own, low_x, high_x, low_y, high_y):
+def start_solve(edge, own, low_y, high_y, low_x, high_x):
     return pl.pallas_call(
         start_kernel,
         out_shape=[shape(*EXT)] * 4 + [shape(*BASIS)] + [shape(*BLOCK)] * 3,
@@ -304,20 +365,17 @@
         scratch_shapes=[pltpu.VMEM((4,) + EXT, F32)] + [pltpu.VMEM(EXT, F32)] * 4,
         compiler_params=PARAMS,
         name="start_solve",
-    )(edge, own, low_x, high_x, low_y, high_y)
-
-
-def next_basis(own, low_x, high_x, low_y, high_y, betas, inverse, before, basis, basis_own, image, scratch):
+    )(edge, own, low_y, high_y, low_x, high_x)
+
+
+def next_basis(own, low_y, high_y, low_x, high_x, betas, inverse, before, basis, basis_own, image, scratch):
     ext, update, first, second = scratch
     ext[:, 12:16, :] = jnp.zeros((YE, 4, DEPTH), F32)
     place(
         ext,
-        lambda rows: own[rows, :],
-        lambda rows: low_x[rows, :],
-        lambda rows: high_x[rows, :],
-        lambda block, rows: low_y[block, rows, :],
-        lambda block, rows: high_y[block, rows, :],
-        lambda value, block, row: value,
+        HALO,
+        *[(lambda rows, ref=ref: ref[rows, :]) for ref in (own, low_y, high_y, low_x, high_x)],
+        lambda value, column, row: value,
     )
 
     def finish(y, value):
@@ -332,21 +390,21 @@
 
 
 def middle_kernel(
-    own, low_x, high_x, low_y, high_y, beta_x, beta_y, beta_z, inverse, before,
+    own, low_y, high_y, low_x, high_x, beta_x, beta_y, beta_z, inverse, before,
     basis, basis_own, image, *scratch,
 ):
     next_basis(
-        own, low_x, high_x, low_y, high_y, (beta_x, beta_y, beta_z), inverse, before,
+        own, low_y, high_y, low_x, high_x, (beta_x, beta_y, beta_z), inverse, before,
         basis, basis_own, image, scratch,
     )
 
 
 def last_kernel(
-    own, low_x, high_x, low_y, high_y, beta_x, beta_y, beta_z, inverse, before,
+    own, low_y, high_y, low_x, high_x, beta_x, beta_y, beta_z, inverse, before,
     own_0, own_1, image_0, source_own, basis, sums, own_2, image_2, *scratch,
 ):
     next_basis(
-        own, low_x, high_x, low_y, high_y, (beta_x, beta_y, beta_z), inverse, before,
+        own, low_y, high_y, low_x, high_x, (beta_x, beta_y, beta_z), inverse, before,
         basis, own_2, image_2, scratch,
     )
     vectors = (own_0[...], own_1[...], own_2[...])
@@ -363,7 +421,7 @@
     sums[...] = jnp.broadcast_to(row, (GROUPS, CAP))
 
 
-def middle_solve(own, low_x, high_x, low_y, high_y, betas, inverse, before):
+def middle_solve(own, low_y, high_y, low_x, high_x, betas, inverse, before):
     return pl.pallas_call(
         middle_kernel,
         out_shape=[shape(*BASIS), shape(*BLOCK), shape(*BLOCK)],
@@ -372,10 +430,10 @@
         scratch_shapes=[pltpu.VMEM(EXT, F32)] * 4,
         compiler_params=PARAMS,
         name="middle_solve",
-    )(own, low_x, high_x, low_y, high_y, *betas, inverse, before)
-
-
-def last_solve(own, low_x, high_x, low_y, high_y, betas, inverse, before, *inner):
+    )(own, low_y, high_y, low_x, high_x, *betas, inverse, before)
+
+
+def last_solve(own, low_y, high_y, low_x, high_x, betas, inverse, before, *inner):
     return pl.pallas_call(
         last_kernel,
         out_shape=[shape(*BASIS), shape(GROUPS, CAP)],
@@ -384,7 +442,7 @@
         scratch_shapes=[pltpu.VMEM(BLOCK, F32)] * 2 + [pltpu.VMEM(EXT, F32)] * 4,
         compiler_params=PARAMS,
         name="last_solve",
-    )(own, low_x, high_x, low_y, high_y, *betas, inverse, before, *inner)
+    )(own, low_y, high_y, low_x, high_x, *betas, inverse, before, *inner)
 
 
 def coefficients(sums):
@@ -485,17 +543,19 @@
     )(sums, *bases, *betas, own, msg)
 
 
-def exchange(block, n_x, n_y):
+def exchange(block, n_x, n_y, corner):
     up_x = [(i, (i + 1) % n_x) for i in range(n_x)]
     up_y = [(i, (i + 1) % n_y) for i in range(n_y)]
-    low_x = lax.ppermute(block, "gx", up_x)
-    high_x = lax.ppermute(block, "gx", [(b, a) for a, b in up_x])
-    half = CELLS // 2
-    upper = jnp.stack([b[..., half:, :] for b in (low_x, block, high_x)])
-    lower = jnp.stack([b[..., :half, :] for b in (low_x, block, high_x)])
-    low_y = lax.ppermute(upper, "yz", up_y)
-    high_y = lax.ppermute(lower, "yz", [(b, a) for a, b in up_y])
-    return low_x, high_x, low_y, high_y
+    down_x, down_y = [[(b, a) for a, b in up] for up in (up_x, up_y)]
+    half = 4 * HALO
+    low_y = lax.ppermute(block[..., CELLS - half :, :], "yz", up_y)
+    high_y = lax.ppermute(block[..., :half, :], "yz", down_y)
+    near = 4 * corner
+    near_low, near_high = low_y, high_y
+    if corner < HALO:
+        near_low, near_high = low_y[..., half - near :, :], high_y[..., :near, :]
+    column = jnp.concatenate([block, near_low, near_high], axis=-2)
+    return low_y, high_y, lax.ppermute(column, "gx", up_x), lax.ppermute(column, "gx", down_x)
 
 
 def by_block(field):
@@ -507,28 +567,26 @@
     n_x, n_y = lax.axis_size("gx"), lax.axis_size("yz")
     at_x, at_y = lax.axis_index("gx"), lax.axis_index("yz")
     edge = jnp.stack([at_x == 0, at_x == n_x - 1, at_y == 0, at_y == n_y - 1]).astype(jnp.int32)
-    slot = jnp.arange(CAP, dtype=jnp.int32)
-    live = (slot[None, :] < slot_counts[0][:, None]).astype(F32)
-    masses = part_mass[0] * live
-    message = jnp.concatenate(
-        [part_vel[0], corner_weight[0], masses[:, None], corner_base[0].astype(F32)[:, None]], axis=1
-    )
-    msg = lax.all_to_all(message.reshape(GROUPS, FIELDS * CAP), ALL, 0, 0, tiled=True)
+    velocity = jnp.swapaxes(part_vel[0], 0, 1)
+    message = pack(
+        part_mass[0], velocity, corner_weight.reshape(8 * GROUPS, CAP), corner_base[0], slot_counts
+    )
+    msg = lax.all_to_all(message.reshape(GROUPS, 1, FIELDS * CAP), ALL, 0, 0, tiled=True)
     msg = msg.reshape(GROUPS * FIELDS, CAP)
     density = by_block(jnp.where(solid_flag == 1, SOLID_WATER, 1.0).astype(F32))
     own = spread(msg, density, by_block(water_vel))
-    *rest, basis_0, own_0, image_0, source = start_solve(edge, own, *exchange(own, n_x, n_y))
+    *rest, basis_0, own_0, image_0, source = start_solve(edge, own, *exchange(own, n_x, n_y, CORNER))
     betas, inverse = rest[:3], rest[3]
-    basis_1, own_1, image_1 = middle_solve(image_0, *exchange(image_0, n_x, n_y), betas, inverse, basis_0)
+    basis_1, own_1, image_1 = middle_solve(image_0, *exchange(image_0, n_x, n_y, HALO), betas, inverse, basis_0)
     basis_2, sums = last_solve(
-        image_1, *exchange(image_1, n_x, n_y), betas, inverse, basis_1, own_0, own_1, image_0, source
+        image_1, *exchange(image_1, n_x, n_y, HALO), betas, inverse, basis_1, own_0, own_1, image_0, source
     )
     sums = lax.all_to_all(sums, ALL, 0, 0, tiled=True)
     sampled, pressure = gather(sums, (basis_0, basis_1, basis_2), betas, own, msg)
-    returned = lax.all_to_all(sampled.reshape(GROUPS, 3 * CAP), ALL, 0, 0, tiled=True)
-    returned = returned.reshape(1, GROUPS, 3, CAP)
+    returned = lax.all_to_all(sampled.reshape(GROUPS, 1, 3 * CAP), ALL, 0, 0, tiled=True)
+    final = unpack(velocity, returned.reshape(3 * GROUPS, CAP))
     pressure = jnp.swapaxes(pressure.reshape(8, 4, DEPTH), 0, 1)
-    return FLIP * part_vel + returned, pressure
+    return jnp.swapaxes(final, 0, 1)[None], pressure
 
 
 def solution(mesh):

time: 156 us -> 142 us (0.910)
  local copies, waits for them, and re-layouts: 7.81 us -> 1.85 us
  Pallas kernels: 40.7 us -> 37.1 us
  waiting for transfers between devices: 44.5 us -> 41.4 us
    unnamed x15 -> x10, local copies, waits for them, and re-layouts: 4.58 us -> 0.85 us
    pallas_call x1, Pallas kernels: 8.57 us -> 5.32 us  [start_solve(): pl.pallas_call(start_kernel, out_shape=[shape(*EXT)] * 4 + [shape(*BASIS)...]
    ppermute x12, waiting for transfers between devices: 18.5 us -> 15.4 us  [the longest x3 9.65 us: exchange(): lax.ppermute(column, 'gx', down_x)]
    pallas_call x0 -> x2, Pallas kernels: none -> 2.99 us  [the longest x1 2.29 us: pack(): pl.pallas_call(pack_kernel, out_shape=shape(GROUPS * FIELDS, CAP), in_spe...]
    all_to_all x2 -> x0, local copies, waits for them, and re-layouts: 2.2 us -> none  [the longest x1 2.05 us: local(): lax.all_to_all(message.reshape(GROUPS, FIELDS * CAP), ALL, 0, 0, tiled=True)]
    pallas_call x1, Pallas kernels: 4.5 us -> 2.83 us  [last_solve(): pl.pallas_call(last_kernel, out_shape=[shape(*BASIS), shape(GROUPS, CAP)]...]
    pallas_call x1, Pallas kernels: 4.33 us -> 2.66 us  [middle_solve(): pl.pallas_call(middle_kernel, out_shape=[shape(*BASIS), shape(*BLOCK), sh...]
  transfers between devices with their start and end apart: 14 -> 14, of which waited for: 9 -> 10; matrix products, arithmetic and copies ran while one was open for 1% -> 1% of each run, Pallas kernels for 0% -> 0%
where the time goes in v3:
time: 142 us
  waiting for transfers between devices  41.4 us (29%)
  starting transfers between devices  41.1 us (29%)
  Pallas kernels  37.1 us (26%)
  blocking collectives  19.3 us (14%)
  local copies, waits for them, and re-layouts  1.85 us (1%)
    all_to_all x1, blocking collectives, local(): sums = lax.all_to_all(sums, ALL, 0, 0, tiled=True)  19.3 us
    all_to_all x1, waiting for transfers between devices, local(): lax.all_to_all(message.reshape(GROUPS, 1, FIELDS * CAP), ALL, 0, 0, tiled...  16.1 us
    ppermute x3, starting transfers between devices, exchange(): high_y = lax.ppermute(block[..., :half, :], 'yz', down_y)  14.5 us
    pallas_call x1, Pallas kernels, spread(): pl.pallas_call(spread_kernel, out_shape=shape(4, CELLS, DEPTH), in_specs=...  11.9 us
    all_to_all x1, starting transfers between devices, local(): lax.all_to_all(message.reshape(GROUPS, 1, FIELDS * CAP), ALL, 0, 0, tiled...  11.5 us
    pallas_call x1, Pallas kernels, gather(): pl.pallas_call(gather_kernel, out_shape=[shape(3 * GROUPS, CAP), shape(*B...  11.3 us
    all_to_all x1, waiting for transfers between devices, local(): lax.all_to_all(sampled.reshape(GROUPS, 1, 3 * CAP), ALL, 0, 0, tiled=True)  9.92 us
    ppermute x3, waiting for transfers between devices, exchange(): lax.ppermute(column, 'gx', down_x)  9.65 us
  transfers between devices with their start and end apart: 14, of which 10 were waited for; matrix products, arithmetic and copies ran while one was open for 1% of the time, Pallas kernels for 0%

profile of v3, /device:TPU:1, one launch (start us, length us, event | category | flops | bytes accessed | tf_op | source)
XLA Modules:
  0.0 141.7 jit_solution(3518455015076188442)
XLA Ops:
  0.6 2.3 %pack.1 = f32[1664,128]{1,0:T(8,128)} custom-call(f32[128,128]{1,0:T(8,128)} %bitcast.40, f32[3,128,128]{2,1,0:T(8,128)} %bitcast.30, f32[1024,128]{1,0:T(8,128)} %bitcast.37, s32[128,128]{1,0:T(8,128)} %bitcast.41, s32[1,128]{1,0:T(1,128)} %count_h.1), custom_call_target="tpu_custom_call" | custom-call | tf_op jit(solution)/shard_map/pack/pallas_call | solution.py:97
  2.9 0.0 copy-start.2
  2.9 11.5 %all-to-all-start = ((f32[128,1,1664]{2,1,0:T(1,128)}), f32[128,1,1664]{2,1,0:T(1,128)S(1)}, u32[]{:S(2)}, u32[]{:S(2)}) async-start(f32[128,1,1664]{2,1,0:T(1,128)} %bitcast.36), calls=%async_computation | async-start | bytes 1703936 | tf_op jit(solution)/shard_map/all_to_all | solution.py:574
  14.4 0.0 copy-done.2
  14.4 0.0 copy-start.1
  14.6 0.8 copy-done.1
  15.4 0.1 copy.14
  15.5 0.1 reshape.34.water
  15.6 16.1 %all-to-all-done = f32[128,1,1664]{2,1,0:T(1,128)S(1)} async-done(((f32[128,1,1664]{2,1,0:T(1,128)}), f32[128,1,1664]{2,1,0:T(1,128)S(1)}, u32[]{:S(2)}, u32[]{:S(2)}) %all-to-all-start) | async-done | bytes 852000 | tf_op jit(solution)/shard_map/all_to_all | solution.py:574
  31.7 11.9 %spread.1.own = f32[4,32,512]{2,1,0:T(8,128)S(1)} custom-call(f32[1664,128]{1,0:T(8,128)S(1)} %bitcast.28, f32[32,512]{1,0:T(8,128)S(1)} %reshape.33.density, f32[3,32,512]{2,1,0:T(8,128)S(1)} %reshape.34.water), custom_call_target="tpu_custom_call" | custom-call | tf_op jit(solution)/shard_map/spread/pallas_call | solution.py:174
  43.6 0.4 collective-permute-start
  44.1 4.4 %collective-permute-start.1 = (f32[4,16,512]{2,1,0:T(8,128)S(1)}, f32[4,16,512]{2,1,0:T(8,128)S(1)}, u32[]{:S(2)}, u32[]{:S(2)}) collective-permute-start(f32[4,16,512]{2,1,0:T(8,128)S(1)} %get-tuple-element.32), channel_id=1, source_target_pairs={{1,0},{2,1},{3,2},{4,3},{5,4},{6,5},{7,6},{8,7},{9,8},{10,9},{11,1... | collective-permute-start | bytes 393224 | tf_op jit(solution)/shard_map/ppermute | solution.py:552
  48.5 2.8 %collective-permute-done.low_y = f32[4,16,512]{2,1,0:T(8,128)S(1)} collective-permute-done((f32[4,16,512]{2,1,0:T(8,128)S(1)}, f32[4,16,512]{2,1,0:T(8,128)S(1)}, u32[]{:S(2)}, u32[]{:S(2)}) %collective-permute-start) | collective-permute-done | bytes 131104 | tf_op jit(solution)/shard_map/ppermute | solution.py:551
  51.3 0.0 collective-permute-done.1.high_y
  51.3 1.7 %collective-permute-start.3 = (f32[4,56,512]{2,1,0:T(8,128)S(1)}, f32[4,56,512]{2,1,0:T(8,128)S(1)}, u32[]{:S(2)}, u32[]{:S(2)}) collective-permute-start(f32[4,56,512]{2,1,0:T(8,128)S(1)} %pad_maximum_fusion), channel_id=1, source_target_pairs={{16,0},{32,16},{48,32},{64,48},{80,64},{96,80},{112,96},{0,112},{1... | collective-permute-start | bytes 1376264 | tf_op jit(solution)/shard_map/ppermute | solution.py:558
  53.0 0.5 collective-permute-start.2
  53.5 0.1 add_convert_fusion.edge
  53.6 6.4 %collective-permute-done.3.high_x = f32[4,56,512]{2,1,0:T(8,128)S(1)} collective-permute-done((f32[4,56,512]{2,1,0:T(8,128)S(1)}, f32[4,56,512]{2,1,0:T(8,128)S(1)}, u32[]{:S(2)}, u32[]{:S(2)}) %collective-permute-start.3) | collective-permute-done | bytes 458784 | tf_op jit(solution)/shard_map/ppermute | solution.py:558
  59.9 0.0 collective-permute-done.2.low_x
  59.9 5.3 %start_solve.1 = (f32[16,16,512]{2,1,0:T(8,128)S(1)}, f32[16,16,512]{2,1,0:T(8,128)S(1)}, f32[16,16,512]{2,1,0:T(8,128)S(1)}, f32[16,16,512]{2,1,0:T(8,128)S(1)}...) custom-call(s32[4]{0:T(128)S(1)} %add_convert_fusion.edge, ...), custom_call_target="tpu_custom_call" | custom-call | tf_op jit(solution)/shard_map/start_solve/pallas_call | solution.py:360
  65.3 0.1 collective-permute-start.4
  65.4 5.0 %collective-permute-start.5 = (f32[16,512]{1,0:T(8,128)S(1)}, f32[16,512]{1,0:T(8,128)S(1)}, u32[]{:S(2)}, u32[]{:S(2)}) collective-permute-start(f32[16,512]{1,0:T(8,128)S(1)} %get-tuple-element.36), channel_id=1, source_target_pairs={{1,0},{2,1},{3,2},{4,3},{5,4},{6,5},{7,6},{8,7},{9,8},{10,9},{11,1... | collective-permute-start | bytes 98312 | tf_op jit(solution)/shard_map/ppermute | solution.py:552
  70.4 1.2 collective-permute-done.4.low_y
  71.6 0.0 collective-permute-done.5.high_y
  71.6 3.3 %collective-permute-start.7 = (f32[64,512]{1,0:T(8,128)S(1)}, f32[64,512]{1,0:T(8,128)S(1)}, u32[]{:S(2)}, u32[]{:S(2)}) collective-permute-start(f32[64,512]{1,0:T(8,128)S(1)} %constant_dynamic-update-slice_fusion), channel_id=1, source_target_pairs={{16,0},{32,16},{48,32},{64,48},{80,64},{96,80},{112,96},{0,112},{1... | collective-permute-start | bytes 393224 | tf_op jit(solution)/shard_map/ppermute | solution.py:558
  74.8 0.0 collective-permute-start.6
  74.8 1.9 %collective-permute-done.7.high_x = f32[64,512]{1,0:T(8,128)S(1)} collective-permute-done((f32[64,512]{1,0:T(8,128)S(1)}, f32[64,512]{1,0:T(8,128)S(1)}, u32[]{:S(2)}, u32[]{:S(2)}) %collective-permute-start.7) | collective-permute-done | bytes 131104 | tf_op jit(solution)/shard_map/ppermute | solution.py:558
  76.7 0.1 collective-permute-done.6.low_x
  76.8 2.7 %middle_solve.1 = (f32[10,16,512]{2,1,0:T(8,128)S(1)}, f32[32,512]{1,0:T(8,128)S(1)}, f32[32,512]{1,0:T(8,128)S(1)}) custom-call(f32[32,512]{1,0:T(8,128)S(1)} %get-tuple-element.17.own.image_0, f32[16,512]{1,0:T(8,128)S(1)} %collective-permute-done.4.low_y, f32[16,512]{1,0:T(8,128)S(1)} %collective-permute-done.5.high_y, ...), custom_call_target="tpu_custom_call" | custom-call | tf_op jit(solution)/shard_map/middle_solve/pallas_call | solution.py:425
  79.5 0.1 collective-permute-start.8
  79.6 5.1 %collective-permute-start.9 = (f32[16,512]{1,0:T(8,128)S(1)}, f32[16,512]{1,0:T(8,128)S(1)}, u32[]{:S(2)}, u32[]{:S(2)}) collective-permute-start(f32[16,512]{1,0:T(8,128)S(1)} %get-tuple-element.34), channel_id=1, source_target_pairs={{1,0},{2,1},{3,2},{4,3},{5,4},{6,5},{7,6},{8,7},{9,8},{10,9},{11,1... | collective-permute-start | bytes 98312 | tf_op jit(solution)/shard_map/ppermute | solution.py:552
  84.7 1.2 collective-permute-done.8.low_y
  85.9 0.0 collective-permute-done.9.high_y
  85.9 4.6 %collective-permute-start.11 = (f32[64,512]{1,0:T(8,128)S(1)}, f32[64,512]{1,0:T(8,128)S(1)}, u32[]{:S(2)}, u32[]{:S(2)}) collective-permute-start(f32[64,512]{1,0:T(8,128)S(1)} %constant_dynamic-update-slice_fusion.3), channel_id=1, source_target_pairs={{16,0},{32,16},{48,32},{64,48},{80,64},{96,80},{112,96},{0,112},{1... | collective-permute-start | bytes 393224 | tf_op jit(solution)/shard_map/ppermute | solution.py:558
  90.5 0.0 collective-permute-start.10
  90.5 1.4 collective-permute-done.11.high_x
  91.9 0.5 collective-permute-done.10.low_x
  92.4 2.8 %last_solve.1 = (f32[10,16,512]{2,1,0:T(8,128)S(1)}, f32[128,128]{1,0:T(8,128)S(1)}) custom-call(f32[32,512]{1,0:T(8,128)S(1)} %get-tuple-element.23.own, f32[16,512]{1,0:T(8,128)S(1)} %collective-permute-done.8.low_y, f32[16,512]{1,0:T(8,128)S(1)} %collective-permute-done.9.high_y, f32[64,512]{1,0:T(8,128)S(1)} %collective-permute-done.10.low_x, ...), custom_call_target="tpu_custom_call" | custom-call | tf_op jit(solution)/shard_map/last_solve/pallas_call | solution.py:437
  95.3 19.3 %all_to_all.21 = f32[128,1,128]{2,1,0:T(1,128)S(1)} all-to-all(f32[128,1,128]{2,1,0:T(1,128)S(1)} %bitcast.35), channel_id=1, replica_groups=mesh['gx'=8,'yz'=16] {'gx','yz'}, dimensions={0} | all-to-all | bytes 131072 | tf_op jit(solution)/shard_map/all_to_all | solution.py:584
  114.6 11.3 %gather.1 = (f32[384,128]{1,0:T(8,128)}, f32[32,512]{1,0:T(8,128)S(1)}) custom-call(f32[128,128]{1,0:T(8,128)S(1)} %bitcast.34, f32[10,16,512]{2,1,0:T(8,128)S(1)} %get-tuple-element.22.before.basis_0, f32[10,16,512]{2,1,0:T(8,128)S(1)} %get-tuple-element.24.before.basis_1, f32[10,16,512]{2,1,0:T(8,128)S(1)} %get-tuple-element.29.basis_2, ...), custom_call_target="tpu_custom_call" | custom-call | tf_op jit(solution)/shard_map/gather/pallas_call | solution.py:535
  125.9 4.5 %all-to-all-start.2 = ((f32[128,1,384]{2,1,0:T(1,128)}), f32[128,1,384]{2,1,0:T(1,128)S(1)}, u32[]{:S(2)}, u32[]{:S(2)}) async-start(f32[128,1,384]{2,1,0:T(1,128)} %bitcast.17), calls=%async_computation.2 | async-start | bytes 393216 | tf_op jit(solution)/shard_map/all_to_all | solution.py:586
  130.4 0.0 copy-start
  130.5 0.7 copy.19
  131.1 9.9 %all-to-all-done.2 = f32[128,1,384]{2,1,0:T(1,128)S(1)} async-done(((f32[128,1,384]{2,1,0:T(1,128)}), f32[128,1,384]{2,1,0:T(1,128)S(1)}, u32[]{:S(2)}, u32[]{:S(2)}) %all-to-all-start.2) | async-done | bytes 196640 | tf_op jit(solution)/shard_map/all_to_all | solution.py:586
  141.0 0.0 copy-done
  141.0 0.7 unpack.1
  (15 shorter events, 0.2 us)
Async XLA Ops:
  2.9 11.5 %copy-start.2 = (s32[4,8,512]{2,1,0:T(8,128)S(1)}, s32[4,8,512]{2,1,0:T(8,128)}, u32[]{:S(2)}) copy-start(s32[4,8,512]{2,1,0:T(8,128)} %param.13) | copy-start | bytes 196612
  2.9 28.7 %all-to-all-start = ((f32[128,1,1664]{2,1,0:T(1,128)}), f32[128,1,1664]{2,1,0:T(1,128)S(1)}, u32[]{:S(2)}, u32[]{:S(2)}) async-start(f32[128,1,1664]{2,1,0:T(1,128)} %bitcast.36), calls=%async_computation | async-start | bytes 1703936 | tf_op jit(solution)/shard_map/all_to_all | solution.py:574
  14.4 0.9 copy-start.1
  43.6 7.6 %collective-permute-start = (f32[4,16,512]{2,1,0:T(8,128)S(1)}, f32[4,16,512]{2,1,0:T(8,128)S(1)}, u32[]{:S(2)}, u32[]{:S(2)}) collective-permute-start(f32[4,16,512]{2,1,0:T(8,128)S(1)} %get-tuple-element.33), channel_id=1, source_target_pairs={{0,1},{1,2},{2,3},{3,4},{4,5},{5,6},{6,7},{7,8},{8,9},{9,10},{10,1... | collective-permute-start | bytes 393224 | tf_op jit(solution)/shard_map/ppermute | solution.py:551
  44.1 7.2 %collective-permute-start.1 = (f32[4,16,512]{2,1,0:T(8,128)S(1)}, f32[4,16,512]{2,1,0:T(8,128)S(1)}, u32[]{:S(2)}, u32[]{:S(2)}) collective-permute-start(f32[4,16,512]{2,1,0:T(8,128)S(1)} %get-tuple-element.32), channel_id=1, source_target_pairs={{1,0},{2,1},{3,2},{4,3},{5,4},{6,5},{7,6},{8,7},{9,8},{10,9},{11,1... | collective-permute-start | bytes 393224 | tf_op jit(solution)/shard_map/ppermute | solution.py:552
  51.3 8.6 %collective-permute-start.3 = (f32[4,56,512]{2,1,0:T(8,128)S(1)}, f32[4,56,512]{2,1,0:T(8,128)S(1)}, u32[]{:S(2)}, u32[]{:S(2)}) collective-permute-start(f32[4,56,512]{2,1,0:T(8,128)S(1)} %pad_maximum_fusion), channel_id=1, source_target_pairs={{16,0},{32,16},{48,32},{64,48},{80,64},{96,80},{112,96},{0,112},{1... | collective-permute-start | bytes 1376264 | tf_op jit(solution)/shard_map/ppermute | solution.py:558
  53.0 6.9 %collective-permute-start.2 = (f32[4,56,512]{2,1,0:T(8,128)S(1)}, f32[4,56,512]{2,1,0:T(8,128)S(1)}, u32[]{:S(2)}, u32[]{:S(2)}) collective-permute-start(f32[4,56,512]{2,1,0:T(8,128)S(1)} %pad_maximum_fusion), channel_id=1, source_target_pairs={{0,16},{16,32},{32,48},{48,64},{64,80},{80,96},{96,112},{112,0},{1... | collective-permute-start | bytes 1376264 | tf_op jit(solution)/shard_map/ppermute | solution.py:558
  65.3 6.3 %collective-permute-start.4 = (f32[16,512]{1,0:T(8,128)S(1)}, f32[16,512]{1,0:T(8,128)S(1)}, u32[]{:S(2)}, u32[]{:S(2)}) collective-permute-start(f32[16,512]{1,0:T(8,128)S(1)} %get-tuple-element.37), channel_id=1, source_target_pairs={{0,1},{1,2},{2,3},{3,4},{4,5},{5,6},{6,7},{7,8},{8,9},{9,10},{10,1... | collective-permute-start | bytes 98312 | tf_op jit(solution)/shard_map/ppermute | solution.py:551
  65.4 6.2 %collective-permute-start.5 = (f32[16,512]{1,0:T(8,128)S(1)}, f32[16,512]{1,0:T(8,128)S(1)}, u32[]{:S(2)}, u32[]{:S(2)}) collective-permute-start(f32[16,512]{1,0:T(8,128)S(1)} %get-tuple-element.36), channel_id=1, source_target_pairs={{1,0},{2,1},{3,2},{4,3},{5,4},{6,5},{7,6},{8,7},{9,8},{10,9},{11,1... | collective-permute-start | bytes 98312 | tf_op jit(solution)/shard_map/ppermute | solution.py:552
  71.6 5.1 %collective-permute-start.7 = (f32[64,512]{1,0:T(8,128)S(1)}, f32[64,512]{1,0:T(8,128)S(1)}, u32[]{:S(2)}, u32[]{:S(2)}) collective-permute-start(f32[64,512]{1,0:T(8,128)S(1)} %constant_dynamic-update-slice_fusion), channel_id=1, source_target_pairs={{16,0},{32,16},{48,32},{64,48},{80,64},{96,80},{112,96},{0,112},{1... | collective-permute-start | bytes 393224 | tf_op jit(solution)/shard_map/ppermute | solution.py:558
  74.8 2.0 %collective-permute-start.6 = (f32[64,512]{1,0:T(8,128)S(1)}, f32[64,512]{1,0:T(8,128)S(1)}, u32[]{:S(2)}, u32[]{:S(2)}) collective-permute-start(f32[64,512]{1,0:T(8,128)S(1)} %constant_dynamic-update-slice_fusion), channel_id=1, source_target_pairs={{0,16},{16,32},{32,48},{48,64},{64,80},{80,96},{96,112},{112,0},{1... | collective-permute-start | bytes 393224 | tf_op jit(solution)/shard_map/ppermute | solution.py:558
  79.5 6.4 %collective-permute-start.8 = (f32[16,512]{1,0:T(8,128)S(1)}, f32[16,512]{1,0:T(8,128)S(1)}, u32[]{:S(2)}, u32[]{:S(2)}) collective-permute-start(f32[16,512]{1,0:T(8,128)S(1)} %get-tuple-element.35), channel_id=1, source_target_pairs={{0,1},{1,2},{2,3},{3,4},{4,5},{5,6},{6,7},{7,8},{8,9},{9,10},{10,1... | collective-permute-start | bytes 98312 | tf_op jit(solution)/shard_map/ppermute | solution.py:551
  79.6 6.3 %collective-permute-start.9 = (f32[16,512]{1,0:T(8,128)S(1)}, f32[16,512]{1,0:T(8,128)S(1)}, u32[]{:S(2)}, u32[]{:S(2)}) collective-permute-start(f32[16,512]{1,0:T(8,128)S(1)} %get-tuple-element.34), channel_id=1, source_target_pairs={{1,0},{2,1},{3,2},{4,3},{5,4},{6,5},{7,6},{8,7},{9,8},{10,9},{11,1... | collective-permute-start | bytes 98312 | tf_op jit(solution)/shard_map/ppermute | solution.py:552
  85.9 6.0 %collective-permute-start.11 = (f32[64,512]{1,0:T(8,128)S(1)}, f32[64,512]{1,0:T(8,128)S(1)}, u32[]{:S(2)}, u32[]{:S(2)}) collective-permute-start(f32[64,512]{1,0:T(8,128)S(1)} %constant_dynamic-update-slice_fusion.3), channel_id=1, source_target_pairs={{16,0},{32,16},{48,32},{64,48},{80,64},{96,80},{112,96},{0,112},{1... | collective-permute-start | bytes 393224 | tf_op jit(solution)/shard_map/ppermute | solution.py:558
  90.5 2.0 %collective-permute-start.10 = (f32[64,512]{1,0:T(8,128)S(1)}, f32[64,512]{1,0:T(8,128)S(1)}, u32[]{:S(2)}, u32[]{:S(2)}) collective-permute-start(f32[64,512]{1,0:T(8,128)S(1)} %constant_dynamic-update-slice_fusion.3), channel_id=1, source_target_pairs={{0,16},{16,32},{32,48},{48,64},{64,80},{80,96},{96,112},{112,0},{1... | collective-permute-start | bytes 393224 | tf_op jit(solution)/shard_map/ppermute | solution.py:558
  125.9 15.1 %all-to-all-start.2 = ((f32[128,1,384]{2,1,0:T(1,128)}), f32[128,1,384]{2,1,0:T(1,128)S(1)}, u32[]{:S(2)}, u32[]{:S(2)}) async-start(f32[128,1,384]{2,1,0:T(1,128)} %bitcast.17), calls=%async_computation.2 | async-start | bytes 393216 | tf_op jit(solution)/shard_map/all_to_all | solution.py:586
  130.4 10.6 %copy-start = (f32[1,128,3,128]{3,1,2,0:T(8,128)S(1)}, f32[1,128,3,128]{3,1,2,0:T(8,128)}, u32[]{:S(2)}) copy-start(f32[1,128,3,128]{3,1,2,0:T(8,128)} %param.8) | copy-start | bytes 589828

commit v4 on v3

--- a/solution.py
+++ b/solution.py
@@ -22,6 +22,9 @@
 DEPTH = 512
 CHUNK = 8
 HALO = 4
+UNROLL = 4
+WIDE = 6
+YW = 8 + 2 * WIDE
 CORNER = 3
 YE = 8 + 2 * HALO
 XE = 16
@@ -201,14 +204,16 @@
 
 
 def each_row(first, last, body):
-    def step(pair, carry):
-        body(first + 2 * pair)
-        body(first + 2 * pair + 1)
+    turns, rest = divmod(last - first, UNROLL)
+
+    def step(turn, carry):
+        for k in range(UNROLL):
+            body(first + UNROLL * turn + k)
         return carry
 
-    lax.fori_loop(0, (last - first) // 2, step, 0)
-    if (last - first) % 2:
-        body(last - 1)
+    lax.fori_loop(0, turns, step, 0)
+    for k in range(rest):
+        body(last - rest + k)
 
 
 def operate_row(field, y, offset, beta_x, beta_y, beta_z):
@@ -242,40 +247,40 @@
             ext[HALO + 8 + y, columns, :] = fix(source(slice(first, first + 4)), side, 2)
 
 
-def precondition(residual, inverse, beta_x, beta_y, beta_z, update, first, second, finish):
+def precondition(scaled, inverse, betas, update, first, second, finish, low, high):
     theta = (UPPER + LOWER) / 2.0
     delta = (UPPER - LOWER) / 2.0
     sigma = theta / delta
 
     def start(y):
-        value = inverse[y] * residual[y] * (1.0 / theta)
+        value = scaled[y] * (1.0 / theta)
         update[y] = value
         first[y] = value
 
-    each_row(1, YE - 1, start)
+    each_row(low, high, start)
     previous = 1.0 / sigma
     current = 1.0 / (2.0 * sigma - previous)
 
     def middle(y):
-        misfit = residual[y] - operate_row(first, y, 0, beta_x, beta_y, beta_z)
-        value = current * previous * update[y] + (2.0 * current / delta) * inverse[y] * misfit
+        misfit = scaled[y] - inverse[y] * operate_row(first, y, 0, *betas)
+        value = current * previous * update[y] + (2.0 * current / delta) * misfit
         update[y] = value
         second[y] = first[y] + value
 
-    each_row(2, YE - 2, middle)
+    each_row(low + 1, high - 1, middle)
     latest = 1.0 / (2.0 * sigma - current)
 
     def last(y):
-        misfit = residual[y] - operate_row(second, y, 0, beta_x, beta_y, beta_z)
-        value = latest * current * update[y] + (2.0 * latest / delta) * inverse[y] * misfit
+        misfit = scaled[y] - inverse[y] * operate_row(second, y, 0, *betas)
+        value = latest * current * update[y] + (2.0 * latest / delta) * misfit
         finish(y, second[y] + value)
 
-    each_row(3, YE - 3, last)
-
-
-def each_pair(body):
+    each_row(low + 2, high - 2, last)
+
+
+def each_pair(base, body):
     def step(pair, carry):
-        y = HALO + 2 * pair
+        y = base + 2 * pair
         rows = pl.ds(pl.multiple_of(8 * pair, 8), 8)
         lower_half = lax.broadcasted_iota(jnp.int32, (8, DEPTH), 0) < 4
         for ref, first, second in zip(*body(y)):
@@ -285,133 +290,203 @@
     lax.fori_loop(0, 4, step, 0)
 
 
+def outside_fix(edge, infinite, value, column, row):
+    outside = 0
+    if column != 1:
+        outside = outside + edge[0 if column == 0 else 1]
+    if row != 1:
+        outside = outside + edge[2 if row == 0 else 3]
+    return jnp.where(outside > 0, infinite, value)
+
+
+def face_row(total, y, end, cut, beta_x, beta_y, beta_z):
+    here = total[y]
+    across = 2.0 / (here + next_x(here))
+    beta_x[y] = across if cut is None else jnp.where(cut, 0.0, across)
+    beta_y[y] = 2.0 / (here + total[y + 1])
+    beta_z[y] = jnp.where(end, 0.0, 2.0 / (here + next_z(here)))
+
+
+def inverse_row(y, beta_x, beta_y, beta_z):
+    across, along = beta_x[y], beta_z[y]
+    return 1.0 / (
+        DAMPING + across + prev_x(across) + beta_y[y] + beta_y[y - 1] + along + prev_z(along)
+    )
+
+
 def start_kernel(
     edge, own, low_y, high_y, low_x, high_x,
-    beta_x, beta_y, beta_z, inverse, basis, basis_own, image, source_own,
-    ext, residual, update, first, second,
+    basis, basis_own, image, scaled_own, source_own, total, up, down,
+    ext, residual, scaled, beta_x, beta_y, beta_z, inverse, update, first, second,
 ):
     infinite = jnp.full((4, DEPTH), jnp.inf, F32)
     for f in range(4):
-        empty = jnp.inf if f == 0 else 0.0
-        ext[f, :, 12:16, :] = jnp.full((YE, 4, DEPTH), empty, F32)
+        target = ext.at[f - 1] if f else total
+        empty = 0.0 if f else jnp.inf
+        target[:, 12:16, :] = jnp.full((YE, 4, DEPTH), empty, F32)
         for y in range(HALO - CORNER):
             for row in (y, YE - 1 - y):
-                ext[f, row] = jnp.full((XE, DEPTH), empty, F32)
+                target[row] = jnp.full((XE, DEPTH), empty, F32)
 
         def fix(value, column, row, f=f):
-            if f:
-                return value
-            outside = 0
-            if column != 1:
-                outside = outside + edge[0 if column == 0 else 1]
-            if row != 1:
-                outside = outside + edge[2 if row == 0 else 3]
-            return jnp.where(outside > 0, infinite, value)
+            return outside_fix(edge, infinite, value, column, row) if f == 0 else value
 
         place(
-            ext.at[f],
+            target,
             CORNER,
             *[(lambda rows, ref=ref, f=f: ref[f, rows, :]) for ref in (own, low_y, high_y, low_x, high_x)],
             fix,
         )
     end = lax.broadcasted_iota(jnp.int32, (XE, DEPTH), 1) == DEPTH - 1
-
-    def faces(y):
-        total = ext[0, y]
-        beta_x[y] = 2.0 / (total + next_x(total))
-        beta_y[y] = 2.0 / (total + ext[0, y + 1])
-        beta_z[y] = jnp.where(end, 0.0, 2.0 / (total + next_z(total)))
-
-    each_row(0, YE - 1, faces)
+    betas = (beta_x, beta_y, beta_z)
+    each_row(0, YE - 1, lambda y: face_row(total, y, end, None, *betas))
 
     def source(y):
-        across, along = beta_x[y], beta_z[y]
-        diagonal = (
-            DAMPING + across + prev_x(across) + beta_y[y] + beta_y[y - 1] + along + prev_z(along)
-        )
-        inverse[y] = 1.0 / diagonal
-        vx, vy, vz = ext[1, y], ext[2, y], ext[3, y]
-        flow_x = across * (vx + next_x(vx))
-        flow_z = along * (vz + next_z(vz))
-        flow_y = beta_y[y] * (vy + ext[2, y + 1]) - beta_y[y - 1] * (ext[2, y - 1] + vy)
-        residual[y] = -0.5 * (
-            (flow_x - prev_x(flow_x)) + flow_y + (flow_z - prev_z(flow_z))
-        )
+        weight = inverse_row(y, *betas)
+        inverse[y] = weight
+        vx, vy, vz = ext[0, y], ext[1, y], ext[2, y]
+        flow_x = beta_x[y] * (vx + next_x(vx))
+        flow_z = beta_z[y] * (vz + next_z(vz))
+        flow_y = beta_y[y] * (vy + ext[1, y + 1]) - beta_y[y - 1] * (ext[1, y - 1] + vy)
+        value = -0.5 * ((flow_x - prev_x(flow_x)) + flow_y + (flow_z - prev_z(flow_z)))
+        residual[y] = value
+        scaled[y] = weight * value
 
     each_row(1, YE - 1, source)
 
     def finish(y, value):
         basis[y - 3] = value
 
-    precondition(residual, inverse, beta_x, beta_y, beta_z, update, first, second, finish)
+    precondition(scaled, inverse, betas, update, first, second, finish, 1, YE - 1)
 
     def apply(y):
-        return operate_row(basis, y, 3, beta_x, beta_y, beta_z), basis[y - 3], residual[y]
-
-    each_pair(lambda y: ((image, basis_own, source_own), apply(y), apply(y + 1)))
+        value = operate_row(basis, y, 3, *betas)
+        return value, basis[y - 3], residual[y], inverse[y] * value
+
+    each_pair(HALO, lambda y: ((image, basis_own, source_own, scaled_own), apply(y), apply(y + 1)))
+    up[:24, :] = scaled_own[8:, :]
+    up[24:, :] = own[0, 8:16, :]
+    down[:24, :] = scaled_own[:24, :]
+    down[24:, :] = own[0, 16:24, :]
 
 
 EXT = (YE, XE, DEPTH)
+BROAD = (YW, XE, DEPTH)
 BASIS = (10, XE, DEPTH)
 BLOCK = (CELLS, DEPTH)
 
 
-def start_solve(edge, own, low_y, high_y, low_x, high_x):
+def start_solve(edge, own, near):
     return pl.pallas_call(
         start_kernel,
-        out_shape=[shape(*EXT)] * 4 + [shape(*BASIS)] + [shape(*BLOCK)] * 3,
+        out_shape=[shape(*BASIS)] + [shape(*BLOCK)] * 4 + [shape(*EXT)] + [shape(*BLOCK)] * 2,
         in_specs=[SM] + [VM] * 5,
         out_specs=[VM] * 8,
-        scratch_shapes=[pltpu.VMEM((4,) + EXT, F32)] + [pltpu.VMEM(EXT, F32)] * 4,
+        scratch_shapes=[pltpu.VMEM((3,) + EXT, F32)] + [pltpu.VMEM(EXT, F32)] * 9,
         compiler_params=PARAMS,
         name="start_solve",
-    )(edge, own, low_y, high_y, low_x, high_x)
-
-
-def next_basis(own, low_y, high_y, low_x, high_x, betas, inverse, before, basis, basis_own, image, scratch):
-    ext, update, first, second = scratch
-    ext[:, 12:16, :] = jnp.zeros((YE, 4, DEPTH), F32)
-    place(
-        ext,
-        HALO,
-        *[(lambda rows, ref=ref: ref[rows, :]) for ref in (own, low_y, high_y, low_x, high_x)],
-        lambda value, column, row: value,
-    )
-
-    def finish(y, value):
-        basis[y - 3] = before[y - 3] - value
-
-    precondition(ext, inverse, *betas, update, first, second, finish)
+    )(edge, own, *near)
+
+
+def four(index):
+    return slice(4 * index, 4 * index + 4)
+
+
+def two(index):
+    return slice(2 * index, 2 * index + 2)
+
+
+def solve_kernel(
+    edge, total_near, scaled_own, wide_ly, wide_hy, wide_lx, wide_hx, far_lx, far_hx,
+    basis_0, own_0, image_0, source_own,
+    basis_1, basis_2, out_x, out_y, out_z, sums,
+    total, scaled, beta_x, beta_y, beta_z, inverse, update, first, second, vector, scaled_1, vector_2,
+    own_1, image_1, own_2, image_2,
+):
+    infinite = jnp.full((4, DEPTH), jnp.inf, F32)
+    for y in range(YE):
+        total[y + 2] = total_near[y]
+    for y in range(YW):
+        if y < 2 or y >= YW - 2:
+            total[y] = jnp.full((XE, DEPTH), jnp.inf, F32)
+        scaled[y] = jnp.zeros((XE, DEPTH), F32)
+
+    def put(y, columns, value, column):
+        row = 0 if y < WIDE else 2
+        total[y, columns, :] = outside_fix(edge, infinite, value, column, row)
+
+    middle = slice(4, 8)
+    for y in range(8):
+        scaled[WIDE + y, middle, :] = scaled_own[four(y), :]
+    for y in range(WIDE):
+        scaled[y, middle, :] = wide_ly[four(y), :]
+        scaled[WIDE + 8 + y, middle, :] = wide_hy[four(y), :]
+    for y in range(2):
+        put(y, middle, wide_ly[four(WIDE + y), :], 1)
+        put(WIDE + 12 + y, middle, wide_hy[four(WIDE + y), :], 1)
+    for side, columns, wide in ((0, slice(0, 4), wide_lx), (2, slice(8, 12), wide_hx)):
+        for y in range(8):
+            scaled[WIDE + y, columns, :] = wide[four(y), :]
+        for y in range(5):
+            scaled[1 + y, columns, :] = wide[four(8 + y), :]
+            scaled[WIDE + 8 + y, columns, :] = wide[four(13 + y), :]
+        for place_in, y in enumerate((1, 2, WIDE + 11, WIDE + 12)):
+            put(y, columns, wide[four(18 + place_in), :], side)
+    for flag, columns, far in ((4, slice(14, 16), far_lx), (5, slice(12, 14), far_hx)):
+        for y in range(10):
+            row = 0 if y == 0 else (2 if y == 9 else 1)
+            outside = edge[flag]
+            if row != 1:
+                outside = outside + edge[2 if row == 0 else 3]
+            value = far[two(10 + y), :]
+            total[WIDE - 1 + y, columns, :] = jnp.where(outside > 0, infinite[:2], value)
+            scaled[WIDE - 1 + y, columns, :] = far[two(y), :]
+
+    end = lax.broadcasted_iota(jnp.int32, (XE, DEPTH), 1) == DEPTH - 1
+    cut = lax.broadcasted_iota(jnp.int32, (XE, DEPTH), 0) == 13
+    betas = (beta_x, beta_y, beta_z)
+    each_row(0, YW - 1, lambda y: face_row(total, y, end, cut, *betas))
+
+    def invert(y):
+        inverse[y] = inverse_row(y, *betas)
+
+    each_row(1, YW - 1, invert)
+
+    def finish_1(y, value):
+        vector[y] = value
+
+    precondition(scaled, inverse, betas, update, first, second, finish_1, 0, YW)
+
+    def rescale(y):
+        value = operate_row(vector, y, 0, *betas)
+        second[y] = value
+        scaled_1[y] = inverse[y] * value
+
+    each_row(3, YW - 3, rescale)
+    each_pair(WIDE, lambda y: ((own_1, image_1), (vector[y], second[y]), (vector[y + 1], second[y + 1])))
+
+    def finish_2(y, value):
+        before = basis_0[y - 5]
+        vector_2[y - 5] = value
+        basis_1[y - 5] = before - vector[y]
+        basis_2[y - 5] = (before - vector[y]) - (vector[y] - value)
+        out_x[y - 5] = beta_x[y]
+        out_y[y - 5] = beta_y[y]
+        out_z[y - 5] = beta_z[y]
+
+    precondition(scaled_1, inverse, betas, update, first, second, finish_2, 3, YW - 3)
 
     def apply(y):
-        return operate_row(basis, y, 3, *betas), basis[y - 3]
-
-    each_pair(lambda y: ((image, basis_own), apply(y), apply(y + 1)))
-
-
-def middle_kernel(
-    own, low_y, high_y, low_x, high_x, beta_x, beta_y, beta_z, inverse, before,
-    basis, basis_own, image, *scratch,
-):
-    next_basis(
-        own, low_y, high_y, low_x, high_x, (beta_x, beta_y, beta_z), inverse, before,
-        basis, basis_own, image, scratch,
-    )
-
-
-def last_kernel(
-    own, low_y, high_y, low_x, high_x, beta_x, beta_y, beta_z, inverse, before,
-    own_0, own_1, image_0, source_own, basis, sums, own_2, image_2, *scratch,
-):
-    next_basis(
-        own, low_y, high_y, low_x, high_x, (beta_x, beta_y, beta_z), inverse, before,
-        basis, own_2, image_2, scratch,
-    )
-    vectors = (own_0[...], own_1[...], own_2[...])
-    images = (image_0[...], own[...], image_2[...])
+        return vector_2[y - 5], operate_row(vector_2, y, 5, *betas)
+
+    each_pair(WIDE, lambda y: ((own_2, image_2), apply(y), apply(y + 1)))
+    v0, v1, v2 = own_0[...], own_1[...], own_2[...]
+    a0, a1, a2 = image_0[...], image_1[...], image_2[...]
+    vectors = (v0, v0 - v1, (v0 - v1) - (v1 - v2))
+    images = (a0, a0 - a1, (a0 - a1) - (a1 - a2))
     source = source_own[...]
     pairs = [(vectors[i], images[j]) for i in range(3) for j in range(i, 3)]
-    pairs += [(vector, source) for vector in vectors]
+    pairs += [(item, source) for item in vectors]
     lane = lax.broadcasted_iota(jnp.int32, (1, CAP), 1)
     row = jnp.zeros((1, CAP), F32)
     for place_in, (a, b) in enumerate(pairs):
@@ -421,28 +496,46 @@
     sums[...] = jnp.broadcast_to(row, (GROUPS, CAP))
 
 
-def middle_solve(own, low_y, high_y, low_x, high_x, betas, inverse, before):
+def widen_kernel(block, low_y, high_y, total, column, far_up, far_down):
+    column[:32, :] = block[...]
+    column[32:52, :] = low_y[4:24, :]
+    column[52:72, :] = high_y[:20, :]
+    column[72:76, :] = low_y[28:32, :]
+    column[76:80, :] = total[0, 4:8, :]
+    column[80:84, :] = total[YE - 1, 4:8, :]
+    column[84:88, :] = high_y[24:28, :]
+    for first, target in ((2, far_up), (0, far_down)):
+        target[two(0), :] = low_y[20 + first : 22 + first, :]
+        for y in range(8):
+            target[two(1 + y), :] = block[4 * y + first : 4 * y + first + 2, :]
+        target[two(9), :] = high_y[first : first + 2, :]
+        for y in range(10):
+            target[two(10 + y), :] = total[HALO - 1 + y, 4 + first : 6 + first, :]
+
+
+def widen(block, low_y, high_y, total):
     return pl.pallas_call(
-        middle_kernel,
-        out_shape=[shape(*BASIS), shape(*BLOCK), shape(*BLOCK)],
-        in_specs=[VM] * 10,
+        widen_kernel,
+        out_shape=[shape(88, DEPTH), shape(40, DEPTH), shape(40, DEPTH)],
+        in_specs=[VM] * 4,
         out_specs=[VM] * 3,
-        scratch_shapes=[pltpu.VMEM(EXT, F32)] * 4,
+        compiler_params=SMALL,
+        name="widen",
+    )(block, low_y, high_y, total)
+
+
+def solve(edge, total, scaled, wide, basis_0, *inner):
+    return pl.pallas_call(
+        solve_kernel,
+        out_shape=[shape(*BASIS)] * 5 + [shape(GROUPS, CAP)],
+        in_specs=[SM] + [VM] * 12,
+        out_specs=[VM] * 6,
+        scratch_shapes=[pltpu.VMEM(BROAD, F32)] * 11
+        + [pltpu.VMEM(BASIS, F32)]
+        + [pltpu.VMEM(BLOCK, F32)] * 4,
         compiler_params=PARAMS,
-        name="middle_solve",
-    )(own, low_y, high_y, low_x, high_x, *betas, inverse, before)
-
-
-def last_solve(own, low_y, high_y, low_x, high_x, betas, inverse, before, *inner):
-    return pl.pallas_call(
-        last_kernel,
-        out_shape=[shape(*BASIS), shape(GROUPS, CAP)],
-        in_specs=[VM] * 14,
-        out_specs=[VM] * 2,
-        scratch_shapes=[pltpu.VMEM(BLOCK, F32)] * 2 + [pltpu.VMEM(EXT, F32)] * 4,
-        compiler_params=PARAMS,
-        name="last_solve",
-    )(own, low_y, high_y, low_x, high_x, *betas, inverse, before, *inner)
+        name="solve",
+    )(edge, total, scaled, *wide, basis_0, *inner)
 
 
 def coefficients(sums):
@@ -477,11 +570,11 @@
     each_row(0, 10, combine)
 
     def slopes(y):
-        here = pressure[y - 3]
+        here = pressure[y]
         flux_x = beta_x[y] * (here - next_x(here))
         flux_z = beta_z[y] * (here - next_z(here))
-        flux_y = beta_y[y] * (here - pressure[y - 2])
-        from_y = beta_y[y - 1] * (pressure[y - 4] - here)
+        flux_y = beta_y[y] * (here - pressure[y + 1])
+        from_y = beta_y[y - 1] * (pressure[y - 1] - here)
         return (
             (flux_x + prev_x(flux_x)) * 0.5,
             (flux_y + from_y) * 0.5,
@@ -490,7 +583,7 @@
         )
 
     targets = (carried.at[0], carried.at[1], carried.at[2], pressure_out)
-    each_pair(lambda y: (targets, slopes(y), slopes(y + 1)))
+    each_pair(1, lambda y: (targets, slopes(y), slopes(y + 1)))
     for axis in range(3):
         velocity = own[1 + axis]
         value = (velocity + carried[axis]) - FLIP * velocity
@@ -558,6 +651,20 @@
     return low_y, high_y, lax.ppermute(column, "gx", up_x), lax.ppermute(column, "gx", down_x)
 
 
+def exchange_wide(block, up, down, total, n_x, n_y):
+    up_x, up_xx = [[(i, (i + k) % n_x) for i in range(n_x)] for k in (1, 2)]
+    up_y = [(i, (i + 1) % n_y) for i in range(n_y)]
+    down_x, down_xx, down_y = [[(b, a) for a, b in pairs] for pairs in (up_x, up_xx, up_y)]
+    low_y = lax.ppermute(up, "yz", up_y)
+    high_y = lax.ppermute(down, "yz", down_y)
+    column, far_up, far_down = widen(block, low_y, high_y, total)
+    far_lx = lax.ppermute(far_up, "gx", up_xx)
+    far_hx = lax.ppermute(far_down, "gx", down_xx)
+    low_x = lax.ppermute(column, "gx", up_x)
+    high_x = lax.ppermute(column, "gx", down_x)
+    return low_y, high_y, low_x, high_x, far_lx, far_hx
+
+
 def by_block(field):
     turned = jnp.swapaxes(field, -3, -2)
     return turned.reshape(turned.shape[:-3] + (CELLS, DEPTH))
@@ -566,7 +673,9 @@
 def local(part_mass, part_vel, corner_weight, corner_base, slot_counts, water_vel, solid_flag):
     n_x, n_y = lax.axis_size("gx"), lax.axis_size("yz")
     at_x, at_y = lax.axis_index("gx"), lax.axis_index("yz")
-    edge = jnp.stack([at_x == 0, at_x == n_x - 1, at_y == 0, at_y == n_y - 1]).astype(jnp.int32)
+    edge = jnp.stack(
+        [at_x == 0, at_x == n_x - 1, at_y == 0, at_y == n_y - 1, at_x <= 1, at_x >= n_x - 2]
+    ).astype(jnp.int32)
     velocity = jnp.swapaxes(part_vel[0], 0, 1)
     message = pack(
         part_mass[0], velocity, corner_weight.reshape(8 * GROUPS, CAP), corner_base[0], slot_counts
@@ -575,11 +684,11 @@
     msg = msg.reshape(GROUPS * FIELDS, CAP)
     density = by_block(jnp.where(solid_flag == 1, SOLID_WATER, 1.0).astype(F32))
     own = spread(msg, density, by_block(water_vel))
-    *rest, basis_0, own_0, image_0, source = start_solve(edge, own, *exchange(own, n_x, n_y, CORNER))
-    betas, inverse = rest[:3], rest[3]
-    basis_1, own_1, image_1 = middle_solve(image_0, *exchange(image_0, n_x, n_y, HALO), betas, inverse, basis_0)
-    basis_2, sums = last_solve(
-        image_1, *exchange(image_1, n_x, n_y, HALO), betas, inverse, basis_1, own_0, own_1, image_0, source
+    near = exchange(own, n_x, n_y, CORNER)
+    basis_0, own_0, image_0, scaled, source, total, up, down = start_solve(edge, own, near)
+    wide = exchange_wide(scaled, up, down, total, n_x, n_y)
+    basis_1, basis_2, *betas, sums = solve(
+        edge, total, scaled, wide, basis_0, own_0, image_0, source
     )
     sums = lax.all_to_all(sums, ALL, 0, 0, tiled=True)
     sampled, pressure = gather(sums, (basis_0, basis_1, basis_2), betas, own, msg)

time: 142 us -> 132 us (0.930)
  starting transfers between devices: 41.1 us -> 34 us
  blocking collectives: 19.3 us -> 17.2 us
    ppermute x0 -> x6, starting transfers between devices: none -> 11 us  [the longest x1 5 us: exchange_wide(): high_y = lax.ppermute(down, 'yz', down_y)]
    ppermute x3 -> x1, starting transfers between devices: 14.5 us -> 4.41 us  [exchange(): high_y = lax.ppermute(block[..., :half, :], 'yz', down_y)]
    ppermute x3 -> x1, starting transfers between devices: 9.53 us -> 1.71 us  [exchange(): lax.ppermute(column, 'gx', down_x)]
    ppermute x0 -> x6, waiting for transfers between devices: none -> 6.13 us  [the longest x1 4.54 us: exchange_wide(): far_lx = lax.ppermute(far_up, 'gx', up_xx)]
    ppermute x3 -> x1, waiting for transfers between devices: 9.65 us -> 6.32 us  [exchange(): lax.ppermute(column, 'gx', down_x)]
    ppermute x3 -> x1, waiting for transfers between devices: 5.17 us -> 2.75 us  [exchange(): low_y = lax.ppermute(block[..., CELLS - half:, :], 'yz', up_y)]
    all_to_all x1, blocking collectives: 19.3 us -> 17.2 us  [local(): sums = lax.all_to_all(sums, ALL, 0, 0, tiled=True)]
  transfers between devices with their start and end apart: 14 -> 12, of which waited for: 10 -> 6; matrix products, arithmetic and copies ran while one was open for 1% -> 1% of each run, Pallas kernels for 0% -> 0%
where the time goes in v4:
time: 132 us
  waiting for transfers between devices  41.2 us (31%)
  Pallas kernels  36.8 us (28%)
  starting transfers between devices  34 us (26%)
  blocking collectives  17.2 us (13%)
  local copies, waits for them, and re-layouts  1.91 us (1%)
    all_to_all x1, blocking collectives, local(): sums = lax.all_to_all(sums, ALL, 0, 0, tiled=True)  17.2 us
    all_to_all x1, waiting for transfers between devices, local(): lax.all_to_all(message.reshape(GROUPS, 1, FIELDS * CAP), ALL, 0, 0, tiled...  16.1 us
    pallas_call x1, Pallas kernels, spread(): pl.pallas_call(spread_kernel, out_shape=shape(4, CELLS, DEPTH), in_specs=...  11.9 us
    all_to_all x1, starting transfers between devices, local(): lax.all_to_all(message.reshape(GROUPS, 1, FIELDS * CAP), ALL, 0, 0, tiled...  11.5 us
    pallas_call x1, Pallas kernels, gather(): pl.pallas_call(gather_kernel, out_shape=[shape(3 * GROUPS, CAP), shape(*B...  11.4 us
    all_to_all x1, waiting for transfers between devices, local(): lax.all_to_all(sampled.reshape(GROUPS, 1, 3 * CAP), ALL, 0, 0, tiled=True)  9.92 us
    pallas_call x1, Pallas kernels, solve(): pl.pallas_call(solve_kernel, out_shape=[shape(*BASIS)] * 5 + [shape(GROUP...  6.5 us
    ppermute x1, waiting for transfers between devices, exchange(): lax.ppermute(column, 'gx', down_x)  6.32 us
  transfers between devices with their start and end apart: 12, of which 6 were waited for; matrix products, arithmetic and copies ran while one was open for 1% of the time, Pallas kernels for 0%

profile of v4, /device:TPU:1, one launch (start us, length us, event | category | flops | bytes accessed | tf_op | source)
XLA Modules:
  0.0 132.0 jit_solution(2965010044551742881)
XLA Ops:
  0.6 2.3 %pack.1 = f32[1664,128]{1,0:T(8,128)} custom-call(f32[128,128]{1,0:T(8,128)} %bitcast.42, f32[3,128,128]{2,1,0:T(8,128)} %bitcast.32, f32[1024,128]{1,0:T(8,128)} %bitcast.39, s32[128,128]{1,0:T(8,128)} %bitcast.43, s32[1,128]{1,0:T(1,128)} %count_h.1), custom_call_target="tpu_custom_call" | custom-call | tf_op jit(solution)/shard_map/pack/pallas_call | solution.py:100
  2.9 0.0 copy-start.2
  2.9 11.5 %all-to-all-start = ((f32[128,1,1664]{2,1,0:T(1,128)}), f32[128,1,1664]{2,1,0:T(1,128)S(1)}, u32[]{:S(2)}, u32[]{:S(2)}) async-start(f32[128,1,1664]{2,1,0:T(1,128)} %bitcast.38), calls=%async_computation | async-start | bytes 1703936 | tf_op jit(solution)/shard_map/all_to_all | solution.py:683
  14.4 0.0 copy-done.2
  14.4 0.0 copy-start.1
  14.5 0.8 copy-done.1
  15.4 0.1 copy.14
  15.5 0.1 reshape.34.water
  15.6 16.1 %all-to-all-done = f32[128,1,1664]{2,1,0:T(1,128)S(1)} async-done(((f32[128,1,1664]{2,1,0:T(1,128)}), f32[128,1,1664]{2,1,0:T(1,128)S(1)}, u32[]{:S(2)}, u32[]{:S(2)}) %all-to-all-start) | async-done | bytes 852000 | tf_op jit(solution)/shard_map/all_to_all | solution.py:683
  31.6 11.9 %spread.1.own = f32[4,32,512]{2,1,0:T(8,128)S(1)} custom-call(f32[1664,128]{1,0:T(8,128)S(1)} %bitcast.30, f32[32,512]{1,0:T(8,128)S(1)} %reshape.33.density, f32[3,32,512]{2,1,0:T(8,128)S(1)} %reshape.34.water), custom_call_target="tpu_custom_call" | custom-call | tf_op jit(solution)/shard_map/spread/pallas_call | solution.py:177
  43.6 0.4 collective-permute-start
  44.1 4.4 %collective-permute-start.1 = (f32[4,16,512]{2,1,0:T(8,128)S(1)}, f32[4,16,512]{2,1,0:T(8,128)S(1)}, u32[]{:S(2)}, u32[]{:S(2)}) collective-permute-start(f32[4,16,512]{2,1,0:T(8,128)S(1)} %get-tuple-element.40), channel_id=1, source_target_pairs={{1,0},{2,1},{3,2},{4,3},{5,4},{6,5},{7,6},{8,7},{9,8},{10,9},{11,1... | collective-permute-start | bytes 393224 | tf_op jit(solution)/shard_map/ppermute | solution.py:645
  48.5 2.8 %collective-permute-done.low_y = f32[4,16,512]{2,1,0:T(8,128)S(1)} collective-permute-done((f32[4,16,512]{2,1,0:T(8,128)S(1)}, f32[4,16,512]{2,1,0:T(8,128)S(1)}, u32[]{:S(2)}, u32[]{:S(2)}) %collective-permute-start) | collective-permute-done | bytes 131104 | tf_op jit(solution)/shard_map/ppermute | solution.py:644
  51.2 0.0 collective-permute-done.1.high_y
  51.3 1.7 %collective-permute-start.3 = (f32[4,56,512]{2,1,0:T(8,128)S(1)}, f32[4,56,512]{2,1,0:T(8,128)S(1)}, u32[]{:S(2)}, u32[]{:S(2)}) collective-permute-start(f32[4,56,512]{2,1,0:T(8,128)S(1)} %pad_maximum_fusion), channel_id=1, source_target_pairs={{16,0},{32,16},{48,32},{64,48},{80,64},{96,80},{112,96},{0,112},{1... | collective-permute-start | bytes 1376264 | tf_op jit(solution)/shard_map/ppermute | solution.py:651
  53.0 0.5 collective-permute-start.2
  53.5 0.1 stack.27
  53.6 6.3 %collective-permute-done.3.high_x = f32[4,56,512]{2,1,0:T(8,128)S(1)} collective-permute-done((f32[4,56,512]{2,1,0:T(8,128)S(1)}, f32[4,56,512]{2,1,0:T(8,128)S(1)}, u32[]{:S(2)}, u32[]{:S(2)}) %collective-permute-start.3) | collective-permute-done | bytes 458784 | tf_op jit(solution)/shard_map/ppermute | solution.py:651
  59.9 0.0 collective-permute-done.2.low_x
  59.9 3.9 %start_solve.1 = (f32[10,16,512]{2,1,0:T(8,128)S(1)}, f32[32,512]{1,0:T(8,128)S(1)}, f32[32,512]{1,0:T(8,128)S(1)}, f32[32,512]{1,0:T(8,128)S(1)}, f32[32,512]{1...) custom-call(s32[6]{0:T(128)S(1)} %convert_element_type.3.edge, ...), custom_call_target="tpu_custom_call" | custom-call | tf_op jit(solution)/shard_map/start_solve/pallas_call | solution.py:380
  63.8 0.1 collective-permute-start.4
  63.9 5.0 %collective-permute-start.5 = (f32[32,512]{1,0:T(8,128)S(1)}, f32[32,512]{1,0:T(8,128)S(1)}, u32[]{:S(2)}, u32[]{:S(2)}) collective-permute-start(f32[32,512]{1,0:T(8,128)S(1)} %get-tuple-element.24), channel_id=1, source_target_pairs={{1,0},{2,1},{3,2},{4,3},{5,4},{6,5},{7,6},{8,7},{9,8},{10,9},{11,1... | collective-permute-start | bytes 196616 | tf_op jit(solution)/shard_map/ppermute | solution.py:659
  68.9 1.6 %collective-permute-done.4.low_y.wide_ly = f32[32,512]{1,0:T(8,128)S(1)} collective-permute-done((f32[32,512]{1,0:T(8,128)S(1)}, f32[32,512]{1,0:T(8,128)S(1)}, u32[]{:S(2)}, u32[]{:S(2)}) %collective-permute-start.4) | collective-permute-done | bytes 65568 | tf_op jit(solution)/shard_map/ppermute | solution.py:658
  70.5 0.0 collective-permute-done.5.high_y.wide_hy
  70.5 0.1 widen.1
  70.6 3.3 %collective-permute-start.7 = (f32[88,512]{1,0:T(8,128)S(1)}, f32[88,512]{1,0:T(8,128)S(1)}, u32[]{:S(2)}, u32[]{:S(2)}) collective-permute-start(f32[88,512]{1,0:T(8,128)S(1)} %get-tuple-element.25), channel_id=1, source_target_pairs={{16,0},{32,16},{48,32},{64,48},{80,64},{96,80},{112,96},{0,112},{1... | collective-permute-start | bytes 540680 | tf_op jit(solution)/shard_map/ppermute | solution.py:664
  73.8 0.0 collective-permute-start.6
  73.8 0.0 collective-permute-start.8
  73.8 2.7 %collective-permute-start.9 = (f32[40,512]{1,0:T(8,128)S(1)}, f32[40,512]{1,0:T(8,128)S(1)}, u32[]{:S(2)}, u32[]{:S(2)}) collective-permute-start(f32[40,512]{1,0:T(8,128)S(1)} %get-tuple-element.27), channel_id=1, source_target_pairs={{32,0},{48,16},{64,32},{80,48},{96,64},{112,80},{0,96},{16,112},{3... | collective-permute-start | bytes 245768 | tf_op jit(solution)/shard_map/ppermute | solution.py:662
  76.5 4.5 %collective-permute-done.8.far_lx = f32[40,512]{1,0:T(8,128)S(1)} collective-permute-done((f32[40,512]{1,0:T(8,128)S(1)}, f32[40,512]{1,0:T(8,128)S(1)}, u32[]{:S(2)}, u32[]{:S(2)}) %collective-permute-start.8) | collective-permute-done | bytes 81952 | tf_op jit(solution)/shard_map/ppermute | solution.py:661
  81.1 0.0 collective-permute-done.9.far_hx
  81.1 0.0 collective-permute-done.7.wide_hx
  81.1 0.0 collective-permute-done.6.wide_lx
  81.1 6.5 %solve.1 = (f32[10,16,512]{2,1,0:T(8,128)S(1)}, f32[10,16,512]{2,1,0:T(8,128)S(1)}, f32[10,16,512]{2,1,0:T(8,128)S(1)}, f32[10,16,512]{2,1,0:T(8,128)S(1)}, f32[...) custom-call(s32[6]{0:T(128)S(1)} %convert_element_type.3.edge, f32[16,16,512]{2,1,0:T(8,128)S(1)} %get-tuple-element.21.total.total_near, ...), custom_call_target="tpu_custom_call" | custom-call | tf_op jit(solution)/shard_map/solve/pallas_call | solution.py:528
  87.6 17.2 %all_to_all.21 = f32[128,1,128]{2,1,0:T(1,128)S(1)} all-to-all(f32[128,1,128]{2,1,0:T(1,128)S(1)} %bitcast.37), channel_id=1, replica_groups=mesh['gx'=8,'yz'=16] {'gx','yz'}, dimensions={0} | all-to-all | bytes 131072 | tf_op jit(solution)/shard_map/all_to_all | solution.py:693
  104.8 11.4 %gather.1 = (f32[384,128]{1,0:T(8,128)}, f32[32,512]{1,0:T(8,128)S(1)}) custom-call(f32[128,128]{1,0:T(8,128)S(1)} %bitcast.36, f32[10,16,512]{2,1,0:T(8,128)S(1)} %get-tuple-element.28.basis_0, f32[10,16,512]{2,1,0:T(8,128)S(1)} %get-tuple-element.33.basis_1, f32[10,16,512]{2,1,0:T(8,128)S(1)} %get-tuple-element.34.basis_2, ...), custom_call_target="tpu_custom_call" | custom-call | tf_op jit(solution)/shard_map/gather/pallas_call | solution.py:628
  116.2 4.5 %all-to-all-start.2 = ((f32[128,1,384]{2,1,0:T(1,128)}), f32[128,1,384]{2,1,0:T(1,128)S(1)}, u32[]{:S(2)}, u32[]{:S(2)}) async-start(f32[128,1,384]{2,1,0:T(1,128)} %bitcast.19), calls=%async_computation.2 | async-start | bytes 393216 | tf_op jit(solution)/shard_map/all_to_all | solution.py:695
  120.6 0.0 copy-start
  120.7 0.7 copy.19
  121.3 9.9 %all-to-all-done.2 = f32[128,1,384]{2,1,0:T(1,128)S(1)} async-done(((f32[128,1,384]{2,1,0:T(1,128)}), f32[128,1,384]{2,1,0:T(1,128)S(1)}, u32[]{:S(2)}, u32[]{:S(2)}) %all-to-all-start.2) | async-done | bytes 196640 | tf_op jit(solution)/shard_map/all_to_all | solution.py:695
  131.3 0.0 copy-done
  131.3 0.7 unpack.1
  (8 shorter events, 0.2 us)
Async XLA Ops:
  2.9 11.5 %copy-start.2 = (s32[4,8,512]{2,1,0:T(8,128)S(1)}, s32[4,8,512]{2,1,0:T(8,128)}, u32[]{:S(2)}) copy-start(s32[4,8,512]{2,1,0:T(8,128)} %param.13) | copy-start | bytes 196612
  2.9 28.7 %all-to-all-start = ((f32[128,1,1664]{2,1,0:T(1,128)}), f32[128,1,1664]{2,1,0:T(1,128)S(1)}, u32[]{:S(2)}, u32[]{:S(2)}) async-start(f32[128,1,1664]{2,1,0:T(1,128)} %bitcast.38), calls=%async_computation | async-start | bytes 1703936 | tf_op jit(solution)/shard_map/all_to_all | solution.py:683
  14.4 0.9 copy-start.1
  43.6 7.6 %collective-permute-start = (f32[4,16,512]{2,1,0:T(8,128)S(1)}, f32[4,16,512]{2,1,0:T(8,128)S(1)}, u32[]{:S(2)}, u32[]{:S(2)}) collective-permute-start(f32[4,16,512]{2,1,0:T(8,128)S(1)} %get-tuple-element.41), channel_id=1, source_target_pairs={{0,1},{1,2},{2,3},{3,4},{4,5},{5,6},{6,7},{7,8},{8,9},{9,10},{10,1... | collective-permute-start | bytes 393224 | tf_op jit(solution)/shard_map/ppermute | solution.py:644
  44.1 7.2 %collective-permute-start.1 = (f32[4,16,512]{2,1,0:T(8,128)S(1)}, f32[4,16,512]{2,1,0:T(8,128)S(1)}, u32[]{:S(2)}, u32[]{:S(2)}) collective-permute-start(f32[4,16,512]{2,1,0:T(8,128)S(1)} %get-tuple-element.40), channel_id=1, source_target_pairs={{1,0},{2,1},{3,2},{4,3},{5,4},{6,5},{7,6},{8,7},{9,8},{10,9},{11,1... | collective-permute-start | bytes 393224 | tf_op jit(solution)/shard_map/ppermute | solution.py:645
  51.3 8.6 %collective-permute-start.3 = (f32[4,56,512]{2,1,0:T(8,128)S(1)}, f32[4,56,512]{2,1,0:T(8,128)S(1)}, u32[]{:S(2)}, u32[]{:S(2)}) collective-permute-start(f32[4,56,512]{2,1,0:T(8,128)S(1)} %pad_maximum_fusion), channel_id=1, source_target_pairs={{16,0},{32,16},{48,32},{64,48},{80,64},{96,80},{112,96},{0,112},{1... | collective-permute-start | bytes 1376264 | tf_op jit(solution)/shard_map/ppermute | solution.py:651
  53.0 6.9 %collective-permute-start.2 = (f32[4,56,512]{2,1,0:T(8,128)S(1)}, f32[4,56,512]{2,1,0:T(8,128)S(1)}, u32[]{:S(2)}, u32[]{:S(2)}) collective-permute-start(f32[4,56,512]{2,1,0:T(8,128)S(1)} %pad_maximum_fusion), channel_id=1, source_target_pairs={{0,16},{16,32},{32,48},{48,64},{64,80},{80,96},{96,112},{112,0},{1... | collective-permute-start | bytes 1376264 | tf_op jit(solution)/shard_map/ppermute | solution.py:651
  63.8 6.7 %collective-permute-start.4 = (f32[32,512]{1,0:T(8,128)S(1)}, f32[32,512]{1,0:T(8,128)S(1)}, u32[]{:S(2)}, u32[]{:S(2)}) collective-permute-start(f32[32,512]{1,0:T(8,128)S(1)} %get-tuple-element.23), channel_id=1, source_target_pairs={{0,1},{1,2},{2,3},{3,4},{4,5},{5,6},{6,7},{7,8},{8,9},{9,10},{10,1... | collective-permute-start | bytes 196616 | tf_op jit(solution)/shard_map/ppermute | solution.py:658
  63.9 6.6 %collective-permute-start.5 = (f32[32,512]{1,0:T(8,128)S(1)}, f32[32,512]{1,0:T(8,128)S(1)}, u32[]{:S(2)}, u32[]{:S(2)}) collective-permute-start(f32[32,512]{1,0:T(8,128)S(1)} %get-tuple-element.24), channel_id=1, source_target_pairs={{1,0},{2,1},{3,2},{4,3},{5,4},{6,5},{7,6},{8,7},{9,8},{10,9},{11,1... | collective-permute-start | bytes 196616 | tf_op jit(solution)/shard_map/ppermute | solution.py:659
  70.6 10.5 %collective-permute-start.7 = (f32[88,512]{1,0:T(8,128)S(1)}, f32[88,512]{1,0:T(8,128)S(1)}, u32[]{:S(2)}, u32[]{:S(2)}) collective-permute-start(f32[88,512]{1,0:T(8,128)S(1)} %get-tuple-element.25), channel_id=1, source_target_pairs={{16,0},{32,16},{48,32},{64,48},{80,64},{96,80},{112,96},{0,112},{1... | collective-permute-start | bytes 540680 | tf_op jit(solution)/shard_map/ppermute | solution.py:664
  73.8 7.2 %collective-permute-start.6 = (f32[88,512]{1,0:T(8,128)S(1)}, f32[88,512]{1,0:T(8,128)S(1)}, u32[]{:S(2)}, u32[]{:S(2)}) collective-permute-start(f32[88,512]{1,0:T(8,128)S(1)} %get-tuple-element.25), channel_id=1, source_target_pairs={{0,16},{16,32},{32,48},{48,64},{64,80},{80,96},{96,112},{112,0},{1... | collective-permute-start | bytes 540680 | tf_op jit(solution)/shard_map/ppermute | solution.py:663
  73.8 7.2 %collective-permute-start.8 = (f32[40,512]{1,0:T(8,128)S(1)}, f32[40,512]{1,0:T(8,128)S(1)}, u32[]{:S(2)}, u32[]{:S(2)}) collective-permute-start(f32[40,512]{1,0:T(8,128)S(1)} %get-tuple-element.26), channel_id=1, source_target_pairs={{0,32},{16,48},{32,64},{48,80},{64,96},{80,112},{96,0},{112,16},{1... | collective-permute-start | bytes 245768 | tf_op jit(solution)/shard_map/ppermute | solution.py:661
  73.8 7.2 %collective-permute-start.9 = (f32[40,512]{1,0:T(8,128)S(1)}, f32[40,512]{1,0:T(8,128)S(1)}, u32[]{:S(2)}, u32[]{:S(2)}) collective-permute-start(f32[40,512]{1,0:T(8,128)S(1)} %get-tuple-element.27), channel_id=1, source_target_pairs={{32,0},{48,16},{64,32},{80,48},{96,64},{112,80},{0,96},{16,112},{3... | collective-permute-start | bytes 245768 | tf_op jit(solution)/shard_map/ppermute | solution.py:662
  116.2 15.1 %all-to-all-start.2 = ((f32[128,1,384]{2,1,0:T(1,128)}), f32[128,1,384]{2,1,0:T(1,128)S(1)}, u32[]{:S(2)}, u32[]{:S(2)}) async-start(f32[128,1,384]{2,1,0:T(1,128)} %bitcast.19), calls=%async_computation.2 | async-start | bytes 393216 | tf_op jit(solution)/shard_map/all_to_all | solution.py:695
  120.6 10.6 %copy-start = (f32[1,128,3,128]{3,1,2,0:T(8,128)S(1)}, f32[1,128,3,128]{3,1,2,0:T(8,128)}, u32[]{:S(2)}) copy-start(f32[1,128,3,128]{3,1,2,0:T(8,128)} %param.8) | copy-start | bytes 589828

commit v5 on v4

--- a/solution.py
+++ b/solution.py
@@ -21,6 +21,7 @@
 CELLS = 32
 DEPTH = 512
 CHUNK = 8
+PICK = 16
 HALO = 4
 UNROLL = 4
 WIDE = 6
@@ -29,6 +30,7 @@
 YE = 8 + 2 * HALO
 XE = 16
 PARAMS = pltpu.CompilerParams(vmem_limit_bytes=20 * 1024 * 1024)
+LARGE = pltpu.CompilerParams(vmem_limit_bytes=28 * 1024 * 1024)
 SMALL = pltpu.CompilerParams(vmem_limit_bytes=8 * 1024 * 1024)
 VM = pl.BlockSpec(memory_space=pltpu.VMEM)
 SM = pl.BlockSpec(memory_space=pltpu.SMEM)
@@ -203,12 +205,12 @@
     return pltpu.roll(row, 1, 1)
 
 
-def each_row(first, last, body):
-    turns, rest = divmod(last - first, UNROLL)
+def each_row(first, last, body, unroll=UNROLL):
+    turns, rest = divmod(last - first, unroll)
 
     def step(turn, carry):
-        for k in range(UNROLL):
-            body(first + UNROLL * turn + k)
+        for k in range(unroll):
+            body(first + unroll * turn + k)
         return carry
 
     lax.fori_loop(0, turns, step, 0)
@@ -247,7 +249,7 @@
             ext[HALO + 8 + y, columns, :] = fix(source(slice(first, first + 4)), side, 2)
 
 
-def precondition(scaled, inverse, betas, update, first, second, finish, low, high):
+def precondition(scaled, inverse, betas, update, first, second, finish, low, high, unroll=UNROLL):
     theta = (UPPER + LOWER) / 2.0
     delta = (UPPER - LOWER) / 2.0
     sigma = theta / delta
@@ -257,7 +259,7 @@
         update[y] = value
         first[y] = value
 
-    each_row(low, high, start)
+    each_row(low, high, start, unroll)
     previous = 1.0 / sigma
     current = 1.0 / (2.0 * sigma - previous)
 
@@ -267,7 +269,7 @@
         update[y] = value
         second[y] = first[y] + value
 
-    each_row(low + 1, high - 1, middle)
+    each_row(low + 1, high - 1, middle, unroll)
     latest = 1.0 / (2.0 * sigma - current)
 
     def last(y):
@@ -275,7 +277,7 @@
         value = latest * current * update[y] + (2.0 * latest / delta) * misfit
         finish(y, second[y] + value)
 
-    each_row(low + 2, high - 2, last)
+    each_row(low + 2, high - 2, last, unroll)
 
 
 def each_pair(base, body):
@@ -445,24 +447,24 @@
     end = lax.broadcasted_iota(jnp.int32, (XE, DEPTH), 1) == DEPTH - 1
     cut = lax.broadcasted_iota(jnp.int32, (XE, DEPTH), 0) == 13
     betas = (beta_x, beta_y, beta_z)
-    each_row(0, YW - 1, lambda y: face_row(total, y, end, cut, *betas))
+    each_row(0, YW - 1, lambda y: face_row(total, y, end, cut, *betas), 8)
 
     def invert(y):
         inverse[y] = inverse_row(y, *betas)
 
-    each_row(1, YW - 1, invert)
+    each_row(1, YW - 1, invert, 8)
 
     def finish_1(y, value):
         vector[y] = value
 
-    precondition(scaled, inverse, betas, update, first, second, finish_1, 0, YW)
+    precondition(scaled, inverse, betas, update, first, second, finish_1, 0, YW, 8)
 
     def rescale(y):
         value = operate_row(vector, y, 0, *betas)
         second[y] = value
         scaled_1[y] = inverse[y] * value
 
-    each_row(3, YW - 3, rescale)
+    each_row(3, YW - 3, rescale, 8)
     each_pair(WIDE, lambda y: ((own_1, image_1), (vector[y], second[y]), (vector[y + 1], second[y + 1])))
 
     def finish_2(y, value):
@@ -474,7 +476,7 @@
         out_y[y - 5] = beta_y[y]
         out_z[y - 5] = beta_z[y]
 
-    precondition(scaled_1, inverse, betas, update, first, second, finish_2, 3, YW - 3)
+    precondition(scaled_1, inverse, betas, update, first, second, finish_2, 3, YW - 3, 8)
 
     def apply(y):
         return vector_2[y - 5], operate_row(vector_2, y, 5, *betas)
@@ -595,21 +597,21 @@
     level = lax.broadcasted_iota(jnp.int32, (DEPTH, CAP), 0)
 
     def build(chunk, hot):
-        for j in range(CHUNK):
-            depth_row = depth_s[pl.ds(chunk * CHUNK + j, 1), :]
+        for j in range(PICK):
+            depth_row = depth_s[pl.ds(chunk * PICK + j, 1), :]
             hot[:, j * CAP : (j + 1) * CAP] = jnp.where(level == depth_row, 1.0, 0.0)
 
     def pick(chunk, hot):
         both = one_pass(table_s[...], hot[...])
         table = both[:192] + both[192:]
-        for j in range(CHUNK):
-            source = chunk * CHUNK + j
+        for j in range(PICK):
+            source = chunk * PICK + j
             weights = tile_weights(msg, source, plane_s[pl.ds(source, 1), :])
             for axis in range(3):
                 picked = table[axis * 64 : (axis + 1) * 64, j * CAP : (j + 1) * CAP] * weights
                 out[pl.ds(3 * source + axis, 1), :] = jnp.sum(picked, axis=0, keepdims=True)
 
-    turns = GROUPS // CHUNK
+    turns = GROUPS // PICK
     build(0, hot_a)
 
     def body(turn, carry):
@@ -624,14 +626,14 @@
 
 def gather(sums, bases, betas, own, msg):
     index = pltpu.VMEM((GROUPS, CAP), jnp.int32)
-    hot = pltpu.VMEM((DEPTH, CHUNK * CAP), F32)
+    hot = pltpu.VMEM((DEPTH, PICK * CAP), F32)
     return pl.pallas_call(
         gather_kernel,
         out_shape=[shape(3 * GROUPS, CAP), shape(*BLOCK)],
         in_specs=[VM] * 9,
         out_specs=[VM] * 2,
         scratch_shapes=[index, index, pltpu.VMEM(BASIS, F32), pltpu.VMEM((3,) + BLOCK, F32), pltpu.VMEM((384, DEPTH), F32), hot, hot],
-        compiler_params=PARAMS,
+        compiler_params=LARGE,
         name="gather",
     )(sums, *bases, *betas, own, msg)
 

time: 132 us -> 132 us (level)
  no operation moved by 1% of the time
where the time goes in v5:
time: 132 us; the launch traced here: 131 us
  waiting for transfers between devices  41.2 us (31%)
  Pallas kernels  36 us (27%)
  starting transfers between devices  34 us (26%)
  blocking collectives  17.2 us (13%)
  local copies, waits for them, and re-layouts  1.91 us (1%)
    all_to_all x1, blocking collectives, local(): sums = lax.all_to_all(sums, ALL, 0, 0, tiled=True)  17.2 us
    all_to_all x1, waiting for transfers between devices, local(): lax.all_to_all(message.reshape(GROUPS, 1, FIELDS * CAP), ALL, 0, 0, tiled...  16.1 us
    pallas_call x1, Pallas kernels, spread(): pl.pallas_call(spread_kernel, out_shape=shape(4, CELLS, DEPTH), in_specs=...  11.9 us
    all_to_all x1, starting transfers between devices, local(): lax.all_to_all(message.reshape(GROUPS, 1, FIELDS * CAP), ALL, 0, 0, tiled...  11.5 us
    pallas_call x1, Pallas kernels, gather(): pl.pallas_call(gather_kernel, out_shape=[shape(3 * GROUPS, CAP), shape(*B...  11.1 us
    all_to_all x1, waiting for transfers between devices, local(): lax.all_to_all(sampled.reshape(GROUPS, 1, 3 * CAP), ALL, 0, 0, tiled=True)  9.92 us
    ppermute x1, waiting for transfers between devices, exchange(): lax.ppermute(column, 'gx', down_x)  6.32 us
    pallas_call x1, Pallas kernels, solve(): pl.pallas_call(solve_kernel, out_shape=[shape(*BASIS)] * 5 + [shape(GROUP...  5.97 us
  transfers between devices with their start and end apart: 12, of which 6 were waited for; matrix products, arithmetic and copies ran while one was open for 1% of the time, Pallas kernels for 0%

profile of v5, /device:TPU:1, one launch (start us, length us, event | category | flops | bytes accessed | tf_op | source)
XLA Modules:
  0.0 131.2 jit_solution(1296340431421231258)
XLA Ops:
  0.6 2.3 %pack.1 = f32[1664,128]{1,0:T(8,128)} custom-call(f32[128,128]{1,0:T(8,128)} %bitcast.42, f32[3,128,128]{2,1,0:T(8,128)} %bitcast.32, f32[1024,128]{1,0:T(8,128)} %bitcast.39, s32[128,128]{1,0:T(8,128)} %bitcast.43, s32[1,128]{1,0:T(1,128)} %count_h.1), custom_call_target="tpu_custom_call" | custom-call | tf_op jit(solution)/shard_map/pack/pallas_call | solution.py:102
  2.9 0.0 copy-start.2
  2.9 11.5 %all-to-all-start = ((f32[128,1,1664]{2,1,0:T(1,128)}), f32[128,1,1664]{2,1,0:T(1,128)S(1)}, u32[]{:S(2)}, u32[]{:S(2)}) async-start(f32[128,1,1664]{2,1,0:T(1,128)} %bitcast.38), calls=%async_computation | async-start | bytes 1703936 | tf_op jit(solution)/shard_map/all_to_all | solution.py:685
  14.4 0.0 copy-done.2
  14.4 0.0 copy-start.1
  14.5 0.8 copy-done.1
  15.4 0.1 copy.14
  15.5 0.1 reshape.34.water
  15.6 16.1 %all-to-all-done = f32[128,1,1664]{2,1,0:T(1,128)S(1)} async-done(((f32[128,1,1664]{2,1,0:T(1,128)}), f32[128,1,1664]{2,1,0:T(1,128)S(1)}, u32[]{:S(2)}, u32[]{:S(2)}) %all-to-all-start) | async-done | bytes 852000 | tf_op jit(solution)/shard_map/all_to_all | solution.py:685
  31.6 11.9 %spread.1.own = f32[4,32,512]{2,1,0:T(8,128)S(1)} custom-call(f32[1664,128]{1,0:T(8,128)S(1)} %bitcast.30, f32[32,512]{1,0:T(8,128)S(1)} %reshape.33.density, f32[3,32,512]{2,1,0:T(8,128)S(1)} %reshape.34.water), custom_call_target="tpu_custom_call" | custom-call | tf_op jit(solution)/shard_map/spread/pallas_call | solution.py:179
  43.6 0.4 collective-permute-start
  44.1 4.4 %collective-permute-start.1 = (f32[4,16,512]{2,1,0:T(8,128)S(1)}, f32[4,16,512]{2,1,0:T(8,128)S(1)}, u32[]{:S(2)}, u32[]{:S(2)}) collective-permute-start(f32[4,16,512]{2,1,0:T(8,128)S(1)} %get-tuple-element.40), channel_id=1, source_target_pairs={{1,0},{2,1},{3,2},{4,3},{5,4},{6,5},{7,6},{8,7},{9,8},{10,9},{11,1... | collective-permute-start | bytes 393224 | tf_op jit(solution)/shard_map/ppermute | solution.py:647
  48.5 2.8 %collective-permute-done.low_y = f32[4,16,512]{2,1,0:T(8,128)S(1)} collective-permute-done((f32[4,16,512]{2,1,0:T(8,128)S(1)}, f32[4,16,512]{2,1,0:T(8,128)S(1)}, u32[]{:S(2)}, u32[]{:S(2)}) %collective-permute-start) | collective-permute-done | bytes 131104 | tf_op jit(solution)/shard_map/ppermute | solution.py:646
  51.2 0.0 collective-permute-done.1.high_y
  51.3 1.7 %collective-permute-start.3 = (f32[4,56,512]{2,1,0:T(8,128)S(1)}, f32[4,56,512]{2,1,0:T(8,128)S(1)}, u32[]{:S(2)}, u32[]{:S(2)}) collective-permute-start(f32[4,56,512]{2,1,0:T(8,128)S(1)} %pad_maximum_fusion), channel_id=1, source_target_pairs={{16,0},{32,16},{48,32},{64,48},{80,64},{96,80},{112,96},{0,112},{1... | collective-permute-start | bytes 1376264 | tf_op jit(solution)/shard_map/ppermute | solution.py:653
  53.0 0.5 collective-permute-start.2
  53.5 0.1 stack.27
  53.6 6.3 %collective-permute-done.3.high_x = f32[4,56,512]{2,1,0:T(8,128)S(1)} collective-permute-done((f32[4,56,512]{2,1,0:T(8,128)S(1)}, f32[4,56,512]{2,1,0:T(8,128)S(1)}, u32[]{:S(2)}, u32[]{:S(2)}) %collective-permute-start.3) | collective-permute-done | bytes 458784 | tf_op jit(solution)/shard_map/ppermute | solution.py:653
  59.9 0.0 collective-permute-done.2.low_x
  59.9 3.9 %start_solve.1 = (f32[10,16,512]{2,1,0:T(8,128)S(1)}, f32[32,512]{1,0:T(8,128)S(1)}, f32[32,512]{1,0:T(8,128)S(1)}, f32[32,512]{1,0:T(8,128)S(1)}, f32[32,512]{1...) custom-call(s32[6]{0:T(128)S(1)} %convert_element_type.3.edge, ...), custom_call_target="tpu_custom_call" | custom-call | tf_op jit(solution)/shard_map/start_solve/pallas_call | solution.py:382
  63.8 0.1 collective-permute-start.4
  63.9 5.0 %collective-permute-start.5 = (f32[32,512]{1,0:T(8,128)S(1)}, f32[32,512]{1,0:T(8,128)S(1)}, u32[]{:S(2)}, u32[]{:S(2)}) collective-permute-start(f32[32,512]{1,0:T(8,128)S(1)} %get-tuple-element.24), channel_id=1, source_target_pairs={{1,0},{2,1},{3,2},{4,3},{5,4},{6,5},{7,6},{8,7},{9,8},{10,9},{11,1... | collective-permute-start | bytes 196616 | tf_op jit(solution)/shard_map/ppermute | solution.py:661
  68.9 1.6 %collective-permute-done.4.low_y.wide_ly = f32[32,512]{1,0:T(8,128)S(1)} collective-permute-done((f32[32,512]{1,0:T(8,128)S(1)}, f32[32,512]{1,0:T(8,128)S(1)}, u32[]{:S(2)}, u32[]{:S(2)}) %collective-permute-start.4) | collective-permute-done | bytes 65568 | tf_op jit(solution)/shard_map/ppermute | solution.py:660
  70.5 0.0 collective-permute-done.5.high_y.wide_hy
  70.5 0.1 widen.1
  70.6 3.3 %collective-permute-start.7 = (f32[88,512]{1,0:T(8,128)S(1)}, f32[88,512]{1,0:T(8,128)S(1)}, u32[]{:S(2)}, u32[]{:S(2)}) collective-permute-start(f32[88,512]{1,0:T(8,128)S(1)} %get-tuple-element.25), channel_id=1, source_target_pairs={{16,0},{32,16},{48,32},{64,48},{80,64},{96,80},{112,96},{0,112},{1... | collective-permute-start | bytes 540680 | tf_op jit(solution)/shard_map/ppermute | solution.py:666
  73.8 0.0 collective-permute-start.6
  73.8 0.0 collective-permute-start.8
  73.8 2.7 %collective-permute-start.9 = (f32[40,512]{1,0:T(8,128)S(1)}, f32[40,512]{1,0:T(8,128)S(1)}, u32[]{:S(2)}, u32[]{:S(2)}) collective-permute-start(f32[40,512]{1,0:T(8,128)S(1)} %get-tuple-element.27), channel_id=1, source_target_pairs={{32,0},{48,16},{64,32},{80,48},{96,64},{112,80},{0,96},{16,112},{3... | collective-permute-start | bytes 245768 | tf_op jit(solution)/shard_map/ppermute | solution.py:664
  76.5 4.5 %collective-permute-done.8.far_lx = f32[40,512]{1,0:T(8,128)S(1)} collective-permute-done((f32[40,512]{1,0:T(8,128)S(1)}, f32[40,512]{1,0:T(8,128)S(1)}, u32[]{:S(2)}, u32[]{:S(2)}) %collective-permute-start.8) | collective-permute-done | bytes 81952 | tf_op jit(solution)/shard_map/ppermute | solution.py:663
  81.1 0.0 collective-permute-done.9.far_hx
  81.1 0.0 collective-permute-done.7.wide_hx
  81.1 0.0 collective-permute-done.6.wide_lx
  81.1 6.0 %solve.1 = (f32[10,16,512]{2,1,0:T(8,128)S(1)}, f32[10,16,512]{2,1,0:T(8,128)S(1)}, f32[10,16,512]{2,1,0:T(8,128)S(1)}, f32[10,16,512]{2,1,0:T(8,128)S(1)}, f32[...) custom-call(s32[6]{0:T(128)S(1)} %convert_element_type.3.edge, f32[16,16,512]{2,1,0:T(8,128)S(1)} %get-tuple-element.21.total.total_near, ...), custom_call_target="tpu_custom_call" | custom-call | tf_op jit(solution)/shard_map/solve/pallas_call | solution.py:530
  87.1 17.2 %all_to_all.21 = f32[128,1,128]{2,1,0:T(1,128)S(1)} all-to-all(f32[128,1,128]{2,1,0:T(1,128)S(1)} %bitcast.37), channel_id=1, replica_groups=mesh['gx'=8,'yz'=16] {'gx','yz'}, dimensions={0} | all-to-all | bytes 131072 | tf_op jit(solution)/shard_map/all_to_all | solution.py:695
  104.3 11.1 %gather.1 = (f32[384,128]{1,0:T(8,128)}, f32[32,512]{1,0:T(8,128)S(1)}) custom-call(f32[128,128]{1,0:T(8,128)S(1)} %bitcast.36, f32[10,16,512]{2,1,0:T(8,128)S(1)} %get-tuple-element.28.basis_0, f32[10,16,512]{2,1,0:T(8,128)S(1)} %get-tuple-element.33.basis_1, f32[10,16,512]{2,1,0:T(8,128)S(1)} %get-tuple-element.34.basis_2, ...), custom_call_target="tpu_custom_call" | custom-call | tf_op jit(solution)/shard_map/gather/pallas_call | solution.py:630
  115.4 4.5 %all-to-all-start.2 = ((f32[128,1,384]{2,1,0:T(1,128)}), f32[128,1,384]{2,1,0:T(1,128)S(1)}, u32[]{:S(2)}, u32[]{:S(2)}) async-start(f32[128,1,384]{2,1,0:T(1,128)} %bitcast.19), calls=%async_computation.2 | async-start | bytes 393216 | tf_op jit(solution)/shard_map/all_to_all | solution.py:697
  119.9 0.0 copy-start
  119.9 0.7 copy.19
  120.6 9.9 %all-to-all-done.2 = f32[128,1,384]{2,1,0:T(1,128)S(1)} async-done(((f32[128,1,384]{2,1,0:T(1,128)}), f32[128,1,384]{2,1,0:T(1,128)S(1)}, u32[]{:S(2)}, u32[]{:S(2)}) %all-to-all-start.2) | async-done | bytes 196640 | tf_op jit(solution)/shard_map/all_to_all | solution.py:697
  130.5 0.0 copy-done
  130.5 0.7 unpack.1
  (8 shorter events, 0.2 us)
Async XLA Ops:
  2.9 11.5 %copy-start.2 = (s32[4,8,512]{2,1,0:T(8,128)S(1)}, s32[4,8,512]{2,1,0:T(8,128)}, u32[]{:S(2)}) copy-start(s32[4,8,512]{2,1,0:T(8,128)} %param.13) | copy-start | bytes 196612
  2.9 28.7 %all-to-all-start = ((f32[128,1,1664]{2,1,0:T(1,128)}), f32[128,1,1664]{2,1,0:T(1,128)S(1)}, u32[]{:S(2)}, u32[]{:S(2)}) async-start(f32[128,1,1664]{2,1,0:T(1,128)} %bitcast.38), calls=%async_computation | async-start | bytes 1703936 | tf_op jit(solution)/shard_map/all_to_all | solution.py:685
  14.4 0.9 copy-start.1
  43.6 7.6 %collective-permute-start = (f32[4,16,512]{2,1,0:T(8,128)S(1)}, f32[4,16,512]{2,1,0:T(8,128)S(1)}, u32[]{:S(2)}, u32[]{:S(2)}) collective-permute-start(f32[4,16,512]{2,1,0:T(8,128)S(1)} %get-tuple-element.41), channel_id=1, source_target_pairs={{0,1},{1,2},{2,3},{3,4},{4,5},{5,6},{6,7},{7,8},{8,9},{9,10},{10,1... | collective-permute-start | bytes 393224 | tf_op jit(solution)/shard_map/ppermute | solution.py:646
  44.1 7.2 %collective-permute-start.1 = (f32[4,16,512]{2,1,0:T(8,128)S(1)}, f32[4,16,512]{2,1,0:T(8,128)S(1)}, u32[]{:S(2)}, u32[]{:S(2)}) collective-permute-start(f32[4,16,512]{2,1,0:T(8,128)S(1)} %get-tuple-element.40), channel_id=1, source_target_pairs={{1,0},{2,1},{3,2},{4,3},{5,4},{6,5},{7,6},{8,7},{9,8},{10,9},{11,1... | collective-permute-start | bytes 393224 | tf_op jit(solution)/shard_map/ppermute | solution.py:647
  51.3 8.6 %collective-permute-start.3 = (f32[4,56,512]{2,1,0:T(8,128)S(1)}, f32[4,56,512]{2,1,0:T(8,128)S(1)}, u32[]{:S(2)}, u32[]{:S(2)}) collective-permute-start(f32[4,56,512]{2,1,0:T(8,128)S(1)} %pad_maximum_fusion), channel_id=1, source_target_pairs={{16,0},{32,16},{48,32},{64,48},{80,64},{96,80},{112,96},{0,112},{1... | collective-permute-start | bytes 1376264 | tf_op jit(solution)/shard_map/ppermute | solution.py:653
  53.0 6.9 %collective-permute-start.2 = (f32[4,56,512]{2,1,0:T(8,128)S(1)}, f32[4,56,512]{2,1,0:T(8,128)S(1)}, u32[]{:S(2)}, u32[]{:S(2)}) collective-permute-start(f32[4,56,512]{2,1,0:T(8,128)S(1)} %pad_maximum_fusion), channel_id=1, source_target_pairs={{0,16},{16,32},{32,48},{48,64},{64,80},{80,96},{96,112},{112,0},{1... | collective-permute-start | bytes 1376264 | tf_op jit(solution)/shard_map/ppermute | solution.py:653
  63.8 6.7 %collective-permute-start.4 = (f32[32,512]{1,0:T(8,128)S(1)}, f32[32,512]{1,0:T(8,128)S(1)}, u32[]{:S(2)}, u32[]{:S(2)}) collective-permute-start(f32[32,512]{1,0:T(8,128)S(1)} %get-tuple-element.23), channel_id=1, source_target_pairs={{0,1},{1,2},{2,3},{3,4},{4,5},{5,6},{6,7},{7,8},{8,9},{9,10},{10,1... | collective-permute-start | bytes 196616 | tf_op jit(solution)/shard_map/ppermute | solution.py:660
  63.9 6.6 %collective-permute-start.5 = (f32[32,512]{1,0:T(8,128)S(1)}, f32[32,512]{1,0:T(8,128)S(1)}, u32[]{:S(2)}, u32[]{:S(2)}) collective-permute-start(f32[32,512]{1,0:T(8,128)S(1)} %get-tuple-element.24), channel_id=1, source_target_pairs={{1,0},{2,1},{3,2},{4,3},{5,4},{6,5},{7,6},{8,7},{9,8},{10,9},{11,1... | collective-permute-start | bytes 196616 | tf_op jit(solution)/shard_map/ppermute | solution.py:661
  70.6 10.5 %collective-permute-start.7 = (f32[88,512]{1,0:T(8,128)S(1)}, f32[88,512]{1,0:T(8,128)S(1)}, u32[]{:S(2)}, u32[]{:S(2)}) collective-permute-start(f32[88,512]{1,0:T(8,128)S(1)} %get-tuple-element.25), channel_id=1, source_target_pairs={{16,0},{32,16},{48,32},{64,48},{80,64},{96,80},{112,96},{0,112},{1... | collective-permute-start | bytes 540680 | tf_op jit(solution)/shard_map/ppermute | solution.py:666
  73.8 7.2 %collective-permute-start.6 = (f32[88,512]{1,0:T(8,128)S(1)}, f32[88,512]{1,0:T(8,128)S(1)}, u32[]{:S(2)}, u32[]{:S(2)}) collective-permute-start(f32[88,512]{1,0:T(8,128)S(1)} %get-tuple-element.25), channel_id=1, source_target_pairs={{0,16},{16,32},{32,48},{48,64},{64,80},{80,96},{96,112},{112,0},{1... | collective-permute-start | bytes 540680 | tf_op jit(solution)/shard_map/ppermute | solution.py:665
  73.8 7.2 %collective-permute-start.8 = (f32[40,512]{1,0:T(8,128)S(1)}, f32[40,512]{1,0:T(8,128)S(1)}, u32[]{:S(2)}, u32[]{:S(2)}) collective-permute-start(f32[40,512]{1,0:T(8,128)S(1)} %get-tuple-element.26), channel_id=1, source_target_pairs={{0,32},{16,48},{32,64},{48,80},{64,96},{80,112},{96,0},{112,16},{1... | collective-permute-start | bytes 245768 | tf_op jit(solution)/shard_map/ppermute | solution.py:663
  73.8 7.2 %collective-permute-start.9 = (f32[40,512]{1,0:T(8,128)S(1)}, f32[40,512]{1,0:T(8,128)S(1)}, u32[]{:S(2)}, u32[]{:S(2)}) collective-permute-start(f32[40,512]{1,0:T(8,128)S(1)} %get-tuple-element.27), channel_id=1, source_target_pairs={{32,0},{48,16},{64,32},{80,48},{96,64},{112,80},{0,96},{16,112},{3... | collective-permute-start | bytes 245768 | tf_op jit(solution)/shard_map/ppermute | solution.py:664
  115.4 15.1 %all-to-all-start.2 = ((f32[128,1,384]{2,1,0:T(1,128)}), f32[128,1,384]{2,1,0:T(1,128)S(1)}, u32[]{:S(2)}, u32[]{:S(2)}) async-start(f32[128,1,384]{2,1,0:T(1,128)} %bitcast.19), calls=%async_computation.2 | async-start | bytes 393216 | tf_op jit(solution)/shard_map/all_to_all | solution.py:697
  119.9 10.6 %copy-start = (f32[1,128,3,128]{3,1,2,0:T(8,128)S(1)}, f32[1,128,3,128]{3,1,2,0:T(8,128)}, u32[]{:S(2)}) copy-start(f32[1,128,3,128]{3,1,2,0:T(8,128)} %param.8) | copy-start | bytes 589828

commit v6 on v5

--- a/solution.py
+++ b/solution.py
@@ -126,7 +126,7 @@
     )(velocity, returned)
 
 
-def spread_kernel(msg, density, water, out, plane_s, depth_s, value_s, left_a, hot_a, left_b, hot_b, acc):
+def spread_kernel(msg, density, water, out, up, down, plane_s, depth_s, value_s, left_a, hot_a, left_b, hot_b, acc):
     cells_of(msg, plane_s, depth_s)
     depth_s[...] = depth_s[...].astype(F32).T.astype(jnp.int32)
     mass = msg[pl.ds(ROW_M, GROUPS, stride=FIELDS), :]
@@ -167,9 +167,11 @@
         both = acc[f * 64 : (f + 1) * 64, :] + acc[256 + f * 64 : 256 + (f + 1) * 64, :]
         grid.append(both[:CELLS] + pltpu.roll(both[CELLS:], 1, 1))
     total = grid[0] + density[...]
-    out[0] = total
-    for axis in range(3):
-        out[1 + axis] = (grid[1 + axis] + density[...] * water[axis]) / total
+    values = [total] + [(grid[1 + axis] + density[...] * water[axis]) / total for axis in range(3)]
+    for f, value in enumerate(values):
+        out[f] = value
+        up[f] = value[CELLS // 2 :]
+        down[f] = value[: CELLS // 2]
 
 
 def spread(msg, density, water):
@@ -178,9 +180,9 @@
     index = pltpu.VMEM((GROUPS, CAP), jnp.int32)
     return pl.pallas_call(
         spread_kernel,
-        out_shape=shape(4, CELLS, DEPTH),
+        out_shape=[shape(4, CELLS, DEPTH)] + [shape(4, CELLS // 2, DEPTH)] * 2,
         in_specs=[VM] * 3,
-        out_specs=VM,
+        out_specs=[VM] * 3,
         scratch_shapes=[index, index, pltpu.VMEM((4, GROUPS, CAP), F32)]
         + [left, hot, left, hot]
         + [pltpu.VMEM((512, DEPTH), F32)],
@@ -638,13 +640,13 @@
     )(sums, *bases, *betas, own, msg)
 
 
-def exchange(block, n_x, n_y, corner):
+def exchange(block, up, down, n_x, n_y, corner):
     up_x = [(i, (i + 1) % n_x) for i in range(n_x)]
     up_y = [(i, (i + 1) % n_y) for i in range(n_y)]
     down_x, down_y = [[(b, a) for a, b in up] for up in (up_x, up_y)]
     half = 4 * HALO
-    low_y = lax.ppermute(block[..., CELLS - half :, :], "yz", up_y)
-    high_y = lax.ppermute(block[..., :half, :], "yz", down_y)
+    low_y = lax.ppermute(up, "yz", up_y)
+    high_y = lax.ppermute(down, "yz", down_y)
     near = 4 * corner
     near_low, near_high = low_y, high_y
     if corner < HALO:
@@ -685,8 +687,8 @@
     msg = lax.all_to_all(message.reshape(GROUPS, 1, FIELDS * CAP), ALL, 0, 0, tiled=True)
     msg = msg.reshape(GROUPS * FIELDS, CAP)
     density = by_block(jnp.where(solid_flag == 1, SOLID_WATER, 1.0).astype(F32))
-    own = spread(msg, density, by_block(water_vel))
-    near = exchange(own, n_x, n_y, CORNER)
+    own, top, bottom = spread(msg, density, by_block(water_vel))
+    near = exchange(own, top, bottom, n_x, n_y, CORNER)
     basis_0, own_0, image_0, scaled, source, total, up, down = start_solve(edge, own, near)
     wide = exchange_wide(scaled, up, down, total, n_x, n_y)
     basis_1, basis_2, *betas, sums = solve(

time: 132 us -> 131 us (level)
  no operation moved by 1% of the time
where the time goes in v6:
time: 131 us
  waiting for transfers between devices  41.2 us (31%)
  Pallas kernels  36 us (27%)
  starting transfers between devices  34 us (26%)
  blocking collectives  17.2 us (13%)
  local copies, waits for them, and re-layouts  1.89 us (1%)
    all_to_all x1, blocking collectives, local(): sums = lax.all_to_all(sums, ALL, 0, 0, tiled=True)  17.2 us
    all_to_all x1, waiting for transfers between devices, local(): lax.all_to_all(message.reshape(GROUPS, 1, FIELDS * CAP), ALL, 0, 0, tiled...  16.1 us
    pallas_call x1, Pallas kernels, spread(): pl.pallas_call(spread_kernel, out_shape=[shape(4, CELLS, DEPTH)] + [shape...  11.9 us
    all_to_all x1, starting transfers between devices, local(): lax.all_to_all(message.reshape(GROUPS, 1, FIELDS * CAP), ALL, 0, 0, tiled...  11.5 us
    pallas_call x1, Pallas kernels, gather(): pl.pallas_call(gather_kernel, out_shape=[shape(3 * GROUPS, CAP), shape(*B...  11.1 us
    all_to_all x1, waiting for transfers between devices, local(): lax.all_to_all(sampled.reshape(GROUPS, 1, 3 * CAP), ALL, 0, 0, tiled=True)  9.91 us
    ppermute x1, waiting for transfers between devices, exchange(): lax.ppermute(column, 'gx', down_x)  6.32 us
    pallas_call x1, Pallas kernels, solve(): pl.pallas_call(solve_kernel, out_shape=[shape(*BASIS)] * 5 + [shape(GROUP...  5.97 us
  transfers between devices with their start and end apart: 12, of which 6 were waited for; matrix products, arithmetic and copies ran while one was open for 1% of the time, Pallas kernels for 0%

profile of v6, /device:TPU:1, one launch (start us, length us, event | category | flops | bytes accessed | tf_op | source)
XLA Modules:
  0.0 131.2 jit_solution(12159060156716242448)
XLA Ops:
  0.6 2.3 %pack.1 = f32[1664,128]{1,0:T(8,128)} custom-call(f32[128,128]{1,0:T(8,128)} %bitcast.42, f32[3,128,128]{2,1,0:T(8,128)} %bitcast.32, f32[1024,128]{1,0:T(8,128)} %bitcast.39, s32[128,128]{1,0:T(8,128)} %bitcast.43, s32[1,128]{1,0:T(1,128)} %count_h.1), custom_call_target="tpu_custom_call" | custom-call | tf_op jit(solution)/shard_map/pack/pallas_call | solution.py:102
  2.9 0.0 copy-start.2
  2.9 11.5 %all-to-all-start = ((f32[128,1,1664]{2,1,0:T(1,128)}), f32[128,1,1664]{2,1,0:T(1,128)S(1)}, u32[]{:S(2)}, u32[]{:S(2)}) async-start(f32[128,1,1664]{2,1,0:T(1,128)} %bitcast.38), calls=%async_computation | async-start | bytes 1703936 | tf_op jit(solution)/shard_map/all_to_all | solution.py:687
  14.4 0.0 copy-done.2
  14.4 0.0 copy-start.1
  14.5 0.8 copy-done.1
  15.4 0.1 copy.14
  15.5 0.1 reshape.34.water
  15.6 16.1 %all-to-all-done = f32[128,1,1664]{2,1,0:T(1,128)S(1)} async-done(((f32[128,1,1664]{2,1,0:T(1,128)}), f32[128,1,1664]{2,1,0:T(1,128)S(1)}, u32[]{:S(2)}, u32[]{:S(2)}) %all-to-all-start) | async-done | bytes 852000 | tf_op jit(solution)/shard_map/all_to_all | solution.py:687
  31.6 11.9 %spread.1 = (f32[4,32,512]{2,1,0:T(8,128)S(1)}, f32[4,16,512]{2,1,0:T(8,128)S(1)}, f32[4,16,512]{2,1,0:T(8,128)S(1)}) custom-call(f32[1664,128]{1,0:T(8,128)S(1)} %bitcast.30, f32[32,512]{1,0:T(8,128)S(1)} %reshape.33.density, f32[3,32,512]{2,1,0:T(8,128)S(1)} %reshape.34.water), custom_call_target="tpu_custom_call" | custom-call | tf_op jit(solution)/shard_map/spread/pallas_call | solution.py:181
  43.6 0.4 collective-permute-start
  44.0 4.4 %collective-permute-start.1 = (f32[4,16,512]{2,1,0:T(8,128)S(1)}, f32[4,16,512]{2,1,0:T(8,128)S(1)}, u32[]{:S(2)}, u32[]{:S(2)}) collective-permute-start(f32[4,16,512]{2,1,0:T(8,128)S(1)} %get-tuple-element.26), channel_id=1, source_target_pairs={{1,0},{2,1},{3,2},{4,3},{5,4},{6,5},{7,6},{8,7},{9,8},{10,9},{11,1... | collective-permute-start | bytes 393224 | tf_op jit(solution)/shard_map/ppermute | solution.py:649
  48.4 2.8 %collective-permute-done.low_y = f32[4,16,512]{2,1,0:T(8,128)S(1)} collective-permute-done((f32[4,16,512]{2,1,0:T(8,128)S(1)}, f32[4,16,512]{2,1,0:T(8,128)S(1)}, u32[]{:S(2)}, u32[]{:S(2)}) %collective-permute-start) | collective-permute-done | bytes 131104 | tf_op jit(solution)/shard_map/ppermute | solution.py:648
  51.2 0.0 collective-permute-done.1.high_y
  51.3 1.7 %collective-permute-start.3 = (f32[4,56,512]{2,1,0:T(8,128)S(1)}, f32[4,56,512]{2,1,0:T(8,128)S(1)}, u32[]{:S(2)}, u32[]{:S(2)}) collective-permute-start(f32[4,56,512]{2,1,0:T(8,128)S(1)} %pad_maximum_fusion), channel_id=1, source_target_pairs={{16,0},{32,16},{48,32},{64,48},{80,64},{96,80},{112,96},{0,112},{1... | collective-permute-start | bytes 1376264 | tf_op jit(solution)/shard_map/ppermute | solution.py:655
  53.0 0.5 collective-permute-start.2
  53.5 0.1 stack.27
  53.6 6.3 %collective-permute-done.3.high_x = f32[4,56,512]{2,1,0:T(8,128)S(1)} collective-permute-done((f32[4,56,512]{2,1,0:T(8,128)S(1)}, f32[4,56,512]{2,1,0:T(8,128)S(1)}, u32[]{:S(2)}, u32[]{:S(2)}) %collective-permute-start.3) | collective-permute-done | bytes 458784 | tf_op jit(solution)/shard_map/ppermute | solution.py:655
  59.9 0.0 collective-permute-done.2.low_x
  59.9 3.9 %start_solve.1 = (f32[10,16,512]{2,1,0:T(8,128)S(1)}, f32[32,512]{1,0:T(8,128)S(1)}, f32[32,512]{1,0:T(8,128)S(1)}, f32[32,512]{1,0:T(8,128)S(1)}, f32[32,512]{1...) custom-call(s32[6]{0:T(128)S(1)} %convert_element_type.3.edge, ...), custom_call_target="tpu_custom_call" | custom-call | tf_op jit(solution)/shard_map/start_solve/pallas_call | solution.py:384
  63.8 0.1 collective-permute-start.4
  63.9 5.0 %collective-permute-start.5 = (f32[32,512]{1,0:T(8,128)S(1)}, f32[32,512]{1,0:T(8,128)S(1)}, u32[]{:S(2)}, u32[]{:S(2)}) collective-permute-start(f32[32,512]{1,0:T(8,128)S(1)} %get-tuple-element.30), channel_id=1, source_target_pairs={{1,0},{2,1},{3,2},{4,3},{5,4},{6,5},{7,6},{8,7},{9,8},{10,9},{11,1... | collective-permute-start | bytes 196616 | tf_op jit(solution)/shard_map/ppermute | solution.py:663
  68.9 1.6 %collective-permute-done.4.low_y.wide_ly = f32[32,512]{1,0:T(8,128)S(1)} collective-permute-done((f32[32,512]{1,0:T(8,128)S(1)}, f32[32,512]{1,0:T(8,128)S(1)}, u32[]{:S(2)}, u32[]{:S(2)}) %collective-permute-start.4) | collective-permute-done | bytes 65568 | tf_op jit(solution)/shard_map/ppermute | solution.py:662
  70.5 0.0 collective-permute-done.5.high_y.wide_hy
  70.5 0.1 widen.1
  70.6 3.3 %collective-permute-start.7 = (f32[88,512]{1,0:T(8,128)S(1)}, f32[88,512]{1,0:T(8,128)S(1)}, u32[]{:S(2)}, u32[]{:S(2)}) collective-permute-start(f32[88,512]{1,0:T(8,128)S(1)} %get-tuple-element.31), channel_id=1, source_target_pairs={{16,0},{32,16},{48,32},{64,48},{80,64},{96,80},{112,96},{0,112},{1... | collective-permute-start | bytes 540680 | tf_op jit(solution)/shard_map/ppermute | solution.py:668
  73.8 0.0 collective-permute-start.6
  73.8 0.0 collective-permute-start.8
  73.8 2.7 %collective-permute-start.9 = (f32[40,512]{1,0:T(8,128)S(1)}, f32[40,512]{1,0:T(8,128)S(1)}, u32[]{:S(2)}, u32[]{:S(2)}) collective-permute-start(f32[40,512]{1,0:T(8,128)S(1)} %get-tuple-element.33), channel_id=1, source_target_pairs={{32,0},{48,16},{64,32},{80,48},{96,64},{112,80},{0,96},{16,112},{3... | collective-permute-start | bytes 245768 | tf_op jit(solution)/shard_map/ppermute | solution.py:666
  76.5 4.5 %collective-permute-done.8.far_lx = f32[40,512]{1,0:T(8,128)S(1)} collective-permute-done((f32[40,512]{1,0:T(8,128)S(1)}, f32[40,512]{1,0:T(8,128)S(1)}, u32[]{:S(2)}, u32[]{:S(2)}) %collective-permute-start.8) | collective-permute-done | bytes 81952 | tf_op jit(solution)/shard_map/ppermute | solution.py:665
  81.0 0.0 collective-permute-done.9.far_hx
  81.0 0.0 collective-permute-done.7.wide_hx
  81.0 0.0 collective-permute-done.6.wide_lx
  81.0 6.0 %solve.1 = (f32[10,16,512]{2,1,0:T(8,128)S(1)}, f32[10,16,512]{2,1,0:T(8,128)S(1)}, f32[10,16,512]{2,1,0:T(8,128)S(1)}, f32[10,16,512]{2,1,0:T(8,128)S(1)}, f32[...) custom-call(s32[6]{0:T(128)S(1)} %convert_element_type.3.edge, f32[16,16,512]{2,1,0:T(8,128)S(1)} %get-tuple-element.27.total.total_near, ...), custom_call_target="tpu_custom_call" | custom-call | tf_op jit(solution)/shard_map/solve/pallas_call | solution.py:532
  87.0 17.2 %all_to_all.21 = f32[128,1,128]{2,1,0:T(1,128)S(1)} all-to-all(f32[128,1,128]{2,1,0:T(1,128)S(1)} %bitcast.37), channel_id=1, replica_groups=mesh['gx'=8,'yz'=16] {'gx','yz'}, dimensions={0} | all-to-all | bytes 131072 | tf_op jit(solution)/shard_map/all_to_all | solution.py:697
  104.3 11.1 %gather.1 = (f32[384,128]{1,0:T(8,128)}, f32[32,512]{1,0:T(8,128)S(1)}) custom-call(f32[128,128]{1,0:T(8,128)S(1)} %bitcast.36, f32[10,16,512]{2,1,0:T(8,128)S(1)} %get-tuple-element.34.basis_0, f32[10,16,512]{2,1,0:T(8,128)S(1)} %get-tuple-element.39.basis_1, f32[10,16,512]{2,1,0:T(8,128)S(1)} %get-tuple-element.40.basis_2, ...), custom_call_target="tpu_custom_call" | custom-call | tf_op jit(solution)/shard_map/gather/pallas_call | solution.py:632
  115.4 4.5 %all-to-all-start.2 = ((f32[128,1,384]{2,1,0:T(1,128)}), f32[128,1,384]{2,1,0:T(1,128)S(1)}, u32[]{:S(2)}, u32[]{:S(2)}) async-start(f32[128,1,384]{2,1,0:T(1,128)} %bitcast.19), calls=%async_computation.2 | async-start | bytes 393216 | tf_op jit(solution)/shard_map/all_to_all | solution.py:699
  119.9 0.0 copy-start
  119.9 0.7 copy.19
  120.6 9.9 %all-to-all-done.2 = f32[128,1,384]{2,1,0:T(1,128)S(1)} async-done(((f32[128,1,384]{2,1,0:T(1,128)}), f32[128,1,384]{2,1,0:T(1,128)S(1)}, u32[]{:S(2)}, u32[]{:S(2)}) %all-to-all-start.2) | async-done | bytes 196640 | tf_op jit(solution)/shard_map/all_to_all | solution.py:699
  130.5 0.0 copy-done
  130.5 0.7 unpack.1
  (7 shorter events, 0.2 us)
Async XLA Ops:
  2.9 11.5 %copy-start.2 = (s32[4,8,512]{2,1,0:T(8,128)S(1)}, s32[4,8,512]{2,1,0:T(8,128)}, u32[]{:S(2)}) copy-start(s32[4,8,512]{2,1,0:T(8,128)} %param.13) | copy-start | bytes 196612
  2.9 28.7 %all-to-all-start = ((f32[128,1,1664]{2,1,0:T(1,128)}), f32[128,1,1664]{2,1,0:T(1,128)S(1)}, u32[]{:S(2)}, u32[]{:S(2)}) async-start(f32[128,1,1664]{2,1,0:T(1,128)} %bitcast.38), calls=%async_computation | async-start | bytes 1703936 | tf_op jit(solution)/shard_map/all_to_all | solution.py:687
  14.4 0.9 copy-start.1
  43.6 7.6 %collective-permute-start = (f32[4,16,512]{2,1,0:T(8,128)S(1)}, f32[4,16,512]{2,1,0:T(8,128)S(1)}, u32[]{:S(2)}, u32[]{:S(2)}) collective-permute-start(f32[4,16,512]{2,1,0:T(8,128)S(1)} %get-tuple-element.25), channel_id=1, source_target_pairs={{0,1},{1,2},{2,3},{3,4},{4,5},{5,6},{6,7},{7,8},{8,9},{9,10},{10,1... | collective-permute-start | bytes 393224 | tf_op jit(solution)/shard_map/ppermute | solution.py:648
  44.0 7.2 %collective-permute-start.1 = (f32[4,16,512]{2,1,0:T(8,128)S(1)}, f32[4,16,512]{2,1,0:T(8,128)S(1)}, u32[]{:S(2)}, u32[]{:S(2)}) collective-permute-start(f32[4,16,512]{2,1,0:T(8,128)S(1)} %get-tuple-element.26), channel_id=1, source_target_pairs={{1,0},{2,1},{3,2},{4,3},{5,4},{6,5},{7,6},{8,7},{9,8},{10,9},{11,1... | collective-permute-start | bytes 393224 | tf_op jit(solution)/shard_map/ppermute | solution.py:649
  51.3 8.6 %collective-permute-start.3 = (f32[4,56,512]{2,1,0:T(8,128)S(1)}, f32[4,56,512]{2,1,0:T(8,128)S(1)}, u32[]{:S(2)}, u32[]{:S(2)}) collective-permute-start(f32[4,56,512]{2,1,0:T(8,128)S(1)} %pad_maximum_fusion), channel_id=1, source_target_pairs={{16,0},{32,16},{48,32},{64,48},{80,64},{96,80},{112,96},{0,112},{1... | collective-permute-start | bytes 1376264 | tf_op jit(solution)/shard_map/ppermute | solution.py:655
  53.0 6.9 %collective-permute-start.2 = (f32[4,56,512]{2,1,0:T(8,128)S(1)}, f32[4,56,512]{2,1,0:T(8,128)S(1)}, u32[]{:S(2)}, u32[]{:S(2)}) collective-permute-start(f32[4,56,512]{2,1,0:T(8,128)S(1)} %pad_maximum_fusion), channel_id=1, source_target_pairs={{0,16},{16,32},{32,48},{48,64},{64,80},{80,96},{96,112},{112,0},{1... | collective-permute-start | bytes 1376264 | tf_op jit(solution)/shard_map/ppermute | solution.py:655
  63.8 6.7 %collective-permute-start.4 = (f32[32,512]{1,0:T(8,128)S(1)}, f32[32,512]{1,0:T(8,128)S(1)}, u32[]{:S(2)}, u32[]{:S(2)}) collective-permute-start(f32[32,512]{1,0:T(8,128)S(1)} %get-tuple-element.29), channel_id=1, source_target_pairs={{0,1},{1,2},{2,3},{3,4},{4,5},{5,6},{6,7},{7,8},{8,9},{9,10},{10,1... | collective-permute-start | bytes 196616 | tf_op jit(solution)/shard_map/ppermute | solution.py:662
  63.9 6.6 %collective-permute-start.5 = (f32[32,512]{1,0:T(8,128)S(1)}, f32[32,512]{1,0:T(8,128)S(1)}, u32[]{:S(2)}, u32[]{:S(2)}) collective-permute-start(f32[32,512]{1,0:T(8,128)S(1)} %get-tuple-element.30), channel_id=1, source_target_pairs={{1,0},{2,1},{3,2},{4,3},{5,4},{6,5},{7,6},{8,7},{9,8},{10,9},{11,1... | collective-permute-start | bytes 196616 | tf_op jit(solution)/shard_map/ppermute | solution.py:663
  70.6 10.5 %collective-permute-start.7 = (f32[88,512]{1,0:T(8,128)S(1)}, f32[88,512]{1,0:T(8,128)S(1)}, u32[]{:S(2)}, u32[]{:S(2)}) collective-permute-start(f32[88,512]{1,0:T(8,128)S(1)} %get-tuple-element.31), channel_id=1, source_target_pairs={{16,0},{32,16},{48,32},{64,48},{80,64},{96,80},{112,96},{0,112},{1... | collective-permute-start | bytes 540680 | tf_op jit(solution)/shard_map/ppermute | solution.py:668
  73.8 7.2 %collective-permute-start.6 = (f32[88,512]{1,0:T(8,128)S(1)}, f32[88,512]{1,0:T(8,128)S(1)}, u32[]{:S(2)}, u32[]{:S(2)}) collective-permute-start(f32[88,512]{1,0:T(8,128)S(1)} %get-tuple-element.31), channel_id=1, source_target_pairs={{0,16},{16,32},{32,48},{48,64},{64,80},{80,96},{96,112},{112,0},{1... | collective-permute-start | bytes 540680 | tf_op jit(solution)/shard_map/ppermute | solution.py:667
  73.8 7.2 %collective-permute-start.8 = (f32[40,512]{1,0:T(8,128)S(1)}, f32[40,512]{1,0:T(8,128)S(1)}, u32[]{:S(2)}, u32[]{:S(2)}) collective-permute-start(f32[40,512]{1,0:T(8,128)S(1)} %get-tuple-element.32), channel_id=1, source_target_pairs={{0,32},{16,48},{32,64},{48,80},{64,96},{80,112},{96,0},{112,16},{1... | collective-permute-start | bytes 245768 | tf_op jit(solution)/shard_map/ppermute | solution.py:665
  73.8 7.2 %collective-permute-start.9 = (f32[40,512]{1,0:T(8,128)S(1)}, f32[40,512]{1,0:T(8,128)S(1)}, u32[]{:S(2)}, u32[]{:S(2)}) collective-permute-start(f32[40,512]{1,0:T(8,128)S(1)} %get-tuple-element.33), channel_id=1, source_target_pairs={{32,0},{48,16},{64,32},{80,48},{96,64},{112,80},{0,96},{16,112},{3... | collective-permute-start | bytes 245768 | tf_op jit(solution)/shard_map/ppermute | solution.py:666
  115.4 15.1 %all-to-all-start.2 = ((f32[128,1,384]{2,1,0:T(1,128)}), f32[128,1,384]{2,1,0:T(1,128)S(1)}, u32[]{:S(2)}, u32[]{:S(2)}) async-start(f32[128,1,384]{2,1,0:T(1,128)} %bitcast.19), calls=%async_computation.2 | async-start | bytes 393216 | tf_op jit(solution)/shard_map/all_to_all | solution.py:699
  119.9 10.6 %copy-start = (f32[1,128,3,128]{3,1,2,0:T(8,128)S(1)}, f32[1,128,3,128]{3,1,2,0:T(8,128)}, u32[]{:S(2)}) copy-start(f32[1,128,3,128]{3,1,2,0:T(8,128)} %param.8) | copy-start | bytes 589828
